TPU v7x, 128 devices: a whole 4x4x4 slice. The times are simulated.
128 devices in a mesh: row: 8 (over x_hi, z), col: 16 (over y, x_lo, core).
Axes of the slice: x: 4 (x_hi: 2, x_lo: 2; x = x_hi * 2 + x_lo), y: 4, z: 4, core: 2. Of those that a mesh axis runs over, the one named last changes fastest.
Arguments:
- a_held: float32 [4096, 128, 128], P(('row', 'col')), may hold values from -0.5 to 0.5
- a_slot: int32 [4096], P(('row', 'col')), may hold values from 0 to 4095, as said below
- a_col: int32 [4096], P(('row', 'col')), may hold values from -1 to 15, as said below
- b_held: float32 [8192, 128, 128], P(('row', 'col')), may hold values from -6 to 6
- b_slot: int32 [8192], P(('row', 'col')), may hold values from 0 to 8191, as said below
- b_col: int32 [8192], P(('row', 'col')), may hold values from -1 to 15, as said below
- c_col: int32 [128, 96], P('row', 'col'), may hold values from -1 to 15, as said below
Outputs:
- product: float32 [128, 96, 128, 128], P('row', 'col')
Inputs may be any that keep to these rules, and one draw needn't show every extreme that they name: `a_slot`: a permutation of 0 to 4095; one device holds at most 1 slots of one left panel, and some device holds exactly that many. `a_col`: the filled columns of one block row of a left panel are distinct; some block row of every panel has all 4 slots filled. `b_slot`: a permutation of 0 to 8191; one device holds at most 1 slots of one right panel, and some device holds exactly that many. `b_col`: the filled columns of one inner block row of a right panel are distinct; some block row of every panel has all 4 slots filled. `c_col`: the retained columns of one block row within one grid column are distinct, -1 marks an empty slot; every grid column has a block row with all 6 slots retained.
All inputs are finite; a program needn't handle non-finite values.
Results may differ from a plain program's by a relative error of at most 0.0003.
Values sent between devices are 32-bit elements; how exact they have to be, the bound alone decides.
A program may use at most 192 MiB of HBM per device.

v0:
```python
import jax
import jax.numpy as jnp
from jax import lax
from jax.sharding import PartitionSpec as P

KPB = 16
WA = 4
WB = 4
STEPS = 3


def shifted(value, axis, steps):
    count = lax.axis_size(axis)
    pairs = [(source, (source + steps) % count) for source in range(count)]
    return lax.ppermute(value, axis, pairs)


def route_matrix(dests, capacity, devices_all):
    flat_dest = dests.reshape(-1)
    position = jnp.arange(flat_dest.shape[0])
    before = (flat_dest[:, None] == flat_dest[None, :]) & (position[:, None] > position[None, :])
    rank_dest = jnp.sum(before.astype(jnp.int32), axis=1)
    target = flat_dest * capacity + rank_dest
    onehot_matrix = (target[None, :] == jnp.arange(devices_all * capacity)[:, None]).astype(
        jnp.float32
    )
    return onehot_matrix.reshape(devices_all * capacity, dests.shape[0], dests.shape[1]).sum(axis=2)


def pack_blocks(held_blocks, local_slot, column_indices, dests, capacity, devices_all):
    select = route_matrix(dests, capacity, devices_all)
    edge = held_blocks.shape[1]
    block_list = jnp.dot(
        select, held_blocks.reshape(held_blocks.shape[0], -1), precision=lax.Precision.HIGHEST
    )
    block_labels = jnp.stack(
        [
            local_slot.astype(jnp.float32),
            column_indices.astype(jnp.float32),
            jnp.ones(local_slot.shape, jnp.float32),
        ],
        axis=1,
    )
    marker_flags = jnp.dot(select, block_labels, precision=lax.Precision.HIGHEST)
    return (block_list.reshape(-1, edge, edge), marker_flags)


def expand_block_list(block_list, marker_flags, slot_count):
    present_flags = marker_flags[:, 2] > 0.5
    slot_location = marker_flags[:, 0].astype(jnp.int32)
    onehot_matrix = (
        (slot_location[None, :] == jnp.arange(slot_count)[:, None]) & present_flags[None, :]
    ).astype(jnp.float32)
    placed = jnp.dot(
        onehot_matrix, block_list.reshape(block_list.shape[0], -1), precision=lax.Precision.HIGHEST
    )
    filled = jnp.sum(onehot_matrix, axis=1) > 0.5
    block_labels = jnp.where(
        filled, jnp.dot(onehot_matrix, marker_flags[:, 1], precision=lax.Precision.HIGHEST), -1.0
    )
    return (placed, block_labels)


def panel_products(left, left_labels, right, right_labels, kept):
    left_cols = left_labels.astype(jnp.int32)
    safe = jnp.maximum(left_cols, 0)
    chosen = jnp.take(right, safe, axis=0)
    chosen_cols = jnp.take(right_labels, safe, axis=0).astype(jnp.int32)
    match = (
        (left_cols >= 0)[:, None, :, None]
        & (chosen_cols[:, None, :, :] == kept[:, :, None, None])
        & (kept >= 0)[:, :, None, None]
    )
    match = match.astype(jnp.float32)
    pieces = jnp.einsum("rwij,rwvjl->rwvil", left, chosen, precision=lax.Precision.HIGHEST)
    return jnp.einsum("rtwv,rwvil->rtil", match, pieces, precision=lax.Precision.HIGHEST)


def on_device(a_held, a_slot, a_col, b_held, b_slot, b_col, c_col):
    grid_rows = lax.axis_size("row")
    grid_cols = lax.axis_size("col")
    devices_all = grid_rows * grid_cols
    rows_dev = c_col.shape[0]
    retained_width = c_col.shape[1]
    edge = a_held.shape[1]
    slots_left = rows_dev * WA
    slots_right = KPB * WB
    capacity_left = max(1, slots_left // devices_all)
    capacity_right = max(1, slots_right // devices_all)
    copies = grid_cols // grid_rows
    panel_left = a_slot // slots_left
    left_grid_row = panel_left // grid_rows
    left_inner = panel_left % grid_rows
    first_col = (left_inner - left_grid_row) % grid_rows
    dest_left = (left_grid_row * grid_cols + first_col)[:, None] + grid_rows * jnp.arange(
        copies, dtype=jnp.int32
    )[None, :]
    panel_right = b_slot // slots_right
    right_inner = panel_right // grid_cols
    right_grid_col = panel_right % grid_cols
    dest_right = ((right_inner - right_grid_col) % grid_rows * grid_cols + right_grid_col)[:, None]
    send_left, marker_left = pack_blocks(
        a_held, a_slot % slots_left, a_col, dest_left, capacity_left, devices_all
    )
    send_right, marker_right = pack_blocks(
        b_held, b_slot % slots_right, b_col, dest_right, capacity_right, devices_all
    )
    recv_left, rmark_left, recv_right, rmark_right = (
        lax.all_to_all(send_left, ("row", "col"), split_axis=0, concat_axis=0, tiled=True),
        lax.all_to_all(marker_left, ("row", "col"), split_axis=0, concat_axis=0, tiled=True),
        lax.all_to_all(send_right, ("row", "col"), split_axis=0, concat_axis=0, tiled=True),
        lax.all_to_all(marker_right, ("row", "col"), split_axis=0, concat_axis=0, tiled=True),
    )
    left_flat, left_labels = expand_block_list(recv_left, rmark_left, slots_left)
    left_home = left_flat.reshape(rows_dev, WA, edge, edge)
    left_labels = left_labels.reshape(rows_dev, WA)
    right_flat, right_labels = expand_block_list(recv_right, rmark_right, slots_right)
    right_home = right_flat.reshape(KPB, WB, edge, edge)
    right_labels = right_labels.reshape(KPB, WB)
    accum = jnp.zeros((rows_dev, retained_width, edge, edge), jnp.float32)
    for iteration in range(STEPS):
        accum = accum + panel_products(left_home, left_labels, right_home, right_labels, c_col)
        if iteration + 1 < STEPS:
            left_home, left_labels = shifted((left_home, left_labels), "col", -1)
            right_home, right_labels = shifted((right_home, right_labels), "row", -1)
    return accum


def solution(mesh):
    return jax.shard_map(
        on_device,
        mesh=mesh,
        in_specs=(
            P(("row", "col"), None, None),
            P(("row", "col")),
            P(("row", "col")),
            P(("row", "col"), None, None),
            P(("row", "col")),
            P(("row", "col")),
            P("row", "col"),
        ),
        out_specs=P("row", "col", None, None),
        check_vma=False,
    )
```

profile of v0, /device:TPU:11, one launch (start us, length us, event | category | flops | bytes accessed | tf_op | source)
XLA Modules:
  0.0 703.7 jit_solution(842317872033297929)
XLA Ops:
  0.0 0.7 fusion.113
  0.7 0.2 convert_reduce_fusion.1
  0.9 0.7 convert_bitcast_fusion
  1.6 1.0 fusion.67
  2.6 10.7 %all-to-all-start.1 = ((f32[128,1,3]{2,1,0:T(1,128)}), f32[128,1,3]{2,1,0:T(1,128)S(1)}, u32[]{:S(2)}, u32[]{:S(2)}) async-start(f32[128,1,3]{2,1,0:T(1,128)} %bitcast.64), calls=%async_computation.1 | async-start | bytes 131072 | tf_op jit(solution)/shard_map/all_to_all | solution.py:112
  13.3 0.7 fusion.109
  14.2 0.2 convert_reduce_fusion.4
  14.7 0.7 convert_bitcast_fusion.1
  15.4 0.9 fusion.95
  16.3 4.6 all-to-all-done.1
  20.9 6.4 all-to-all-start
  27.3 8.4 %fusion.25 = f32[128,128,128]{2,0,1:T(8,128)S(1)} fusion(s32[64]{0:T(128)S(1)} %add.111, f32[8,8,128,128]{3,2,1,0:T(8,128)} %bitcast.138), kind=kOutput, calls=%fused_computation.28 | convolution fusion | flops 1610620928 | bytes 12583168 | tf_op jit(solution)/shard_map/dot_general | solution.py:33
  35.7 8.1 %copy.146 = f32[128,128,128]{2,1,0:T(8,128)} copy(f32[128,128,128]{2,0,1:T(8,128)S(1)} %fusion.25) | data formatting | bytes 16777216 | tf_op jit(solution)/shard_map/dot_general | solution.py:33
  43.8 10.4 %all-to-all-start.2 = ((f32[128,128,128]{2,1,0:T(8,128)}), f32[128,128,128]{2,1,0:T(8,128)}, u32[]{:S(2)}, u32[]{:S(2)}) async-start(f32[128,128,128]{2,1,0:T(8,128)} %copy.146), calls=%async_computation.2 | async-start | bytes 16777216 | tf_op jit(solution)/shard_map/all_to_all | solution.py:111
  54.2 7.3 %fusion.31 = f32[128,128,128]{2,0,1:T(8,128)S(1)} fusion(f32[128,32]{0,1:T(8,128)S(1)} %convert_reduce_fusion.3, f32[4,8,128,128]{3,2,1,0:T(8,128)S(1)} %bitcast.139), kind=kOutput, calls=%fused_computation.35 | convolution fusion | flops 805306368 | bytes 10502144 | tf_op jit(solution)/shard_map/dot_general | solution.py:33
  61.5 8.6 %copy.151 = f32[128,128,128]{2,1,0:T(8,128)} copy(f32[128,128,128]{2,0,1:T(8,128)S(1)} %fusion.31) | data formatting | bytes 16777216 | tf_op jit(solution)/shard_map/dot_general | solution.py:33
  70.1 91.1 %all-to-all-done.2 = f32[128,128,128]{2,1,0:T(8,128)} async-done(((f32[128,128,128]{2,1,0:T(8,128)}), f32[128,128,128]{2,1,0:T(8,128)}, u32[]{:S(2)}, u32[]{:S(2)}) %all-to-all-start.2) | async-done | bytes 8388640 | tf_op jit(solution)/shard_map/all_to_all | solution.py:111
  161.1 9.7 %all-to-all-start.3 = ((f32[128,128,128]{2,1,0:T(8,128)}), f32[128,128,128]{2,1,0:T(8,128)}, u32[]{:S(2)}, u32[]{:S(2)}) async-start(f32[128,128,128]{2,1,0:T(8,128)} %copy.151), calls=%async_computation.3 | async-start | bytes 16777216 | tf_op jit(solution)/shard_map/all_to_all | solution.py:109
  170.9 0.1 fusion.51
  171.0 0.2 fusion.59
  171.2 0.2 fusion.58
  171.4 9.3 %copy.147 = f32[128,128,128]{0,2,1:T(8,128)} copy(f32[128,128,128]{2,1,0:T(8,128)} %all-to-all-done.2) | data formatting | bytes 16777216 | tf_op jit(solution)/shard_map/all_to_all | solution.py:111
  180.7 10.4 %fusion.17 = f32[16,4,128,128]{3,0,2,1:T(8,128)} fusion(f32[128,128,128]{0,2,1:T(8,128)} %copy.147, s32[16,4]{0,1:T(4,128)S(1)} %multiply_add_fusion, s32[128]{0:T(128)S(1)} %fusion.50, pred[128]{0:T(512)(128)(4,1)S(1)} %fusion.59), kind=kOutput, calls=%fused_computation.17 | convolution fusion | flops 1610629120 | bytes 12583808 | tf_op jit(solution)/shard_map/dot_general | solution.py:54
  191.1 4.7 collective-permute-start.2
  195.8 86.0 %all-to-all-done.3 = f32[128,128,128]{2,1,0:T(8,128)} async-done(((f32[128,128,128]{2,1,0:T(8,128)}), f32[128,128,128]{2,1,0:T(8,128)}, u32[]{:S(2)}, u32[]{:S(2)}) %all-to-all-start.3) | async-done | bytes 8388640 | tf_op jit(solution)/shard_map/all_to_all | solution.py:109
  281.8 9.3 %copy.152 = f32[128,128,128]{0,2,1:T(8,128)} copy(f32[128,128,128]{2,1,0:T(8,128)} %all-to-all-done.3) | data formatting | bytes 16777216 | tf_op jit(solution)/shard_map/all_to_all | solution.py:109
  291.1 10.5 %fusion.15 = f32[16,4,128,128]{3,0,2,1:T(8,128)} fusion(f32[128,128,128]{0,2,1:T(8,128)} %copy.152, s32[128]{0:T(128)S(1)} %fusion.51, s32[16,4]{0,1:T(4,128)S(1)} %multiply_add_fusion, pred[128]{0:T(512)(128)(4,1)S(1)} %fusion.58), kind=kOutput, calls=%fused_computation.15 | convolution fusion | flops 1610629120 | bytes 12583808 | tf_op jit(solution)/shard_map/dot_general | solution.py:54
  301.6 0.9 collective-permute-start.3
  302.8 0.2 slice_reduce_fusion.1
  302.9 0.1 fusion.35
  303.1 0.1 reshape.181
  303.4 0.2 slice_reduce_fusion
  303.6 0.1 fusion.34
  303.7 0.1 reshape.182
  303.8 9.0 %collective-permute-start.1 = (f32[16,4]{1,0:T(8,128)S(1)}, f32[16,4]{1,0:T(8,128)S(1)}, u32[]{:S(2)}, u32[]{:S(2)}) collective-permute-start(f32[16,4]{1,0:T(8,128)S(1)} %reshape.182), channel_id=1, source_target_pairs={{0,112},{16,0},{32,16},{48,32},{64,48},{80,64},{96,80},{112,96},{1... | collective-permute-start | bytes 776 | tf_op jit(solution)/shard_map/ppermute | solution.py:15
  312.9 0.6 gather_fusion
  313.7 0.1 copy.142
  313.8 95.4 %collective-permute-done = f32[16,4]{1,0:T(8,128)S(1)} collective-permute-done((f32[16,4]{1,0:T(8,128)S(1)}, f32[16,4]{1,0:T(8,128)S(1)}, u32[]{:S(2)}, u32[]{:S(2)}) %collective-permute-start) | collective-permute-done | bytes 288 | tf_op jit(solution)/shard_map/ppermute | solution.py:15
  409.3 0.6 gather_fusion.2
  410.2 2.5 collective-permute-start.4
  412.8 5.8 collective-permute-start.5
  418.7 0.7 collective-permute-done.5
  419.4 0.6 gather_fusion.4
  420.3 5.5 copy.148
  425.8 10.9 %gather_fusion.1 = f32[64,4,128,128]{3,2,1,0:T(8,128)} fusion(f32[16,4,128,128]{3,2,1,0:T(8,128)} %copy.148, s32[1024]{0:T(1024)S(1)} %pad_clamp_fusion.2), kind=kCustom, calls=%fused_computation.1.clone | custom fusion | bytes 33554688 | tf_op jit(solution)/shard_map/jit(_take)/gather | solution.py:67
  436.7 17.6 %copy.149 = f32[16,4,4,128,128]{3,4,2,1,0:T(8,128)} copy(f32[16,4,4,128,128]{4,3,2,1,0:T(8,128)} %bitcast.135) | data formatting | bytes 33554432 | tf_op jit(solution)/shard_map/jit(_take)/gather | solution.py:67
  454.3 5.3 collective-permute-start.6
  459.7 1.7 collective-permute-start.7
  461.3 20.3 %fusion.6 = f32[16,4,4,128,128]{3,4,2,1,0:T(8,128)} fusion(f32[16,4,4,128,128]{3,4,2,1,0:T(8,128)} %copy.149, pred[16,4]{1,0:T(8,128)(4,1)S(1)} %get-tuple-element.10, f32[16,4,128,128,1]{3,0,2,1,4:T(8,128)} %bitcast.30), kind=kOutput, calls=%fused_computation.12 | convolution fusion | flops 6446645248 | bytes 37748800 | tf_op jit(solution)/shard_map/rwij,rwvjl->rwvil/dot_general | solution.py:75
  481.6 19.8 %copy.154 = f32[16,4,4,128,128]{4,1,2,3,0:T(4,128)} copy(f32[16,4,4,128,128]{3,4,2,1,0:T(8,128)} %fusion.6) | data formatting | bytes 33554432 | tf_op jit(solution)/shard_map/rwij,rwvjl->rwvil/transpose | solution.py:75
  501.5 16.0 %fusion.39 = f32[16,6,128,128,1]{3,1,4,2,0:T(8,128)} fusion(f32[16,4,4,128,128]{4,1,2,3,0:T(4,128)} %copy.154, s32[16,6]{1,0:T(8,128)S(1)} %copy.143, s32[16,4,4]{1,2,0:T(4,128)S(1)} %copy.142, pred[16,6]{1,0:T(8,128)(4,1)S(1)} %copy.144, pred[16,4]{1,0:T(8,128)(4,1)S(1)} %get-tuple-element.9), kind=kOutput, calls=%fused_computation.45 | convolution fusion | flops 301994496 | bytes 23070240 | tf_op jit(solution)/shard_map/rtwv,rwvil->rtil/dot_general | solution.py:76
  517.5 5.5 copy.159
  523.1 11.0 %gather_fusion.3 = f32[64,4,128,128]{3,2,1,0:T(8,128)} fusion(f32[16,4,128,128]{3,2,1,0:T(8,128)} %copy.159, s32[1024]{0:T(1024)S(1)} %pad_clamp_fusion.1), kind=kCustom, calls=%fused_computation.4.clone | custom fusion | bytes 33554688 | tf_op jit(solution)/shard_map/jit(_take)/gather | solution.py:67
  534.0 17.6 %copy.160 = f32[16,4,4,128,128]{3,4,2,1,0:T(8,128)} copy(f32[16,4,4,128,128]{4,3,2,1,0:T(8,128)} %bitcast.136) | data formatting | bytes 33554432 | tf_op jit(solution)/shard_map/jit(_take)/gather | solution.py:67
  551.7 20.5 %fusion.9 = f32[16,4,4,128,128]{3,4,2,1,0:T(8,128)} fusion(f32[16,4,4,128,128]{3,4,2,1,0:T(8,128)} %copy.160, pred[16,4]{1,0:T(8,128)(4,1)S(1)} %get-tuple-element.12, f32[16,4,128,128,1]{3,0,2,1,4:T(8,128)} %bitcast.38), kind=kOutput, calls=%fused_computation.13 | convolution fusion | flops 6446645248 | bytes 37748800 | tf_op jit(solution)/shard_map/rwij,rwvjl->rwvil/dot_general | solution.py:75
  572.2 19.8 %copy.162 = f32[16,4,4,128,128]{4,1,2,3,0:T(4,128)} copy(f32[16,4,4,128,128]{3,4,2,1,0:T(8,128)} %fusion.9) | data formatting | bytes 33554432 | tf_op jit(solution)/shard_map/rwij,rwvjl->rwvil/transpose | solution.py:75
  592.0 16.0 %fusion.37 = f32[16,6,128,128,1]{3,1,4,2,0:T(8,128)} fusion(f32[16,4,4,128,128]{4,1,2,3,0:T(4,128)} %copy.162, s32[16,4,4]{1,2,0:T(4,128)S(1)} %copy.158, s32[16,6]{1,0:T(8,128)S(1)} %copy.143, pred[16,4]{1,0:T(8,128)(4,1)S(1)} %get-tuple-element.11, pred[16,6]{1,0:T(8,128)(4,1)S(1)} %copy.144), kind=kOutput, calls=%fused_computation.43 | convolution fusion | flops 301994496 | bytes 23070240 | tf_op jit(solution)/shard_map/rtwv,rwvil->rtil/dot_general | solution.py:76
  608.1 5.6 copy.167
  613.6 11.0 %gather_fusion.5 = f32[64,4,128,128]{3,2,1,0:T(8,128)} fusion(f32[16,4,128,128]{3,2,1,0:T(8,128)} %copy.167, s32[1024]{0:T(1024)S(1)} %pad_clamp_fusion), kind=kCustom, calls=%fused_computation.5.clone | custom fusion | bytes 33554688 | tf_op jit(solution)/shard_map/jit(_take)/gather | solution.py:67
  624.6 17.6 %copy.168 = f32[16,4,4,128,128]{3,4,2,1,0:T(8,128)} copy(f32[16,4,4,128,128]{4,3,2,1,0:T(8,128)} %bitcast.137) | data formatting | bytes 33554432 | tf_op jit(solution)/shard_map/jit(_take)/gather | solution.py:67
  642.2 20.6 %fusion.12 = f32[16,4,4,128,128]{3,4,2,1,0:T(8,128)} fusion(f32[16,4,4,128,128]{3,4,2,1,0:T(8,128)} %copy.168, pred[16,4]{1,0:T(8,128)(4,1)S(1)} %get-tuple-element.8, f32[16,4,128,128,1]{3,0,2,1,4:T(8,128)} %bitcast.46), kind=kOutput, calls=%fused_computation.14 | convolution fusion | flops 6446645248 | bytes 37748800 | tf_op jit(solution)/shard_map/rwij,rwvjl->rwvil/dot_general | solution.py:75
  662.8 19.8 %copy.170 = f32[16,4,4,128,128]{4,1,2,3,0:T(4,128)} copy(f32[16,4,4,128,128]{3,4,2,1,0:T(8,128)} %fusion.12) | data formatting | bytes 33554432 | tf_op jit(solution)/shard_map/rwij,rwvjl->rwvil/transpose | solution.py:75
  682.6 16.8 %bitcast_add_fusion = f32[16,6,128,128]{3,1,2,0:T(8,128)S(1)} fusion(f32[16,6,128,128,1]{3,1,4,2,0:T(8,128)} %fusion.37, f32[16,6,128,128,1]{3,1,4,2,0:T(8,128)} %fusion.39, f32[16,4,4,128,128]{4,1,2,3,0:T(4,128)} %copy.170, s32[16,4,4]{1,2,0:T(4,128)S(1)} %copy.166, s32[16,6]{1,0:T(8,128)S(1)} %copy.143, pred[16,4]{1,0:T(8,128)(4,1)S(1)} %get-tuple-element.6, ...), kind=kOutput, calls=%fused_computation.19 | convolution fusion | flops 305140224 | bytes 35653152 | tf_op jit(solution)/shard_map/rtwv,rwvil->rtil/dot_general | solution.py:76
  699.4 3.8 copy.171
  (51 shorter events, 2.4 us)
Async XLA Ops:
  2.6 18.3 %all-to-all-start.1 = ((f32[128,1,3]{2,1,0:T(1,128)}), f32[128,1,3]{2,1,0:T(1,128)S(1)}, u32[]{:S(2)}, u32[]{:S(2)}) async-start(f32[128,1,3]{2,1,0:T(1,128)} %bitcast.64), calls=%async_computation.1 | async-start | bytes 131072 | tf_op jit(solution)/shard_map/all_to_all | solution.py:112
  20.9 22.9 %all-to-all-start = ((f32[128,1,3]{2,1,0:T(1,128)}), f32[128,1,3]{2,1,0:T(1,128)S(1)}, u32[]{:S(2)}, u32[]{:S(2)}) async-start(f32[128,1,3]{2,1,0:T(1,128)} %bitcast.63), calls=%async_computation | async-start | bytes 131072 | tf_op jit(solution)/shard_map/all_to_all | solution.py:110
  43.8 10.4 %copy-start = (f32[32,128,128]{2,1,0:T(8,128)S(1)}, f32[32,128,128]{2,1,0:T(8,128)}, u32[]{:S(2)}) copy-start(f32[32,128,128]{2,1,0:T(8,128)} %param.11) | copy-start | bytes 6291460
  43.8 117.3 %all-to-all-start.2 = ((f32[128,128,128]{2,1,0:T(8,128)}), f32[128,128,128]{2,1,0:T(8,128)}, u32[]{:S(2)}, u32[]{:S(2)}) async-start(f32[128,128,128]{2,1,0:T(8,128)} %copy.146), calls=%async_computation.2 | async-start | bytes 16777216 | tf_op jit(solution)/shard_map/all_to_all | solution.py:111
  161.1 120.7 %all-to-all-start.3 = ((f32[128,128,128]{2,1,0:T(8,128)}), f32[128,128,128]{2,1,0:T(8,128)}, u32[]{:S(2)}, u32[]{:S(2)}) async-start(f32[128,128,128]{2,1,0:T(8,128)} %copy.151), calls=%async_computation.3 | async-start | bytes 16777216 | tf_op jit(solution)/shard_map/all_to_all | solution.py:109
  191.1 263.2 %collective-permute-start.2 = (f32[16,4,128,128]{3,0,2,1:T(8,128)}, f32[16,4,128,128]{3,0,2,1:T(8,128)}, u32[]{:S(2)}, u32[]{:S(2)}) collective-permute-start(f32[16,4,128,128]{3,0,2,1:T(8,128)} %fusion.17), channel_id=1, source_target_pairs={{0,112},{16,0},{32,16},{48,32},{64,48},{80,64},{96,80},{112,96},{1... | collective-permute-start | bytes 12582920 | tf_op jit(solution)/shard_map/ppermute | solution.py:15
  291.1 11.3 %copy-start.1 = (s32[16,6]{0,1:T(8,128)S(1)}, s32[16,6]{0,1:T(8,128)}, u32[]{:S(2)}) copy-start(s32[16,6]{0,1:T(8,128)} %param.17) | copy-start | bytes 1156
  301.6 158.1 %collective-permute-start.3 = (f32[16,4,128,128]{3,0,2,1:T(8,128)}, f32[16,4,128,128]{3,0,2,1:T(8,128)}, u32[]{:S(2)}, u32[]{:S(2)}) collective-permute-start(f32[16,4,128,128]{3,0,2,1:T(8,128)} %fusion.15), channel_id=1, source_target_pairs={{0,15},{1,0},{2,1},{3,2},{4,3},{5,4},{6,5},{7,6},{8,7},{9,8},{10,9... | collective-permute-start | bytes 12582920 | tf_op jit(solution)/shard_map/ppermute | solution.py:15
  303.2 106.0 %collective-permute-start = (f32[16,4]{1,0:T(8,128)S(1)}, f32[16,4]{1,0:T(8,128)S(1)}, u32[]{:S(2)}, u32[]{:S(2)}) collective-permute-start(f32[16,4]{1,0:T(8,128)S(1)} %reshape.181), channel_id=1, source_target_pairs={{0,15},{1,0},{2,1},{3,2},{4,3},{5,4},{6,5},{7,6},{8,7},{9,8},{10,9... | collective-permute-start | bytes 776 | tf_op jit(solution)/shard_map/ppermute | solution.py:15
  303.8 105.5 %collective-permute-start.1 = (f32[16,4]{1,0:T(8,128)S(1)}, f32[16,4]{1,0:T(8,128)S(1)}, u32[]{:S(2)}, u32[]{:S(2)}) collective-permute-start(f32[16,4]{1,0:T(8,128)S(1)} %reshape.182), channel_id=1, source_target_pairs={{0,112},{16,0},{32,16},{48,32},{64,48},{80,64},{96,80},{112,96},{1... | collective-permute-start | bytes 776 | tf_op jit(solution)/shard_map/ppermute | solution.py:15
  410.2 8.4 %collective-permute-start.4 = (f32[16,4]{1,0:T(8,128)S(1)}, f32[16,4]{1,0:T(8,128)S(1)}, u32[]{:S(2)}, u32[]{:S(2)}) collective-permute-start(f32[16,4]{1,0:T(8,128)S(1)} %collective-permute-done), channel_id=1, source_target_pairs={{0,15},{1,0},{2,1},{3,2},{4,3},{5,4},{6,5},{7,6},{8,7},{9,8},{10,9... | collective-permute-start | bytes 776 | tf_op jit(solution)/shard_map/ppermute | solution.py:15
  412.8 6.6 collective-permute-start.5
  454.3 153.7 %collective-permute-start.6 = (f32[16,4,128,128]{3,0,2,1:T(8,128)}, f32[16,4,128,128]{3,0,2,1:T(8,128)}, u32[]{:S(2)}, u32[]{:S(2)}) collective-permute-start(f32[16,4,128,128]{3,0,2,1:T(8,128)} %collective-permute-done.2), channel_id=1, source_target_pairs={{0,112},{16,0},{32,16},{48,32},{64,48},{80,64},{96,80},{112,96},{1... | collective-permute-start | bytes 12582920 | tf_op jit(solution)/shard_map/ppermute | solution.py:15
  459.7 182.6 %collective-permute-start.7 = (f32[16,4,128,128]{3,0,2,1:T(8,128)}, f32[16,4,128,128]{3,0,2,1:T(8,128)}, u32[]{:S(2)}, u32[]{:S(2)}) collective-permute-start(f32[16,4,128,128]{3,0,2,1:T(8,128)} %collective-permute-done.3), channel_id=1, source_target_pairs={{0,15},{1,0},{2,1},{3,2},{4,3},{5,4},{6,5},{7,6},{8,7},{9,8},{10,9... | collective-permute-start | bytes 12582920 | tf_op jit(solution)/shard_map/ppermute | solution.py:15
where the time goes:
time: 714 us; the launch traced here: 704 us
  waiting for transfers between devices  278 us (39%)
  local copies, waits for them, and re-layouts  205 us (29%)
  matrix products  149 us (21%)
  starting transfers between devices  67.1 us (9%)
    ppermute x8, waiting for transfers between devices, shifted(): return lax.ppermute(value, axis, pairs)  96.1 us
    all_to_all x1, waiting for transfers between devices, on_device(): lax.all_to_all(send_right, ('row', 'col'), split_axis=0, concat_axis=0, t...  91.1 us
    all_to_all x1, waiting for transfers between devices, on_device(): lax.all_to_all(send_left, ('row', 'col'), split_axis=0, concat_axis=0, ti...  86 us
    gather x6, local copies, waits for them, and re-layouts, panel_products(): chosen = jnp.take(right, safe, axis=0)  85.7 us
    dot_general x3, matrix products, panel_products(): jnp.einsum('rwij,rwvjl->rwvil', left, chosen, precision=lax.Precision.HIG...  61.5 us
    transpose x3, local copies, waits for them, and re-layouts, panel_products(): jnp.einsum('rwij,rwvjl->rwvil', left, chosen, precision=lax.Precision.HIG...  59.5 us
    dot_general x3, matrix products, panel_products(): jnp.einsum('rtwv,rwvil->rtil', match, pieces, precision=lax.Precision.HIG...  48.9 us
    ppermute x8, starting transfers between devices, shifted(): return lax.ppermute(value, axis, pairs)  29.9 us
  transfers between devices with their start and end apart: 12, of which 5 were waited for; matrix products, arithmetic and copies ran while one was open for 42% of the time, Pallas kernels for 0%

commit v1 on v0

v1 whole, which is shorter than its diff:
```python
import functools

import jax
import jax.numpy as jnp
from jax import lax
from jax.experimental import pallas as pl
from jax.experimental.pallas import tpu as pltpu
from jax.sharding import PartitionSpec as P

KPB = 16
WA = 4
WB = 4
STEPS = 3
HBM = pl.BlockSpec(memory_space=pl.ANY)


def shifted(value, axis, steps):
    count = lax.axis_size(axis)
    pairs = [(source, (source + steps) % count) for source in range(count)]
    return lax.ppermute(value, axis, pairs)


def pack_right_kernel(dest, held, out, sems):
    count = held.shape[0]

    def copy(entry):
        return pltpu.make_async_copy(held.at[entry], out.at[dest[entry]], sems.at[entry])

    pl.loop(0, count)(lambda entry: copy(entry).start())
    pl.loop(0, count)(lambda entry: copy(entry).wait())


def pack_left_kernel(copies, dest, held, out, sems):
    count = held.shape[0]
    part = out.shape[1]

    def copy(entry, half):
        return pltpu.make_async_copy(
            held.at[entry, pl.ds(half * part, part)],
            out.at[dest[half, entry]],
            sems.at[half, entry],
        )

    for half in range(copies):
        pl.loop(0, count)(lambda entry: copy(entry, half).start())
    for half in range(copies):
        pl.loop(0, count)(lambda entry: copy(entry, half).wait())


def collect_kernel(source, recv, out, sems):
    count = out.shape[0]

    def copy(slot):
        return pltpu.make_async_copy(recv.at[source[slot]], out.at[slot], sems.at[slot])

    pl.loop(0, count)(lambda slot: copy(slot).start())
    pl.loop(0, count)(lambda slot: copy(slot).wait())


SMEM = pl.BlockSpec(memory_space=pltpu.SMEM)


def pack_right(held, dest, devices):
    return pl.pallas_call(
        pack_right_kernel,
        out_shape=jax.ShapeDtypeStruct((devices,) + held.shape[1:], held.dtype),
        in_specs=[SMEM, HBM],
        out_specs=HBM,
        scratch_shapes=[pltpu.SemaphoreType.DMA((held.shape[0],))],
        name="pack_right",
    )(dest, held)


def pack_left(held, dest, devices):
    copies = dest.shape[0]
    count, rows, cols = held.shape
    return pl.pallas_call(
        functools.partial(pack_left_kernel, copies),
        out_shape=jax.ShapeDtypeStruct((devices, rows // copies, cols), held.dtype),
        in_specs=[SMEM, HBM],
        out_specs=HBM,
        scratch_shapes=[pltpu.SemaphoreType.DMA((copies, count))],
        name="pack_left",
    )(dest, held)


def collect(recv, source):
    return pl.pallas_call(
        collect_kernel,
        out_shape=jax.ShapeDtypeStruct(source.shape + recv.shape[1:], recv.dtype),
        in_specs=[SMEM, HBM],
        out_specs=HBM,
        scratch_shapes=[pltpu.SemaphoreType.DMA(source.shape)],
        name="collect",
    )(source, recv)


def split(value):
    high = value.astype(jnp.bfloat16)
    low = (value - high.astype(jnp.float32)).astype(jnp.bfloat16)
    return high, low


def product_kernel(steps, width, index, order, *refs):
    halves = refs[: 2 * steps]
    rights = refs[2 * steps : 3 * steps]
    out = refs[3 * steps]
    buf, high, low, sems = refs[3 * steps + 1 :]
    row = pl.program_id(0)
    slots = rights[0].shape[0]
    edge = out.shape[-1]
    group = buf.shape[1]
    chunks = steps * slots // group

    @pl.when(row == 0)
    def _():
        per = slots // group

        def copy(at):
            return pltpu.make_async_copy(
                rights[at // per].at[pl.ds((at % per) * group, group)], buf.at[at % 2], sems.at[at % 2]
            )

        copy(0).start()
        for at in range(chunks):
            if at + 1 < chunks:
                copy(at + 1).start()
            copy(at).wait()
            step, first = at // per, (at % per) * group

            def body(slot):
                hi, lo = split(buf[at % 2, slot])
                high[step, first + slot] = hi
                low[step, first + slot] = lo

            pl.loop(0, group)(body)
        for step in range(steps):
            high[step, slots] = jnp.zeros((edge, edge), jnp.bfloat16)
            low[step, slots] = jnp.zeros((edge, edge), jnp.bfloat16)

    for kept in range(width):
        out[0, kept] = jnp.zeros((edge, edge), jnp.float32)
    for step in range(steps):
        swap = order[step]
        for slot in range(WA):
            first, second = halves[2 * step][slot], halves[2 * step + 1][slot]
            left = jnp.concatenate(
                [jnp.where(swap > 0, second, first), jnp.where(swap > 0, first, second)], axis=0
            )
            a_hi, a_lo = split(left)
            both = jnp.concatenate([a_hi, a_lo], axis=1)
            for kept in range(width):
                at = index[((row * steps + step) * WA + slot) * width + kept]
                b_hi = high[step, at]
                b_lo = low[step, at]
                out[0, kept] += jnp.dot(
                    both, jnp.concatenate([b_hi, b_hi], axis=0), preferred_element_type=jnp.float32
                ) + jnp.dot(a_hi, b_lo, preferred_element_type=jnp.float32)


def products(index, order, halves, rights, rows, width):
    steps = len(rights)
    slots, edge, _ = rights[0].shape
    part = halves[0].shape[1]
    group = 16
    left_spec = pl.BlockSpec((WA, part, edge), lambda row, *_: (row, 0, 0))
    return pl.pallas_call(
        functools.partial(product_kernel, steps, width),
        grid_spec=pltpu.PrefetchScalarGridSpec(
            num_scalar_prefetch=2,
            grid=(rows,),
            in_specs=[left_spec] * len(halves) + [HBM] * steps,
            out_specs=pl.BlockSpec((1, width, edge, edge), lambda row, *_: (row, 0, 0, 0)),
            scratch_shapes=[
                pltpu.VMEM((2, group, edge, edge), jnp.float32),
                pltpu.VMEM((steps, slots + 1, edge, edge), jnp.bfloat16),
                pltpu.VMEM((steps, slots + 1, edge, edge), jnp.bfloat16),
                pltpu.SemaphoreType.DMA((2,)),
            ],
        ),
        out_shape=jax.ShapeDtypeStruct((rows, width, edge, edge), jnp.float32),
        compiler_params=pltpu.CompilerParams(
            dimension_semantics=("arbitrary",), vmem_limit_bytes=40 * 1024 * 1024
        ),
        name="products",
    )(index, order, *halves, *rights)


def on_device(a_held, a_slot, a_col, b_held, b_slot, b_col, c_col):
    grid_rows = lax.axis_size("row")
    grid_cols = lax.axis_size("col")
    devices = grid_rows * grid_cols
    copies = grid_cols // grid_rows
    i = lax.axis_index("row")
    c = lax.axis_index("col")
    rows, width = c_col.shape
    hold_a, hold_b = a_slot.shape[0], b_slot.shape[0]
    slots_a, slots_b = rows * WA, KPB * WB

    panel = a_slot // slots_a
    at_row, inner = panel // grid_rows, panel % grid_rows
    dest = at_row * grid_cols + (inner - at_row - 1) % grid_rows
    dest_left = dest[None, :] + grid_rows * jnp.arange(copies, dtype=jnp.int32)[:, None]
    panel = b_slot // slots_b
    inner, at_col = panel // grid_cols, panel % grid_cols
    dest_right = ((inner - at_col - 1) % grid_rows) * grid_cols + at_col

    labels = lax.all_gather(jnp.concatenate([a_slot, a_col, b_slot, b_col]), ("row", "col"))
    parts = [hold_a, 2 * hold_a, 2 * hold_a + hold_b]
    all_a, all_acol, all_b, all_bcol = (part.reshape(-1) for part in jnp.split(labels, parts, axis=1))

    k = (i + c + jnp.arange(STEPS, dtype=jnp.int32)) % grid_rows

    def look_up(panels, slots, table, columns, hold):
        wanted = panels[:, None] * slots + jnp.arange(slots, dtype=jnp.int32)[None, :]
        holder = jnp.arange(table.shape[0], dtype=jnp.int32) // hold
        code = holder * 32 + columns + 1
        found = jnp.sum(jnp.where(table[None, None, :] == wanted[:, :, None], code, 0), axis=2)
        return found // 32, found % 32 - 1

    src_left, col_left = look_up(i * grid_rows + k, slots_a, all_a, all_acol, hold_a)
    src_right, col_right = look_up(k * grid_cols + c, slots_b, all_b, all_bcol, hold_b)

    u = jnp.arange(slots_b, dtype=jnp.int32)
    lefts = col_left.reshape(STEPS, rows, WA).transpose(1, 0, 2)[:, :, :, None, None]
    hit = (
        (lefts == (u // WB))
        & (col_right[None, :, None, None, :] == c_col[:, None, None, :, None])
        & (c_col >= 0)[:, None, None, :, None]
    )
    index = slots_b - jnp.sum(jnp.where(hit, slots_b - u, 0), axis=4)
    index = index.reshape(-1).astype(jnp.int32)

    send_left = pack_left(a_held, dest_left, devices)
    send_right = pack_right(b_held, dest_right, devices)
    recv_left = lax.all_to_all(send_left, ("row", "col"), split_axis=0, concat_axis=0, tiled=True)
    recv_right = lax.all_to_all(send_right, ("row", "col"), split_axis=0, concat_axis=0, tiled=True)

    own = collect(recv_left, src_left[1])
    other = shifted(own, "col", grid_rows)
    right = collect(recv_right, src_right[1])
    halves = [
        shifted(own, "col", 1),
        shifted(other, "col", 1),
        own,
        other,
        shifted(own, "col", -1),
        shifted(other, "col", -1),
    ]
    rights = [shifted(right, "row", 1), right, shifted(right, "row", -1)]
    homes = (c + jnp.arange(-1, 2, dtype=jnp.int32)) % grid_cols
    order = (homes >= grid_rows).astype(jnp.int32)
    return products(index, order, halves, rights, rows, width)


def solution(mesh):
    return jax.shard_map(
        on_device,
        mesh=mesh,
        in_specs=(
            P(("row", "col"), None, None),
            P(("row", "col")),
            P(("row", "col")),
            P(("row", "col"), None, None),
            P(("row", "col")),
            P(("row", "col")),
            P("row", "col"),
        ),
        out_specs=P("row", "col", None, None),
        check_vma=False,
    )
```

time: 714 us -> 860 us (1.20)
  the two profiles are of different devices: /device:TPU:11 before, /device:TPU:26 now
where the time goes in v1:
time: 860 us; the launch traced here: 856 us
  Pallas kernels  435 us (51%)
  waiting for transfers between devices  369 us (43%)
  starting transfers between devices  29.7 us (3%)
  between operations  13.7 us (2%)
    unnamed x2, waiting for transfers between devices  215 us
    pallas_call x2, Pallas kernels, collect(): pl.pallas_call(collect_kernel, out_shape=jax.ShapeDtypeStruct(source.shap...  195 us
    ppermute x7, waiting for transfers between devices, shifted(): return lax.ppermute(value, axis, pairs)  155 us
    pallas_call x1, Pallas kernels, pack_right(): pl.pallas_call(pack_right_kernel, out_shape=jax.ShapeDtypeStruct((devices...  129 us
    pallas_call x1, Pallas kernels, pack_left(): pl.pallas_call(functools.partial(pack_left_kernel, copies), out_shape=jax...  65.9 us
    pallas_call x1, Pallas kernels, products(): pl.pallas_call(functools.partial(product_kernel, steps, width), grid_spec...  44.3 us
  transfers between devices with their start and end apart: 10, of which 3 were waited for; matrix products, arithmetic and copies ran while one was open for 1% of the time, Pallas kernels for 38%

profile of v1, /device:TPU:26, one launch (start us, length us, event | category | flops | bytes accessed | tf_op | source)
XLA Modules:
  0.0 856.5 jit_solution(7705154631556071155)
XLA Ops:
  6.5 0.7 fusion.20
  7.2 0.6 broadcast_add_fusion.dest
  7.8 65.9 %pack_left.1 = f32[128,64,128]{2,1,0:T(8,128)} custom-call(s32[2,32]{1,0:T(2,128)} %broadcast_add_fusion.dest, f32[32,128,128]{2,1,0:T(8,128)} %held.2), custom_call_target="tpu_custom_call" | custom-call | tf_op jit(solution)/shard_map/pack_left/pallas_call | solution.py:77
  73.7 0.0 copy-start.4
  73.7 10.7 %all-to-all-start = ((f32[128,64,128]{2,1,0:T(8,128)}), f32[128,64,128]{2,1,0:T(8,128)}, u32[]{:S(2)}, u32[]{:S(2)}) async-start(f32[128,64,128]{2,1,0:T(8,128)} %pack_left.1), calls=%async_computation | async-start | bytes 8388608 | tf_op jit(solution)/shard_map/all_to_all | solution.py:236
  84.5 0.0 copy-done.4
  84.5 0.5 fusion.22.dest
  85.0 129.4 %pack_right.1 = f32[128,128,128]{2,1,0:T(8,128)} custom-call(s32[64]{0:T(128)} %fusion.22.dest, f32[64,128,128]{2,1,0:T(8,128)} %held.3), custom_call_target="tpu_custom_call" | custom-call | tf_op jit(solution)/shard_map/pack_right/pallas_call | solution.py:64
  214.4 0.0 copy-start.3
  214.4 0.0 copy-start.5
  214.4 0.0 copy-start.6
  214.5 0.0 all-to-all-done.recv
  214.5 10.2 %all-to-all-start.1 = ((f32[128,128,128]{2,1,0:T(8,128)}), f32[128,128,128]{2,1,0:T(8,128)}, u32[]{:S(2)}, u32[]{:S(2)}) async-start(f32[128,128,128]{2,1,0:T(8,128)} %pack_right.1), calls=%async_computation.1 | async-start | bytes 16777216 | tf_op jit(solution)/shard_map/all_to_all | solution.py:237
  224.7 0.0 all-reduce.3.cloned.1.call-start
  224.8 0.0 copy-done.3
  224.8 0.0 copy-done.5
  224.8 0.0 copy-done.6
  224.8 0.2 add_dynamic-update-slice_fusion
  225.0 0.0 copy-start.1
  225.0 0.6 copy-done.1
  225.6 0.0 all-reduce.3.cloned.1.call-update
  225.7 0.1 iota_add_fusion
  225.8 0.1 iota_add_fusion.1
  225.8 214.7 %all-reduce.3.cloned.1.call-done = s32[24576]{0:T(1024)} async-done(((s32[24576]{0:T(1024)}), s32[24576]{0:T(1024)}) %all-reduce.3.cloned.1.call-update) | async-done | bytes 98320
  440.5 1.0 reshape.129
  441.5 0.1 fusion.28
  441.6 0.1 eq.85
  441.7 0.1 fusion.27
  441.7 0.1 eq.78
  441.8 0.1 reshape.127
  441.9 0.1 reshape.128
  442.0 0.5 select_reduce_fusion.1
  442.5 0.6 slice_bitcast_fusion.1.source
  443.1 0.9 select_reduce_fusion
  444.0 0.5 slice_bitcast_fusion.source
  444.5 65.9 %collect.2.refs_2_ = f32[64,64,128]{2,1,0:T(8,128)} custom-call(s32[64]{0:T(128)} %slice_bitcast_fusion.1.source, f32[128,64,128]{2,1,0:T(8,128)} %all-to-all-done.recv), custom_call_target="tpu_custom_call" | custom-call | tf_op jit(solution)/shard_map/collect/pallas_call | solution.py:88
  510.4 0.0 copy-start
  510.4 0.0 copy-start.2
  510.4 2.1 collective-permute-start.1
  512.4 1.0 collective-permute-start.3
  513.4 0.0 all-to-all-done.1.recv
  513.4 129.4 %collect.3.refs_7_ = f32[64,128,128]{2,1,0:T(8,128)} custom-call(s32[64]{0:T(128)} %slice_bitcast_fusion.source, f32[128,128,128]{2,1,0:T(8,128)} %all-to-all-done.1.recv), custom_call_target="tpu_custom_call" | custom-call | tf_op jit(solution)/shard_map/collect/pallas_call | solution.py:88
  642.8 1.6 collective-permute-start.6
  644.5 0.5 collective-permute-start.5
  644.9 0.0 copy-done
  644.9 0.0 collective-permute-start
  644.9 0.0 collective-permute-done.1.refs_3_
  644.9 1.7 collective-permute-start.4
  646.7 0.0 collective-permute-done.3.refs_4_
  646.7 1.8 collective-permute-start.2
  648.6 0.0 copy-done.2
  648.6 0.1 reduce_sum.30
  648.7 0.1 copy.14
  648.8 0.1 broadcast_compare_fusion.1
  648.9 0.1 broadcast_compare_fusion
  649.0 1.4 select_reduce_fusion.2
  650.4 0.2 copy.15
  650.5 0.2 sub.91.index
  650.7 131.7 %collective-permute-done.refs_0_ = f32[64,64,128]{2,1,0:T(8,128)} collective-permute-done((f32[64,64,128]{2,1,0:T(8,128)S(1)}, f32[64,64,128]{2,1,0:T(8,128)}, u32[]{:S(2)}, u32[]{:S(2)}) %collective-permute-start) | collective-permute-done | bytes 2097184 | tf_op jit(solution)/shard_map/ppermute | solution.py:20
  782.4 0.0 collective-permute-done.4.refs_5_
  782.4 22.9 %collective-permute-done.2.refs_1_ = f32[64,64,128]{2,1,0:T(8,128)} collective-permute-done((f32[64,64,128]{2,1,0:T(8,128)}, f32[64,64,128]{2,1,0:T(8,128)}, u32[]{:S(2)}, u32[]{:S(2)}) %collective-permute-start.2) | collective-permute-done | bytes 2097184 | tf_op jit(solution)/shard_map/ppermute | solution.py:20
  805.3 0.0 collective-permute-done.6.refs_8_
  805.3 0.0 collective-permute-done.5.refs_6_
  805.3 44.3 %products.1 = f32[16,6,128,128]{3,2,1,0:T(8,128)} custom-call(s32[1152]{0:T(1024)S(1)} %sub.91.index, s32[3]{0:T(128)S(1)} %compare_convert_fusion.order, f32[64,64,128]{2,1,0:T(8,128)} %collective-permute-done.refs_0_, f32[64,64,128]{2,1,0:T(8,128)} %collective-permute-done.2.refs_1_, f32[64,64,128]{2,1,0:T(8,128)S(1)} %copy-done, ...), custom_call_target="tpu_custom_call" | custom-call | tf_op jit(solution)/shard_map/products/pallas_call | solution.py:167
  (13 shorter events, 0.1 us)
Async XLA Ops:
  73.7 10.7 %copy-start.4 = (s32[64]{0:T(128)S(1)}, s32[64]{0:T(128)}, u32[]{:S(2)}) copy-start(s32[64]{0:T(128)} %param.11) | copy-start | bytes 772
  73.7 140.7 %all-to-all-start = ((f32[128,64,128]{2,1,0:T(8,128)}), f32[128,64,128]{2,1,0:T(8,128)}, u32[]{:S(2)}, u32[]{:S(2)}) async-start(f32[128,64,128]{2,1,0:T(8,128)} %pack_left.1), calls=%async_computation | async-start | bytes 8388608 | tf_op jit(solution)/shard_map/all_to_all | solution.py:236
  214.4 10.4 %copy-start.3 = (s32[64]{0:T(128)S(1)}, s32[64]{0:T(128)}, u32[]{:S(2)}) copy-start(s32[64]{0:T(128)} %param.12) | copy-start | bytes 772
  214.4 10.4 %copy-start.5 = (s32[32]{0:T(128)S(1)}, s32[32]{0:T(128)}, u32[]{:S(2)}) copy-start(s32[32]{0:T(128)} %param.9) | copy-start | bytes 388
  214.4 10.4 %copy-start.6 = (s32[32]{0:T(128)S(1)}, s32[32]{0:T(128)}, u32[]{:S(2)}) copy-start(s32[32]{0:T(128)} %param.8) | copy-start | bytes 388
  214.5 298.9 %all-to-all-start.1 = ((f32[128,128,128]{2,1,0:T(8,128)}), f32[128,128,128]{2,1,0:T(8,128)}, u32[]{:S(2)}, u32[]{:S(2)}) async-start(f32[128,128,128]{2,1,0:T(8,128)} %pack_right.1), calls=%async_computation.1 | async-start | bytes 16777216 | tf_op jit(solution)/shard_map/all_to_all | solution.py:237
  224.7 215.8 %all-reduce.3.cloned.1.call-start = ((), (), s32[]{:S(2)}) async-start(), calls=%async_computation.2 | async-start | bytes 196608
  225.0 0.6 copy-start.1
  510.4 134.6 %copy-start = (f32[64,64,128]{2,1,0:T(8,128)S(1)}, f32[64,64,128]{2,1,0:T(8,128)}, u32[]{:S(2)}) copy-start(f32[64,64,128]{2,1,0:T(8,128)} %collect.2.refs_2_) | copy-start | bytes 6291460
  510.4 138.2 %copy-start.2 = (s32[16,6]{0,1:T(8,128)S(1)}, s32[16,6]{0,1:T(8,128)}, u32[]{:S(2)}) copy-start(s32[16,6]{0,1:T(8,128)} %param.13) | copy-start | bytes 1156
  510.4 134.5 %collective-permute-start.1 = (f32[64,64,128]{2,1,0:T(8,128)}, f32[64,64,128]{2,1,0:T(8,128)}, u32[]{:S(2)}, u32[]{:S(2)}) collective-permute-start(f32[64,64,128]{2,1,0:T(8,128)} %collect.2.refs_2_), channel_id=1, source_target_pairs={{0,8},{1,9},{2,10},{3,11},{4,12},{5,13},{6,14},{7,15},{8,0},{9,1},... | collective-permute-start | bytes 6291464 | tf_op jit(solution)/shard_map/ppermute | solution.py:20
  512.4 134.2 %collective-permute-start.3 = (f32[64,64,128]{2,1,0:T(8,128)}, f32[64,64,128]{2,1,0:T(8,128)}, u32[]{:S(2)}, u32[]{:S(2)}) collective-permute-start(f32[64,64,128]{2,1,0:T(8,128)} %collect.2.refs_2_), channel_id=1, source_target_pairs={{0,15},{1,0},{2,1},{3,2},{4,3},{5,4},{6,5},{7,6},{8,7},{9,8},{10,9... | collective-permute-start | bytes 6291464 | tf_op jit(solution)/shard_map/ppermute | solution.py:20
  642.8 162.5 %collective-permute-start.6 = (f32[64,128,128]{2,1,0:T(8,128)}, f32[64,128,128]{2,1,0:T(8,128)}, u32[]{:S(2)}, u32[]{:S(2)}) collective-permute-start(f32[64,128,128]{2,1,0:T(8,128)} %collect.3.refs_7_), channel_id=1, source_target_pairs={{0,112},{16,0},{32,16},{48,32},{64,48},{80,64},{96,80},{112,96},{1... | collective-permute-start | bytes 12582920 | tf_op jit(solution)/shard_map/ppermute | solution.py:20
  644.5 160.8 %collective-permute-start.5 = (f32[64,128,128]{2,1,0:T(8,128)}, f32[64,128,128]{2,1,0:T(8,128)}, u32[]{:S(2)}, u32[]{:S(2)}) collective-permute-start(f32[64,128,128]{2,1,0:T(8,128)} %collect.3.refs_7_), channel_id=1, source_target_pairs={{0,16},{16,32},{32,48},{48,64},{64,80},{80,96},{96,112},{112,0},{1... | collective-permute-start | bytes 12582920 | tf_op jit(solution)/shard_map/ppermute | solution.py:20
  644.9 137.5 %collective-permute-start = (f32[64,64,128]{2,1,0:T(8,128)S(1)}, f32[64,64,128]{2,1,0:T(8,128)}, u32[]{:S(2)}, u32[]{:S(2)}) collective-permute-start(f32[64,64,128]{2,1,0:T(8,128)S(1)} %copy-done), channel_id=1, source_target_pairs={{0,1},{1,2},{2,3},{3,4},{4,5},{5,6},{6,7},{7,8},{8,9},{9,10},{10,1... | collective-permute-start | bytes 6291464 | tf_op jit(solution)/shard_map/ppermute | solution.py:20
  644.9 137.5 %collective-permute-start.4 = (f32[64,64,128]{2,1,0:T(8,128)}, f32[64,64,128]{2,1,0:T(8,128)}, u32[]{:S(2)}, u32[]{:S(2)}) collective-permute-start(f32[64,64,128]{2,1,0:T(8,128)} %collective-permute-done.1.refs_3_), channel_id=1, source_target_pairs={{0,15},{1,0},{2,1},{3,2},{4,3},{5,4},{6,5},{7,6},{8,7},{9,8},{10,9... | collective-permute-start | bytes 6291464 | tf_op jit(solution)/shard_map/ppermute | solution.py:20
  646.7 158.6 %collective-permute-start.2 = (f32[64,64,128]{2,1,0:T(8,128)}, f32[64,64,128]{2,1,0:T(8,128)}, u32[]{:S(2)}, u32[]{:S(2)}) collective-permute-start(f32[64,64,128]{2,1,0:T(8,128)} %collective-permute-done.1.refs_3_), channel_id=1, source_target_pairs={{0,1},{1,2},{2,3},{3,4},{4,5},{5,6},{6,7},{7,8},{8,9},{9,10},{10,1... | collective-permute-start | bytes 6291464 | tf_op jit(solution)/shard_map/ppermute | solution.py:20
Sparse Core Ops, SparseCore 0:
  230.3 210.2 all-reduce.2

commit v2 on v1

--- a/solution.py
+++ b/solution.py
@@ -20,41 +20,66 @@
     return lax.ppermute(value, axis, pairs)
 
 
-def pack_right_kernel(dest, held, out, sems):
+def permuted(value, axis, target):
+    count = lax.axis_size(axis)
+    return lax.ppermute(value, axis, [(at, target(at) % count) for at in range(count)])
+
+
+def relay(count, load, store):
+    pl.loop(0, count)(lambda at: load(at).start())
+
+    def body(at):
+        load(at).wait()
+        store(at)
+
+    pl.loop(0, count)(body)
+
+
+def pack_right_kernel(dest, held, out, buf, sems):
     count = held.shape[0]
 
-    def copy(entry):
-        return pltpu.make_async_copy(held.at[entry], out.at[dest[entry]], sems.at[entry])
-
-    pl.loop(0, count)(lambda entry: copy(entry).start())
-    pl.loop(0, count)(lambda entry: copy(entry).wait())
-
-
-def pack_left_kernel(copies, dest, held, out, sems):
+    def load(at):
+        return pltpu.make_async_copy(held.at[at], buf.at[at], sems.at[0, at])
+
+    def save(at):
+        return pltpu.make_async_copy(buf.at[at], out.at[dest[at]], sems.at[1, at])
+
+    relay(count, load, lambda at: save(at).start())
+    pl.loop(0, count)(lambda at: save(at).wait())
+
+
+def pack_left_kernel(copies, dest, held, out, buf, sems):
     count = held.shape[0]
     part = out.shape[1]
 
-    def copy(entry, half):
+    def load(at):
+        return pltpu.make_async_copy(held.at[at], buf.at[at], sems.at[0, at])
+
+    def save(at, half):
         return pltpu.make_async_copy(
-            held.at[entry, pl.ds(half * part, part)],
-            out.at[dest[half, entry]],
-            sems.at[half, entry],
+            buf.at[at, pl.ds(half * part, part)], out.at[dest[half, at]], sems.at[1 + half, at]
         )
 
+    def store(at):
+        for half in range(copies):
+            save(at, half).start()
+
+    relay(count, load, store)
     for half in range(copies):
-        pl.loop(0, count)(lambda entry: copy(entry, half).start())
-    for half in range(copies):
-        pl.loop(0, count)(lambda entry: copy(entry, half).wait())
-
-
-def collect_kernel(source, recv, out, sems):
+        pl.loop(0, count)(lambda at: save(at, half).wait())
+
+
+def collect_kernel(source, recv, out, buf, sems):
     count = out.shape[0]
 
-    def copy(slot):
-        return pltpu.make_async_copy(recv.at[source[slot]], out.at[slot], sems.at[slot])
-
-    pl.loop(0, count)(lambda slot: copy(slot).start())
-    pl.loop(0, count)(lambda slot: copy(slot).wait())
+    def load(at):
+        return pltpu.make_async_copy(recv.at[source[at]], buf.at[at], sems.at[0, at])
+
+    def save(at):
+        return pltpu.make_async_copy(buf.at[at], out.at[at], sems.at[1, at])
+
+    relay(count, load, lambda at: save(at).start())
+    pl.loop(0, count)(lambda at: save(at).wait())
 
 
 SMEM = pl.BlockSpec(memory_space=pltpu.SMEM)
@@ -66,7 +91,10 @@
         out_shape=jax.ShapeDtypeStruct((devices,) + held.shape[1:], held.dtype),
         in_specs=[SMEM, HBM],
         out_specs=HBM,
-        scratch_shapes=[pltpu.SemaphoreType.DMA((held.shape[0],))],
+        scratch_shapes=[
+            pltpu.VMEM(held.shape, held.dtype),
+            pltpu.SemaphoreType.DMA((2, held.shape[0])),
+        ],
         name="pack_right",
     )(dest, held)
 
@@ -79,7 +107,10 @@
         out_shape=jax.ShapeDtypeStruct((devices, rows // copies, cols), held.dtype),
         in_specs=[SMEM, HBM],
         out_specs=HBM,
-        scratch_shapes=[pltpu.SemaphoreType.DMA((copies, count))],
+        scratch_shapes=[
+            pltpu.VMEM(held.shape, held.dtype),
+            pltpu.SemaphoreType.DMA((1 + copies, count)),
+        ],
         name="pack_left",
     )(dest, held)
 
@@ -90,7 +121,10 @@
         out_shape=jax.ShapeDtypeStruct(source.shape + recv.shape[1:], recv.dtype),
         in_specs=[SMEM, HBM],
         out_specs=HBM,
-        scratch_shapes=[pltpu.SemaphoreType.DMA(source.shape)],
+        scratch_shapes=[
+            pltpu.VMEM(source.shape + recv.shape[1:], recv.dtype),
+            pltpu.SemaphoreType.DMA((2,) + source.shape),
+        ],
         name="collect",
     )(source, recv)
 
@@ -130,13 +164,13 @@
 
             def body(slot):
                 hi, lo = split(buf[at % 2, slot])
-                high[step, first + slot] = hi
-                low[step, first + slot] = lo
+                high[step * (slots + 1) + first + slot] = hi
+                low[step * (slots + 1) + first + slot] = lo
 
             pl.loop(0, group)(body)
         for step in range(steps):
-            high[step, slots] = jnp.zeros((edge, edge), jnp.bfloat16)
-            low[step, slots] = jnp.zeros((edge, edge), jnp.bfloat16)
+            high[step * (slots + 1) + slots] = jnp.zeros((edge, edge), jnp.bfloat16)
+            low[step * (slots + 1) + slots] = jnp.zeros((edge, edge), jnp.bfloat16)
 
     for kept in range(width):
         out[0, kept] = jnp.zeros((edge, edge), jnp.float32)
@@ -151,8 +185,8 @@
             both = jnp.concatenate([a_hi, a_lo], axis=1)
             for kept in range(width):
                 at = index[((row * steps + step) * WA + slot) * width + kept]
-                b_hi = high[step, at]
-                b_lo = low[step, at]
+                b_hi = high[at]
+                b_lo = low[at]
                 out[0, kept] += jnp.dot(
                     both, jnp.concatenate([b_hi, b_hi], axis=0), preferred_element_type=jnp.float32
                 ) + jnp.dot(a_hi, b_lo, preferred_element_type=jnp.float32)
@@ -173,8 +207,8 @@
             out_specs=pl.BlockSpec((1, width, edge, edge), lambda row, *_: (row, 0, 0, 0)),
             scratch_shapes=[
                 pltpu.VMEM((2, group, edge, edge), jnp.float32),
-                pltpu.VMEM((steps, slots + 1, edge, edge), jnp.bfloat16),
-                pltpu.VMEM((steps, slots + 1, edge, edge), jnp.bfloat16),
+                pltpu.VMEM((steps * (slots + 1), edge, edge), jnp.bfloat16),
+                pltpu.VMEM((steps * (slots + 1), edge, edge), jnp.bfloat16),
                 pltpu.SemaphoreType.DMA((2,)),
             ],
         ),
@@ -205,11 +239,15 @@
     inner, at_col = panel // grid_cols, panel % grid_cols
     dest_right = ((inner - at_col - 1) % grid_rows) * grid_cols + at_col
 
-    labels = lax.all_gather(jnp.concatenate([a_slot, a_col, b_slot, b_col]), ("row", "col"))
+    labels = jnp.concatenate([a_slot, a_col, b_slot, b_col])
+    labels = jnp.broadcast_to(labels[None, :], (devices,) + labels.shape)
+    labels = lax.all_to_all(labels, ("row", "col"), split_axis=0, concat_axis=0, tiled=True)
     parts = [hold_a, 2 * hold_a, 2 * hold_a + hold_b]
     all_a, all_acol, all_b, all_bcol = (part.reshape(-1) for part in jnp.split(labels, parts, axis=1))
 
-    k = (i + c + jnp.arange(STEPS, dtype=jnp.int32)) % grid_rows
+    side = 2 * (c % 2) - 1
+    turns = jnp.stack([jnp.int32(1), 1 - side, 1 + side])
+    k = (i + c + turns) % grid_rows
 
     def look_up(panels, slots, table, columns, hold):
         wanted = panels[:, None] * slots + jnp.arange(slots, dtype=jnp.int32)[None, :]
@@ -229,26 +267,28 @@
         & (c_col >= 0)[:, None, None, :, None]
     )
     index = slots_b - jnp.sum(jnp.where(hit, slots_b - u, 0), axis=4)
-    index = index.reshape(-1).astype(jnp.int32)
+    place = jnp.stack([jnp.int32(0), 1 + (1 - side) // 2, 1 + (1 + side) // 2])
+    index = (index + (place * (slots_b + 1))[None, :, None, None]).reshape(-1).astype(jnp.int32)
 
     send_left = pack_left(a_held, dest_left, devices)
     send_right = pack_right(b_held, dest_right, devices)
     recv_left = lax.all_to_all(send_left, ("row", "col"), split_axis=0, concat_axis=0, tiled=True)
     recv_right = lax.all_to_all(send_right, ("row", "col"), split_axis=0, concat_axis=0, tiled=True)
 
-    own = collect(recv_left, src_left[1])
+    own = collect(recv_left, src_left[0])
+    right = collect(recv_right, src_right[0])
     other = shifted(own, "col", grid_rows)
-    right = collect(recv_right, src_right[1])
+    cross = permuted(own, "col", lambda at: ((at - 1) ^ 1) + 1)
     halves = [
-        shifted(own, "col", 1),
-        shifted(other, "col", 1),
         own,
         other,
-        shifted(own, "col", -1),
-        shifted(other, "col", -1),
+        permuted(own, "col", lambda at: at ^ 1),
+        permuted(other, "col", lambda at: at ^ 1),
+        cross,
+        shifted(cross, "col", grid_rows),
     ]
-    rights = [shifted(right, "row", 1), right, shifted(right, "row", -1)]
-    homes = (c + jnp.arange(-1, 2, dtype=jnp.int32)) % grid_cols
+    rights = [right, shifted(right, "row", 1), shifted(right, "row", -1)]
+    homes = (c + jnp.stack([jnp.int32(0), -side, side])) % grid_cols
     order = (homes >= grid_rows).astype(jnp.int32)
     return products(index, order, halves, rights, rows, width)
 

time: 860 us -> 377 us (0.44)
  Pallas kernels: 435 us -> 63.8 us
  waiting for transfers between devices: 369 us -> 269 us
  between operations: 13.7 us -> 0.26 us
    unnamed x2 -> x0, waiting for transfers between devices: 215 us -> none
    pallas_call x2, Pallas kernels: 195 us -> 9.79 us  [collect(): pl.pallas_call(collect_kernel, out_shape=jax.ShapeDtypeStruct(source.shap...]
    all_to_all x1, waiting for transfers between devices: 0.01 us -> 132 us  [on_device(): lax.all_to_all(send_right, ('row', 'col'), split_axis=0, concat_axis=0, t...]
    pallas_call x1, Pallas kernels: 129 us -> 5.83 us  [pack_right(): pl.pallas_call(pack_right_kernel, out_shape=jax.ShapeDtypeStruct((devices...]
    ppermute x7 -> x4, waiting for transfers between devices: 155 us -> 91.8 us  [shifted(): return lax.ppermute(value, axis, pairs)]
    pallas_call x1, Pallas kernels: 65.9 us -> 3.92 us  [pack_left(): pl.pallas_call(functools.partial(pack_left_kernel, copies), out_shape=jax...]
    all_to_all x1, waiting for transfers between devices: 0.01 us -> 42.8 us  [on_device(): lax.all_to_all(send_left, ('row', 'col'), split_axis=0, concat_axis=0, ti...]
    all_to_all x0 -> x1, starting transfers between devices: none -> 10.3 us  [on_device(): lax.all_to_all(labels, ('row', 'col'), split_axis=0, concat_axis=0, tiled...]
  transfers between devices with their start and end apart: 10 -> 10, of which waited for: 3 -> 7; matrix products, arithmetic and copies ran while one was open for 1% -> 2% of each run, Pallas kernels for 38% -> 5%
where the time goes in v2:
time: 377 us; the launch traced here: 376 us
  waiting for transfers between devices  269 us (71%)
  Pallas kernels  63.8 us (17%)
  starting transfers between devices  33 us (9%)
  other arithmetic  6.2 us (2%)
    all_to_all x1, waiting for transfers between devices, on_device(): lax.all_to_all(send_right, ('row', 'col'), split_axis=0, concat_axis=0, t...  132 us
    ppermute x4, waiting for transfers between devices, shifted(): return lax.ppermute(value, axis, pairs)  91.8 us
    pallas_call x1, Pallas kernels, products(): pl.pallas_call(functools.partial(product_kernel, steps, width), grid_spec...  44.3 us
    all_to_all x1, waiting for transfers between devices, on_device(): lax.all_to_all(send_left, ('row', 'col'), split_axis=0, concat_axis=0, ti...  42.8 us
    all_to_all x1, starting transfers between devices, on_device(): lax.all_to_all(send_right, ('row', 'col'), split_axis=0, concat_axis=0, t...  10.7 us
    all_to_all x1, starting transfers between devices, on_device(): lax.all_to_all(labels, ('row', 'col'), split_axis=0, concat_axis=0, tiled...  10.3 us
    pallas_call x2, Pallas kernels, collect(): pl.pallas_call(collect_kernel, out_shape=jax.ShapeDtypeStruct(source.shap...  9.79 us
    all_to_all x1, starting transfers between devices, on_device(): lax.all_to_all(send_left, ('row', 'col'), split_axis=0, concat_axis=0, ti...  8.03 us
  transfers between devices with their start and end apart: 10, of which 7 were waited for; matrix products, arithmetic and copies ran while one was open for 2% of the time, Pallas kernels for 5%

profile of v2, /device:TPU:26, one launch (start us, length us, event | category | flops | bytes accessed | tf_op | source)
XLA Modules:
  0.0 375.6 jit_solution(14828242380187908604)
XLA Ops:
  0.0 0.8 pad_add_fusion
  0.8 0.7 broadcast_in_dim.24
  1.5 10.3 %all-to-all-start = ((s32[128,1,192]{2,1,0:T(1,128)}), s32[128,1,192]{2,1,0:T(1,128)S(1)}, u32[]{:S(2)}, u32[]{:S(2)}) async-start(s32[128,1,192]{2,1,0:T(1,128)} %broadcast_in_dim.24), calls=%async_computation | async-start | bytes 262144 | tf_op jit(solution)/shard_map/all_to_all | solution.py:244
  11.8 0.7 fusion.20
  12.4 0.7 broadcast_add_fusion.dest
  13.1 3.9 %pack_left.1 = f32[128,64,128]{2,1,0:T(8,128)} custom-call(s32[2,32]{1,0:T(2,128)} %broadcast_add_fusion.dest, f32[32,128,128]{2,1,0:T(8,128)} %held.2), custom_call_target="tpu_custom_call" | custom-call | tf_op jit(solution)/shard_map/pack_left/pallas_call | solution.py:105
  17.0 0.0 copy-start.2
  17.0 2.2 all-to-all-done
  19.2 8.0 %all-to-all-start.1 = ((f32[128,64,128]{2,1,0:T(8,128)}), f32[128,64,128]{2,1,0:T(8,128)}, u32[]{:S(2)}, u32[]{:S(2)}) async-start(f32[128,64,128]{2,1,0:T(8,128)} %pack_left.1), calls=%async_computation.1 | async-start | bytes 8388608 | tf_op jit(solution)/shard_map/all_to_all | solution.py:275
  27.3 0.0 copy-done.2
  27.3 0.6 fusion.24.dest
  27.9 5.8 %pack_right.1 = f32[128,128,128]{2,1,0:T(8,128)} custom-call(s32[64]{0:T(128)} %fusion.24.dest, f32[64,128,128]{2,1,0:T(8,128)} %held.3), custom_call_target="tpu_custom_call" | custom-call | tf_op jit(solution)/shard_map/pack_right/pallas_call | solution.py:89
  33.7 42.8 %all-to-all-done.1.recv = f32[128,64,128]{2,1,0:T(8,128)} async-done(((f32[128,64,128]{2,1,0:T(8,128)}), f32[128,64,128]{2,1,0:T(8,128)}, u32[]{:S(2)}, u32[]{:S(2)}) %all-to-all-start.1) | async-done | bytes 4194336 | tf_op jit(solution)/shard_map/all_to_all | solution.py:275
  76.6 10.7 %all-to-all-start.2 = ((f32[128,128,128]{2,1,0:T(8,128)}), f32[128,128,128]{2,1,0:T(8,128)}, u32[]{:S(2)}, u32[]{:S(2)}) async-start(f32[128,128,128]{2,1,0:T(8,128)} %pack_right.1), calls=%async_computation.2 | async-start | bytes 16777216 | tf_op jit(solution)/shard_map/all_to_all | solution.py:276
  87.3 0.1 add_multiply_fusion.1
  87.4 0.1 iota_add_fusion
  87.5 0.1 iota_add_fusion.1
  87.5 0.1 copy.26
  87.7 0.1 copy.30
  87.8 0.1 eq.87
  87.8 0.1 copy.27
  87.9 0.1 eq.80
  88.0 0.1 copy.28
  88.1 0.1 reshape.192
  88.2 0.1 copy.31
  88.3 0.1 reshape.193
  88.4 0.5 select_reduce_fusion.1
  88.9 0.6 slice_bitcast_fusion.1.source
  89.5 0.9 select_reduce_fusion
  90.4 0.6 slice_bitcast_fusion.source
  91.0 4.0 %collect.2.refs_0_ = f32[64,64,128]{2,1,0:T(8,128)} custom-call(s32[64]{0:T(128)} %slice_bitcast_fusion.1.source, f32[128,64,128]{2,1,0:T(8,128)} %all-to-all-done.1.recv), custom_call_target="tpu_custom_call" | custom-call | tf_op jit(solution)/shard_map/collect/pallas_call | solution.py:119
  95.0 0.0 copy-start
  95.0 0.0 copy-start.1
  95.0 0.4 collective-permute-start.3
  95.4 1.4 collective-permute-start
  96.8 132.3 %all-to-all-done.2.recv = f32[128,128,128]{2,1,0:T(8,128)} async-done(((f32[128,128,128]{2,1,0:T(8,128)}), f32[128,128,128]{2,1,0:T(8,128)}, u32[]{:S(2)}, u32[]{:S(2)}) %all-to-all-start.2) | async-done | bytes 8388640 | tf_op jit(solution)/shard_map/all_to_all | solution.py:276
  229.1 5.8 %collect.3.refs_6_ = f32[64,128,128]{2,1,0:T(8,128)} custom-call(s32[64]{0:T(128)} %slice_bitcast_fusion.source, f32[128,128,128]{2,1,0:T(8,128)} %all-to-all-done.2.recv), custom_call_target="tpu_custom_call" | custom-call | tf_op jit(solution)/shard_map/collect/pallas_call | solution.py:119
  234.9 0.1 collective-permute-start.6
  235.0 2.0 collective-permute-start.5
  237.0 0.0 copy-done
  237.0 0.0 collective-permute-start.1
  237.0 0.0 collective-permute-done.3.refs_4_
  237.0 0.1 collective-permute-start.4
  237.1 22.8 %collective-permute-done.refs_1_ = f32[64,64,128]{2,1,0:T(8,128)} collective-permute-done((f32[64,64,128]{2,1,0:T(8,128)}, f32[64,64,128]{2,1,0:T(8,128)}, u32[]{:S(2)}, u32[]{:S(2)}) %collective-permute-start) | collective-permute-done | bytes 2097184 | tf_op jit(solution)/shard_map/ppermute | solution.py:20
  259.9 0.0 collective-permute-start.2
  260.0 0.1 compare_convert_fusion.order
  260.0 0.1 fusion.29
  260.1 0.0 copy-done.1
  260.1 0.1 reduce_sum.30
  260.2 0.1 copy.29
  260.3 0.1 broadcast_compare_fusion.1
  260.4 0.1 broadcast_compare_fusion
  260.5 1.4 select_reduce_fusion.2
  261.9 0.1 subtract_add_fusion
  262.0 0.2 copy.32
  262.1 0.2 add.235.index
  262.3 0.0 collective-permute-done.1.refs_2_
  262.3 42.1 %collective-permute-done.4.refs_5_ = f32[64,64,128]{2,1,0:T(8,128)} collective-permute-done((f32[64,64,128]{2,1,0:T(8,128)}, f32[64,64,128]{2,1,0:T(8,128)}, u32[]{:S(2)}, u32[]{:S(2)}) %collective-permute-start.4) | collective-permute-done | bytes 2097184 | tf_op jit(solution)/shard_map/ppermute | solution.py:20
  304.4 0.0 collective-permute-done.2.refs_3_
  304.4 23.2 %collective-permute-done.6.refs_8_ = f32[64,128,128]{2,1,0:T(8,128)} collective-permute-done((f32[64,128,128]{2,1,0:T(8,128)}, f32[64,128,128]{2,1,0:T(8,128)}, u32[]{:S(2)}, u32[]{:S(2)}) %collective-permute-start.6) | collective-permute-done | bytes 4194336 | tf_op jit(solution)/shard_map/ppermute | solution.py:20
  327.6 3.7 collective-permute-done.5.refs_7_
  331.3 44.3 %products.1 = f32[16,6,128,128]{3,2,1,0:T(8,128)} custom-call(s32[1152]{0:T(1024)S(1)} %add.235.index, s32[3]{0:T(128)S(1)} %compare_convert_fusion.order, f32[64,64,128]{2,1,0:T(8,128)S(1)} %copy-done, f32[64,64,128]{2,1,0:T(8,128)} %collective-permute-done.refs_1_, f32[64,64,128]{2,1,0:T(8,128)} %collective-permute-done.1.refs_2_, ...), custom_call_target="tpu_custom_call" | custom-call | tf_op jit(solution)/shard_map/products/pallas_call | solution.py:201
  (12 shorter events, 0.1 us)
Async XLA Ops:
  1.5 17.8 %all-to-all-start = ((s32[128,1,192]{2,1,0:T(1,128)}), s32[128,1,192]{2,1,0:T(1,128)S(1)}, u32[]{:S(2)}, u32[]{:S(2)}) async-start(s32[128,1,192]{2,1,0:T(1,128)} %broadcast_in_dim.24), calls=%async_computation | async-start | bytes 262144 | tf_op jit(solution)/shard_map/all_to_all | solution.py:244
  17.0 10.3 %copy-start.2 = (s32[64]{0:T(128)S(1)}, s32[64]{0:T(128)}, u32[]{:S(2)}) copy-start(s32[64]{0:T(128)} %param.11) | copy-start | bytes 772
  19.2 57.3 %all-to-all-start.1 = ((f32[128,64,128]{2,1,0:T(8,128)}), f32[128,64,128]{2,1,0:T(8,128)}, u32[]{:S(2)}, u32[]{:S(2)}) async-start(f32[128,64,128]{2,1,0:T(8,128)} %pack_left.1), calls=%async_computation.1 | async-start | bytes 8388608 | tf_op jit(solution)/shard_map/all_to_all | solution.py:275
  76.6 152.5 %all-to-all-start.2 = ((f32[128,128,128]{2,1,0:T(8,128)}), f32[128,128,128]{2,1,0:T(8,128)}, u32[]{:S(2)}, u32[]{:S(2)}) async-start(f32[128,128,128]{2,1,0:T(8,128)} %pack_right.1), calls=%async_computation.2 | async-start | bytes 16777216 | tf_op jit(solution)/shard_map/all_to_all | solution.py:276
  95.0 142.0 %copy-start = (f32[64,64,128]{2,1,0:T(8,128)S(1)}, f32[64,64,128]{2,1,0:T(8,128)}, u32[]{:S(2)}) copy-start(f32[64,64,128]{2,1,0:T(8,128)} %collect.2.refs_0_) | copy-start | bytes 6291460
  95.0 165.1 %copy-start.1 = (s32[16,6]{0,1:T(8,128)S(1)}, s32[16,6]{0,1:T(8,128)}, u32[]{:S(2)}) copy-start(s32[16,6]{0,1:T(8,128)} %param.13) | copy-start | bytes 1156
  95.0 142.0 %collective-permute-start.3 = (f32[64,64,128]{2,1,0:T(8,128)}, f32[64,64,128]{2,1,0:T(8,128)}, u32[]{:S(2)}, u32[]{:S(2)}) collective-permute-start(f32[64,64,128]{2,1,0:T(8,128)} %collect.2.refs_0_), channel_id=1, source_target_pairs={{0,15},{1,2},{2,1},{3,4},{4,3},{5,6},{6,5},{7,8},{8,7},{9,10},{10,... | collective-permute-start | bytes 6291464 | tf_op jit(solution)/shard_map/ppermute | solution.py:25
  95.4 164.5 %collective-permute-start = (f32[64,64,128]{2,1,0:T(8,128)}, f32[64,64,128]{2,1,0:T(8,128)}, u32[]{:S(2)}, u32[]{:S(2)}) collective-permute-start(f32[64,64,128]{2,1,0:T(8,128)} %collect.2.refs_0_), channel_id=1, source_target_pairs={{0,8},{1,9},{2,10},{3,11},{4,12},{5,13},{6,14},{7,15},{8,0},{9,1},... | collective-permute-start | bytes 6291464 | tf_op jit(solution)/shard_map/ppermute | solution.py:20
  234.9 92.7 %collective-permute-start.6 = (f32[64,128,128]{2,1,0:T(8,128)}, f32[64,128,128]{2,1,0:T(8,128)}, u32[]{:S(2)}, u32[]{:S(2)}) collective-permute-start(f32[64,128,128]{2,1,0:T(8,128)} %collect.3.refs_6_), channel_id=1, source_target_pairs={{0,112},{16,0},{32,16},{48,32},{64,48},{80,64},{96,80},{112,96},{1... | collective-permute-start | bytes 12582920 | tf_op jit(solution)/shard_map/ppermute | solution.py:20
  235.0 96.3 %collective-permute-start.5 = (f32[64,128,128]{2,1,0:T(8,128)}, f32[64,128,128]{2,1,0:T(8,128)}, u32[]{:S(2)}, u32[]{:S(2)}) collective-permute-start(f32[64,128,128]{2,1,0:T(8,128)} %collect.3.refs_6_), channel_id=1, source_target_pairs={{0,16},{16,32},{32,48},{48,64},{64,80},{80,96},{96,112},{112,0},{1... | collective-permute-start | bytes 12582920 | tf_op jit(solution)/shard_map/ppermute | solution.py:20
  237.0 25.3 %collective-permute-start.1 = (f32[64,64,128]{2,1,0:T(8,128)S(1)}, f32[64,64,128]{2,1,0:T(8,128)}, u32[]{:S(2)}, u32[]{:S(2)}) collective-permute-start(f32[64,64,128]{2,1,0:T(8,128)S(1)} %copy-done), channel_id=1, source_target_pairs={{0,1},{1,0},{2,3},{3,2},{4,5},{5,4},{6,7},{7,6},{8,9},{9,8},{10,11... | collective-permute-start | bytes 6291464 | tf_op jit(solution)/shard_map/ppermute | solution.py:25
  237.0 67.4 %collective-permute-start.4 = (f32[64,64,128]{2,1,0:T(8,128)}, f32[64,64,128]{2,1,0:T(8,128)}, u32[]{:S(2)}, u32[]{:S(2)}) collective-permute-start(f32[64,64,128]{2,1,0:T(8,128)} %collective-permute-done.3.refs_4_), channel_id=1, source_target_pairs={{0,8},{1,9},{2,10},{3,11},{4,12},{5,13},{6,14},{7,15},{8,0},{9,1},... | collective-permute-start | bytes 6291464 | tf_op jit(solution)/shard_map/ppermute | solution.py:20
  259.9 44.5 %collective-permute-start.2 = (f32[64,64,128]{2,1,0:T(8,128)}, f32[64,64,128]{2,1,0:T(8,128)}, u32[]{:S(2)}, u32[]{:S(2)}) collective-permute-start(f32[64,64,128]{2,1,0:T(8,128)} %collective-permute-done.refs_1_), channel_id=1, source_target_pairs={{0,1},{1,0},{2,3},{3,2},{4,5},{5,4},{6,7},{7,6},{8,9},{9,8},{10,11... | collective-permute-start | bytes 6291464 | tf_op jit(solution)/shard_map/ppermute | solution.py:25

commit v3 on v2

v3 whole, which is shorter than its diff:
```python
import functools

import jax
import jax.numpy as jnp
from jax import lax
from jax.experimental import pallas as pl
from jax.experimental.pallas import tpu as pltpu
from jax.sharding import PartitionSpec as P

KPB = 16
WA = 4
WB = 4
STEPS = 3
HBM = pl.BlockSpec(memory_space=pl.ANY)


def shifted(value, axis, steps):
    count = lax.axis_size(axis)
    pairs = [(source, (source + steps) % count) for source in range(count)]
    return lax.ppermute(value, axis, pairs)


def permuted(value, axis, target):
    count = lax.axis_size(axis)
    return lax.ppermute(value, axis, [(at, target(at) % count) for at in range(count)])


def relay(count, load, store):
    pl.loop(0, count)(lambda at: load(at).start())

    def body(at):
        load(at).wait()
        store(at)

    pl.loop(0, count)(body)


def pack_right_kernel(dest, held, out, buf, sems):
    count = held.shape[0]

    def load(at):
        return pltpu.make_async_copy(held.at[at], buf.at[at], sems.at[0, at])

    def save(at):
        return pltpu.make_async_copy(buf.at[at], out.at[dest[at]], sems.at[1, at])

    relay(count, load, lambda at: save(at).start())
    pl.loop(0, count)(lambda at: save(at).wait())


def pack_left_kernel(copies, part, dest, held, labels, out, buf, sems, mark_sems):
    count = held.shape[0]
    devices = out.shape[0]

    def mark(at):
        return pltpu.make_async_copy(labels, out.at[at, pl.ds(part, 8)], mark_sems.at[at])

    def load(at):
        return pltpu.make_async_copy(held.at[at], buf.at[at], sems.at[0, at])

    def save(at, half):
        return pltpu.make_async_copy(
            buf.at[at, pl.ds(half * part, part)],
            out.at[dest[half, at], pl.ds(0, part)],
            sems.at[1 + half, at],
        )

    def store(at):
        for half in range(copies):
            save(at, half).start()

    relay(count, load, store)
    pl.loop(0, devices)(lambda at: mark(at).start())
    for half in range(copies):
        pl.loop(0, count)(lambda at: save(at, half).wait())
    pl.loop(0, devices)(lambda at: mark(at).wait())


def collect_kernel(source, recv, *refs):
    buf, sems = refs[-2:]
    count, rows, _ = buf.shape
    outs = refs[:-2]
    chunk = count // len(outs)

    def load(at):
        return pltpu.make_async_copy(
            recv.at[source[at], pl.ds(0, rows)], buf.at[at], sems.at[at]
        )

    pl.loop(0, count)(lambda at: load(at).start())
    saves = [
        pltpu.make_async_copy(buf.at[pl.ds(part * chunk, chunk)], out, sems.at[count + part])
        for part, out in enumerate(outs)
    ]
    for part, save in enumerate(saves):
        pl.loop(part * chunk, (part + 1) * chunk)(lambda at: load(at).wait())
        save.start()
    for save in saves:
        save.wait()


SMEM = pl.BlockSpec(memory_space=pltpu.SMEM)


def pack_right(held, dest, devices):
    return pl.pallas_call(
        pack_right_kernel,
        out_shape=jax.ShapeDtypeStruct((devices,) + held.shape[1:], held.dtype),
        in_specs=[SMEM, HBM],
        out_specs=HBM,
        scratch_shapes=[
            pltpu.VMEM(held.shape, held.dtype),
            pltpu.SemaphoreType.DMA((2, held.shape[0])),
        ],
        name="pack_right",
    )(dest, held)


def pack_left(held, dest, labels, devices):
    copies = dest.shape[0]
    count, rows, cols = held.shape
    part = rows // copies
    return pl.pallas_call(
        functools.partial(pack_left_kernel, copies, part),
        out_shape=jax.ShapeDtypeStruct((devices, part + 8, cols), held.dtype),
        in_specs=[SMEM, HBM, pl.BlockSpec(memory_space=pltpu.VMEM)],
        out_specs=HBM,
        scratch_shapes=[
            pltpu.VMEM(held.shape, held.dtype),
            pltpu.SemaphoreType.DMA((1 + copies, count)),
            pltpu.SemaphoreType.DMA((devices,)),
        ],
        name="pack_left",
    )(dest, held, labels)


def collect(recv, source, rows, chunks):
    count, cols = source.shape[0], recv.shape[2]
    part = jax.ShapeDtypeStruct((count // chunks, rows, cols), recv.dtype)
    return pl.pallas_call(
        collect_kernel,
        out_shape=[part] * chunks,
        in_specs=[SMEM, HBM],
        out_specs=[HBM] * chunks,
        scratch_shapes=[
            pltpu.VMEM((count, rows, cols), recv.dtype),
            pltpu.SemaphoreType.DMA((count + chunks,)),
        ],
        name="collect",
    )(source, recv)


def split(value):
    high = value.astype(jnp.bfloat16)
    low = (value - high.astype(jnp.float32)).astype(jnp.bfloat16)
    return high, low


def product_kernel(pieces, parts, first, unroll, counts, items, order, *refs):
    lefts = refs[: 2 * pieces]
    rights = refs[2 * pieces : 2 * pieces + parts]
    refs = refs[2 * pieces + parts :]
    if not first:
        before, refs = refs[0], refs[1:]
    out, left_buf, right_buf, total, load_sems, out_sem = refs
    outs, edge, _ = out.shape
    slots_a = lefts[0].shape[0]
    slots_b = rights[0].shape[0]

    loads = [
        pltpu.make_async_copy(source, left_buf.at[at], load_sems.at[at])
        for at, source in enumerate(lefts)
    ] + [
        pltpu.make_async_copy(
            source, right_buf.at[pl.ds(at * slots_b, slots_b)], load_sems.at[2 * pieces + at]
        )
        for at, source in enumerate(rights)
    ]
    if not first:
        restore = pltpu.make_async_copy(before, total.at[pl.ds(0, outs)], out_sem)
        restore.start()
    for load in loads:
        load.start()
    if first:

        def clear(at):
            total[at] = jnp.zeros((edge, edge), jnp.float32)

        pl.loop(0, outs)(clear)
    else:
        restore.wait()
    for load in loads:
        load.wait()

    def step(at):
        codes = [items[at * unroll + lane] for lane in range(unroll)]
        sums = []
        for code in codes:
            slot_a = code // 16384
            slot_b = (code // 128) % 128
            piece = slot_a // slots_a
            swap = order[piece]
            slot_a = slot_a % slots_a
            left = jnp.concatenate(
                [
                    left_buf[2 * piece + swap, slot_a],
                    left_buf[2 * piece + 1 - swap, slot_a],
                ],
                axis=0,
            )
            a_hi, a_lo = split(left)
            b_hi, b_lo = split(right_buf[slot_b])
            sums.append(
                jnp.dot(
                    jnp.concatenate([a_hi, a_lo], axis=1),
                    jnp.concatenate([b_hi, b_hi], axis=0),
                    preferred_element_type=jnp.float32,
                )
                + jnp.dot(a_hi, b_lo, preferred_element_type=jnp.float32)
            )
        for code, value in zip(codes, sums):
            total[code % 128] += value

    pl.loop(0, counts[0])(step)
    save = pltpu.make_async_copy(total.at[pl.ds(0, outs)], out, out_sem)
    save.start()
    save.wait()


UNROLL = 8
CHUNKS = 2


def products(counts, items, order, halves, rights, before, outs):
    pieces, parts = len(halves) // 2, len(rights)
    slots_b, edge, _ = rights[0].shape
    slots_a, part, _ = halves[0].shape
    first = before is None
    extra = [] if first else [before]
    return pl.pallas_call(
        functools.partial(product_kernel, pieces, parts, first, UNROLL),
        out_shape=jax.ShapeDtypeStruct((outs, edge, edge), jnp.float32),
        in_specs=[SMEM] * 3 + [HBM] * (2 * pieces + parts + len(extra)),
        out_specs=HBM,
        scratch_shapes=[
            pltpu.VMEM((2 * pieces, slots_a, part, edge), jnp.float32),
            pltpu.VMEM((parts * slots_b, edge, edge), jnp.float32),
            pltpu.VMEM((outs + 1, edge, edge), jnp.float32),
            pltpu.SemaphoreType.DMA((2 * pieces + parts,)),
            pltpu.SemaphoreType.DMA,
        ],
        compiler_params=pltpu.CompilerParams(vmem_limit_bytes=40 * 1024 * 1024),
        cost_estimate=pl.CostEstimate(
            flops=pieces * 600_000_000, bytes_accessed=pieces * 8_000_000, transcendentals=0
        ),
        name="products",
    )(counts, items, order, *halves, *rights, *extra)


def work_list(lefts, rights, places, kept, first_row):
    rows, width = kept.shape
    pieces, inner, _ = rights.shape
    outs = rows * width
    slots = rows * WA
    rel = lefts - first_row
    here = rel[:, :, None] == jnp.arange(inner, dtype=jnp.int32)
    chosen = (
        jnp.sum(jnp.where(here[:, :, :, None], rights[:, None, :, :] + 1, 0), axis=2) - 1
    )
    at_row = jnp.repeat(kept, WA, axis=0)
    match = (chosen[:, :, :, None] == at_row[None, :, None, :]) & (chosen >= 0)[:, :, :, None]
    target = jnp.sum(jnp.where(match, jnp.arange(width, dtype=jnp.int32) + 1, 0), axis=3) - 1
    live = target >= 0
    slot = jnp.arange(slots, dtype=jnp.int32)[None, :, None]
    slot_a = slot + slots * jnp.arange(pieces, dtype=jnp.int32)[:, None, None]
    slot_b = (places[:, None, None] * inner + rel[:, :, None]) * WB + jnp.arange(WB, dtype=jnp.int32)
    code = slot_a * 16384 + slot_b * 128 + slot // WA * width + target
    live, code = live.reshape(-1), code.reshape(-1)
    spot = jnp.cumsum(live.astype(jnp.int32)) - 1
    place = jnp.arange(live.shape[0], dtype=jnp.int32)
    here = live[None, :] & (spot[None, :] == place[:, None])
    packed = jnp.sum(jnp.where(here, code[None, :] - outs, 0), axis=1) + outs
    count = (jnp.sum(live.astype(jnp.int32)) + UNROLL - 1) // UNROLL
    return count[None], packed


def on_device(a_held, a_slot, a_col, b_held, b_slot, b_col, c_col):
    grid_rows = lax.axis_size("row")
    grid_cols = lax.axis_size("col")
    devices = grid_rows * grid_cols
    copies = grid_cols // grid_rows
    i = lax.axis_index("row")
    c = lax.axis_index("col")
    rows, width = c_col.shape
    hold_a, hold_b = a_slot.shape[0], b_slot.shape[0]
    slots_a, slots_b = rows * WA, KPB * WB

    panel = a_slot // slots_a
    at_row, inner = panel // grid_rows, panel % grid_rows
    dest = at_row * grid_cols + (inner - at_row - 1) % grid_rows
    dest_left = dest[None, :] + grid_rows * jnp.arange(copies, dtype=jnp.int32)[:, None]
    panel = b_slot // slots_b
    inner, at_col = panel // grid_cols, panel % grid_cols
    dest_right = ((inner - at_col - 1) % grid_rows) * grid_cols + at_col

    edge = a_held.shape[1]
    labels = jnp.concatenate([a_slot, a_col, b_slot, b_col]).astype(jnp.float32)
    tile = jnp.pad(labels, (0, 8 * edge - labels.shape[0])).reshape(8, edge)
    send_left = pack_left(a_held, dest_left, tile, devices)
    send_right = pack_right(b_held, dest_right, devices)
    recv_left = lax.all_to_all(send_left, ("row", "col"), split_axis=0, concat_axis=0, tiled=True)
    recv_right = lax.all_to_all(send_right, ("row", "col"), split_axis=0, concat_axis=0, tiled=True)

    labels = recv_left[:, edge // copies :, :].reshape(devices, -1)[:, : labels.shape[0]]
    labels = labels.astype(jnp.int32)
    parts = [hold_a, 2 * hold_a, 2 * hold_a + hold_b]
    all_a, all_acol, all_b, all_bcol = (part.reshape(-1) for part in jnp.split(labels, parts, axis=1))

    side = 2 * (c % 2) - 1
    turns = jnp.stack([jnp.int32(1), 1 - side, 1 + side])
    k = (i + c + turns) % grid_rows

    def look_up(panels, slots, table, columns, hold):
        wanted = panels[:, None] * slots + jnp.arange(slots, dtype=jnp.int32)[None, :]
        holder = jnp.arange(table.shape[0], dtype=jnp.int32) // hold
        code = holder * 32 + columns + 1
        found = jnp.sum(jnp.where(table[None, None, :] == wanted[:, :, None], code, 0), axis=2)
        return found // 32, found % 32 - 1

    src_left, col_left = look_up(i * grid_rows + k, slots_a, all_a, all_acol, hold_a)
    src_right, col_right = look_up(k * grid_cols + c, slots_b, all_b, all_bcol, hold_b)

    (own,) = collect(recv_left, src_left[0], edge // copies, 1)
    right = collect(recv_right, src_right[0], edge, CHUNKS)
    other = shifted(own, "col", grid_rows)
    cross = permuted(own, "col", lambda at: ((at - 1) ^ 1) + 1)
    mate_first = permuted(own, "col", lambda at: at ^ 1)
    mate_second = permuted(other, "col", lambda at: at ^ 1)
    cross_second = shifted(cross, "col", grid_rows)
    homes = (c + jnp.stack([jnp.int32(0), -side, side])) % grid_cols
    order = (homes >= grid_rows).astype(jnp.int32)

    outs = rows * width
    tables = col_right.reshape(STEPS, KPB, WB)
    count, items = work_list(col_left[:1], tables[:1], jnp.zeros((1,), jnp.int32), c_col, 0)
    total = products(count, items, order[:1], [own, other], right, None, outs)
    places = jnp.stack([(1 - side) // 2, (1 + side) // 2])
    lefts = [mate_first, mate_second, cross, cross_second]
    chunk = slots_b // CHUNKS
    for at in range(CHUNKS):
        shifts = [shifted(right[at], "row", 1), shifted(right[at], "row", -1)]
        first, last = at * chunk // WB, (at + 1) * chunk // WB
        count, items = work_list(col_left[1:], tables[1:, first:last], places, c_col, first)
        total = products(count, items, order[1:], lefts, shifts, total, outs)
    return total.reshape(rows, width, edge, edge)


def solution(mesh):
    return jax.shard_map(
        on_device,
        mesh=mesh,
        in_specs=(
            P(("row", "col"), None, None),
            P(("row", "col")),
            P(("row", "col")),
            P(("row", "col"), None, None),
            P(("row", "col")),
            P(("row", "col")),
            P("row", "col"),
        ),
        out_specs=P("row", "col", None, None),
        check_vma=False,
    )
```

time: 377 us -> 385 us (1.021)
  Pallas kernels: 63.8 us -> 50.2 us
  local copies, waits for them, and re-layouts: 3.18 us -> 11.8 us
  starting transfers between devices: 33 us -> 41.4 us
    all_to_all x1, waiting for transfers between devices: 132 us -> 0.01 us  [on_device(): lax.all_to_all(send_right, ('row', 'col'), split_axis=0, concat_axis=0, t...]
    ppermute x4 -> x6, waiting for transfers between devices: 91.8 us -> 219 us  [shifted(): return lax.ppermute(value, axis, pairs)]
    pallas_call x4 -> x6, Pallas kernels: 58 us -> 44.4 us  [the longest x3 29 us: products(): pl.pallas_call(functools.partial(product_kernel, pieces, parts, first, UN...]
    ppermute x4 -> x6, starting transfers between devices: 3.58 us -> 16.9 us  [shifted(): return lax.ppermute(value, axis, pairs)]
    all_to_all x1 -> x0, starting transfers between devices: 10.3 us -> none  [on_device(): lax.all_to_all(labels, ('row', 'col'), split_axis=0, concat_axis=0, tiled...]
    unnamed x6 -> x11, local copies, waits for them, and re-layouts: 0.02 us -> 4.88 us
    all_to_all x1, waiting for transfers between devices: 42.8 us -> 47.5 us  [on_device(): lax.all_to_all(send_left, ('row', 'col'), split_axis=0, concat_axis=0, ti...]
  transfers between devices with their start and end apart: 10 -> 11, of which waited for: 7 -> 5; matrix products, arithmetic and copies ran while one was open for 2% -> 4% of each run, Pallas kernels for 5% -> 9%
where the time goes in v3:
time: 385 us; the launch traced here: 382 us
  waiting for transfers between devices  267 us (69%)
  Pallas kernels  50.2 us (13%)
  starting transfers between devices  41.4 us (11%)
  local copies, waits for them, and re-layouts  11.8 us (3%)
  other arithmetic  9.23 us (2%)
    ppermute x6, waiting for transfers between devices, shifted(): return lax.ppermute(value, axis, pairs)  219 us
    all_to_all x1, waiting for transfers between devices, on_device(): lax.all_to_all(send_left, ('row', 'col'), split_axis=0, concat_axis=0, ti...  47.5 us
    pallas_call x3, Pallas kernels, products(): pl.pallas_call(functools.partial(product_kernel, pieces, parts, first, UN...  29 us
    ppermute x6, starting transfers between devices, shifted(): return lax.ppermute(value, axis, pairs)  16.9 us
    all_to_all x1, starting transfers between devices, on_device(): lax.all_to_all(send_right, ('row', 'col'), split_axis=0, concat_axis=0, t...  11.7 us
    all_to_all x1, starting transfers between devices, on_device(): lax.all_to_all(send_left, ('row', 'col'), split_axis=0, concat_axis=0, ti...  10.7 us
    pallas_call x2, Pallas kernels, collect(): pl.pallas_call(collect_kernel, out_shape=[part] * chunks, in_specs=[SMEM,...  8.97 us
  transfers between devices with their start and end apart: 11, of which 5 were waited for; matrix products, arithmetic and copies ran while one was open for 4% of the time, Pallas kernels for 9%

profile of v3, /device:TPU:26, one launch (start us, length us, event | category | flops | bytes accessed | tf_op | source)
XLA Modules:
  0.0 381.8 jit_solution(4596903642528112419)
XLA Ops:
  0.0 0.7 fusion.22
  0.7 0.8 add_convert_fusion
  1.5 0.6 pad_bitcast_fusion.labels
  2.1 0.6 broadcast_add_fusion.8.dest
  2.7 6.4 %pack_left.1 = f32[128,72,128]{2,1,0:T(8,128)} custom-call(s32[2,32]{1,0:T(2,128)} %broadcast_add_fusion.8.dest, f32[32,128,128]{2,1,0:T(8,128)} %held.2, f32[8,128]{1,0:T(8,128)} %pad_bitcast_fusion.labels), custom_call_target="tpu_custom_call" | custom-call | tf_op jit(solution)/shard_map/pack_left/pallas_call | solution.py:123
  9.1 10.7 %all-to-all-start = ((f32[128,72,128]{2,1,0:T(8,128)}), f32[128,72,128]{2,1,0:T(8,128)}, u32[]{:S(2)}, u32[]{:S(2)}) async-start(f32[128,72,128]{2,1,0:T(8,128)} %pack_left.1), calls=%async_computation | async-start | bytes 9437184 | tf_op jit(solution)/shard_map/all_to_all | solution.py:311
  20.1 0.1 add.660
  20.3 0.1 add.652
  20.4 0.1 add.656
  20.7 0.5 fusion.25.dest
  21.3 5.8 %pack_right.1 = f32[128,128,128]{2,1,0:T(8,128)} custom-call(s32[64]{0:T(128)} %fusion.25.dest, f32[64,128,128]{2,1,0:T(8,128)} %held.3), custom_call_target="tpu_custom_call" | custom-call | tf_op jit(solution)/shard_map/pack_right/pallas_call | solution.py:106
  27.5 47.5 %all-to-all-done.recv = f32[128,72,128]{2,1,0:T(8,128)} async-done(((f32[128,72,128]{2,1,0:T(8,128)}), f32[128,72,128]{2,1,0:T(8,128)}, u32[]{:S(2)}, u32[]{:S(2)}) %all-to-all-start) | async-done | bytes 4718624 | tf_op jit(solution)/shard_map/all_to_all | solution.py:311
  75.0 11.7 %all-to-all-start.1 = ((f32[128,128,128]{2,1,0:T(8,128)}), f32[128,128,128]{2,1,0:T(8,128)}, u32[]{:S(2)}, u32[]{:S(2)}) async-start(f32[128,128,128]{2,1,0:T(8,128)} %pack_right.1), calls=%async_computation.1 | async-start | bytes 16777216 | tf_op jit(solution)/shard_map/all_to_all | solution.py:312
  86.8 1.1 slice.74
  88.5 0.9 select_reduce_fusion
  89.6 0.5 select_reduce_fusion.1
  90.4 0.6 broadcast_add_fusion.2
  91.7 0.6 slice_bitcast_fusion.2.source
  92.3 4.1 %collect.2.refs_0_ = f32[64,64,128]{2,1,0:T(8,128)} custom-call(s32[64]{0:T(128)} %slice_bitcast_fusion.2.source, f32[128,72,128]{2,1,0:T(8,128)} %all-to-all-done.recv), custom_call_target="tpu_custom_call" | custom-call | tf_op jit(solution)/shard_map/collect/pallas_call | solution.py:140
  96.4 1.5 collective-permute-start.1
  97.9 2.2 collective-permute-start
  100.6 0.1 select_reduce_fusion.8
  100.7 158.1 %collective-permute-done.1.refs_1_ = f32[64,64,128]{2,1,0:T(8,128)} collective-permute-done((f32[64,64,128]{2,1,0:T(8,128)}, f32[64,64,128]{2,1,0:T(8,128)}, u32[]{:S(2)}, u32[]{:S(2)}) %collective-permute-start.1) | collective-permute-done | bytes 2097184 | tf_op jit(solution)/shard_map/ppermute | solution.py:20
  258.9 0.7 convert_reduce_fusion
  260.2 0.1 copy.26
  260.3 0.1 copy.22
  260.5 0.7 convert_reduce_fusion.1
  261.9 0.1 reshape.612
  262.0 0.3 reduce-window.37
  262.5 0.1 sub.205
  262.7 0.1 add.654
  262.9 0.1 copy.27
  263.0 0.1 reshape.610
  263.1 0.3 reduce-window.29
  263.5 0.1 copy.28
  263.6 0.1 reshape.616
  263.7 0.1 reshape.609
  263.9 0.1 copy.23
  264.0 0.1 reshape.606
  264.1 0.3 reduce-window.25
  264.5 0.1 copy.24
  264.6 0.1 reshape.614
  264.7 0.1 reshape.605
  264.9 0.1 slice_reduce_fusion.2
  265.0 0.1 slice_reduce_fusion
  265.2 0.5 slice_bitcast_fusion.1.source
  265.7 4.0 %collective-permute-start.4 = (f32[64,64,128]{2,1,0:T(8,128)S(1)}, f32[64,64,128]{2,1,0:T(8,128)}, u32[]{:S(2)}, u32[]{:S(2)}) collective-permute-start(f32[64,64,128]{2,1,0:T(8,128)S(1)} %collective-permute-done.3.refs_2_), channel_id=1, source_target_pairs={{0,8},{1,9},{2,10},{3,11},{4,12},{5,13},{6,14},{7,15},{8,0},{9,1},... | collective-permute-start | bytes 6291464 | tf_op jit(solution)/shard_map/ppermute | solution.py:20
  269.7 4.9 %collect.3 = (f32[32,128,128]{2,1,0:T(8,128)}, f32[32,128,128]{2,1,0:T(8,128)}) custom-call(s32[64]{0:T(128)} %slice_bitcast_fusion.1.source, f32[128,128,128]{2,1,0:T(8,128)} %all-to-all-done.1.recv), custom_call_target="tpu_custom_call" | custom-call | tf_op jit(solution)/shard_map/collect/pallas_call | solution.py:140
  274.6 1.6 collective-permute-start.7
  276.2 4.1 %collective-permute-start.8 = (f32[32,128,128]{2,1,0:T(8,128)}, f32[32,128,128]{2,1,0:T(8,128)S(1)}, u32[]{:S(2)}, u32[]{:S(2)}) collective-permute-start(f32[32,128,128]{2,1,0:T(8,128)} %get-tuple-element.8.refs_2_), channel_id=1, source_target_pairs={{0,112},{16,0},{32,16},{48,32},{64,48},{80,64},{96,80},{112,96},{1... | collective-permute-start | bytes 6291464 | tf_op jit(solution)/shard_map/ppermute | solution.py:20
  280.3 0.1 slice_reduce_fusion.1
  280.5 5.6 %collective-permute-start.6 = (f32[32,128,128]{2,1,0:T(8,128)}, f32[32,128,128]{2,1,0:T(8,128)S(1)}, u32[]{:S(2)}, u32[]{:S(2)}) collective-permute-start(f32[32,128,128]{2,1,0:T(8,128)} %get-tuple-element.7.refs_3_), channel_id=1, source_target_pairs={{0,112},{16,0},{32,16},{48,32},{64,48},{80,64},{96,80},{112,96},{1... | collective-permute-start | bytes 6291464 | tf_op jit(solution)/shard_map/ppermute | solution.py:20
  286.1 0.1 select_reduce_fusion.4
  286.3 0.3 select_reduce_fusion.2
  286.7 0.3 select_reduce_fusion.3
  287.0 1.6 copy-done
  288.6 1.6 copy-done.1
  290.2 1.6 copy-done.2
  291.8 7.7 %products.3.refs_6_ = f32[96,128,128]{2,1,0:T(8,128)} custom-call(s32[1]{0:T(128)} %bitcast.14.counts, s32[256]{0:T(256)S(1)} %broadcast_add_fusion.6.items, s32[1]{0:T(128)S(1)} %bitcast.39, f32[64,64,128]{2,1,0:T(8,128)S(1)} %copy-done, f32[64,64,128]{2,1,0:T(8,128)} %collective-permute-done.1.refs_1_, f32[32,128,128]{2,1,0:T(8,128)S(1)} %copy-done.2, ...), custom_call_target="tpu_custom_call" | custom-call | flops 600000000 | bytes 8000000 | tf_op jit(solution)/shard_map/products/pallas_call | solution.py:240
  299.6 16.6 %collective-permute-done.4.refs_3_ = f32[64,64,128]{2,1,0:T(8,128)} collective-permute-done((f32[64,64,128]{2,1,0:T(8,128)S(1)}, f32[64,64,128]{2,1,0:T(8,128)}, u32[]{:S(2)}, u32[]{:S(2)}) %collective-permute-start.4) | collective-permute-done | bytes 2097184 | tf_op jit(solution)/shard_map/ppermute | solution.py:20
  316.1 10.8 %collective-permute-done.7.refs_4_ = f32[32,128,128]{2,1,0:T(8,128)S(1)} collective-permute-done((f32[32,128,128]{2,1,0:T(8,128)}, f32[32,128,128]{2,1,0:T(8,128)S(1)}, u32[]{:S(2)}, u32[]{:S(2)}) %collective-permute-start.7) | collective-permute-done | bytes 2097184 | tf_op jit(solution)/shard_map/ppermute | solution.py:20
  326.9 10.6 %products.4.refs_6_ = f32[96,128,128]{2,1,0:T(8,128)} custom-call(s32[1]{0:T(128)} %bitcast.11.counts, s32[512]{0:T(512)S(1)} %broadcast_add_fusion.4.items, s32[2]{0:T(128)S(1)} %slice.63.order, f32[64,64,128]{2,1,0:T(8,128)} %collective-permute-done.refs_0_, f32[64,64,128]{2,1,0:T(8,128)} %collective-permute-done.2.refs_1_, ...), custom_call_target="tpu_custom_call" | custom-call | flops 1200000000 | bytes 16000000 | tf_op jit(solution)/shard_map/products/pallas_call | solution.py:240
  337.6 33.6 %collective-permute-done.5.refs_4_ = f32[32,128,128]{2,1,0:T(8,128)S(1)} collective-permute-done((f32[32,128,128]{2,1,0:T(8,128)}, f32[32,128,128]{2,1,0:T(8,128)S(1)}, u32[]{:S(2)}, u32[]{:S(2)}) %collective-permute-start.5) | collective-permute-done | bytes 2097184 | tf_op jit(solution)/shard_map/ppermute | solution.py:20
  371.2 10.7 %products.5 = f32[96,128,128]{2,1,0:T(8,128)} custom-call(s32[1]{0:T(128)} %bitcast.3.counts, s32[512]{0:T(512)S(1)} %broadcast_add_fusion.5.items, s32[2]{0:T(128)S(1)} %slice.63.order, f32[64,64,128]{2,1,0:T(8,128)} %collective-permute-done.refs_0_, f32[64,64,128]{2,1,0:T(8,128)} %collective-permute-done.2.refs_1_, ...), custom_call_target="tpu_custom_call" | custom-call | flops 1200000000 | bytes 16000000 | tf_op jit(solution)/shard_map/products/pallas_call | solution.py:240
  (90 shorter events, 3.5 us)
Async XLA Ops:
  9.1 10.7 %copy-start.3 = (s32[16,6]{0,1:T(8,128)S(1)}, s32[16,6]{0,1:T(8,128)}, u32[]{:S(2)}) copy-start(s32[16,6]{0,1:T(8,128)} %param.13) | copy-start | bytes 1156
  9.1 11.6 %copy-start.4 = (s32[64]{0:T(128)S(1)}, s32[64]{0:T(128)}, u32[]{:S(2)}) copy-start(s32[64]{0:T(128)} %param.11) | copy-start | bytes 772
  9.1 65.9 %all-to-all-start = ((f32[128,72,128]{2,1,0:T(8,128)}), f32[128,72,128]{2,1,0:T(8,128)}, u32[]{:S(2)}, u32[]{:S(2)}) async-start(f32[128,72,128]{2,1,0:T(8,128)} %pack_left.1), calls=%async_computation | async-start | bytes 9437184 | tf_op jit(solution)/shard_map/all_to_all | solution.py:311
  75.0 194.7 %all-to-all-start.1 = ((f32[128,128,128]{2,1,0:T(8,128)}), f32[128,128,128]{2,1,0:T(8,128)}, u32[]{:S(2)}, u32[]{:S(2)}) async-start(f32[128,128,128]{2,1,0:T(8,128)} %pack_right.1), calls=%async_computation.1 | async-start | bytes 16777216 | tf_op jit(solution)/shard_map/all_to_all | solution.py:312
  96.4 162.4 %collective-permute-start.1 = (f32[64,64,128]{2,1,0:T(8,128)}, f32[64,64,128]{2,1,0:T(8,128)}, u32[]{:S(2)}, u32[]{:S(2)}) collective-permute-start(f32[64,64,128]{2,1,0:T(8,128)} %collect.2.refs_0_), channel_id=1, source_target_pairs={{0,8},{1,9},{2,10},{3,11},{4,12},{5,13},{6,14},{7,15},{8,0},{9,1},... | collective-permute-start | bytes 6291464 | tf_op jit(solution)/shard_map/ppermute | solution.py:20
  97.9 167.8 %collective-permute-start.3 = (f32[64,64,128]{2,1,0:T(8,128)}, f32[64,64,128]{2,1,0:T(8,128)S(1)}, u32[]{:S(2)}, u32[]{:S(2)}) collective-permute-start(f32[64,64,128]{2,1,0:T(8,128)} %collect.2.refs_0_), channel_id=1, source_target_pairs={{0,15},{1,2},{2,1},{3,4},{4,3},{5,6},{6,5},{7,8},{8,7},{9,10},{10,... | collective-permute-start | bytes 6291464 | tf_op jit(solution)/shard_map/ppermute | solution.py:25
  97.9 182.5 %collective-permute-start = (f32[64,64,128]{2,1,0:T(8,128)}, f32[64,64,128]{2,1,0:T(8,128)}, u32[]{:S(2)}, u32[]{:S(2)}) collective-permute-start(f32[64,64,128]{2,1,0:T(8,128)} %collect.2.refs_0_), channel_id=1, source_target_pairs={{0,1},{1,0},{2,3},{3,2},{4,5},{5,4},{6,7},{7,6},{8,9},{9,8},{10,11... | collective-permute-start | bytes 6291464 | tf_op jit(solution)/shard_map/ppermute | solution.py:25
  258.9 21.6 %collective-permute-start.2 = (f32[64,64,128]{2,1,0:T(8,128)}, f32[64,64,128]{2,1,0:T(8,128)}, u32[]{:S(2)}, u32[]{:S(2)}) collective-permute-start(f32[64,64,128]{2,1,0:T(8,128)} %collective-permute-done.1.refs_1_), channel_id=1, source_target_pairs={{0,1},{1,0},{2,3},{3,2},{4,5},{5,4},{6,7},{7,6},{8,9},{9,8},{10,11... | collective-permute-start | bytes 6291464 | tf_op jit(solution)/shard_map/ppermute | solution.py:25
  265.7 50.4 %collective-permute-start.4 = (f32[64,64,128]{2,1,0:T(8,128)S(1)}, f32[64,64,128]{2,1,0:T(8,128)}, u32[]{:S(2)}, u32[]{:S(2)}) collective-permute-start(f32[64,64,128]{2,1,0:T(8,128)S(1)} %collective-permute-done.3.refs_2_), channel_id=1, source_target_pairs={{0,8},{1,9},{2,10},{3,11},{4,12},{5,13},{6,14},{7,15},{8,0},{9,1},... | collective-permute-start | bytes 6291464 | tf_op jit(solution)/shard_map/ppermute | solution.py:20
  274.6 52.4 %collective-permute-start.7 = (f32[32,128,128]{2,1,0:T(8,128)}, f32[32,128,128]{2,1,0:T(8,128)S(1)}, u32[]{:S(2)}, u32[]{:S(2)}) collective-permute-start(f32[32,128,128]{2,1,0:T(8,128)} %get-tuple-element.8.refs_2_), channel_id=1, source_target_pairs={{0,16},{16,32},{32,48},{48,64},{64,80},{80,96},{96,112},{112,0},{1... | collective-permute-start | bytes 6291464 | tf_op jit(solution)/shard_map/ppermute | solution.py:20
  276.2 50.7 %collective-permute-start.8 = (f32[32,128,128]{2,1,0:T(8,128)}, f32[32,128,128]{2,1,0:T(8,128)S(1)}, u32[]{:S(2)}, u32[]{:S(2)}) collective-permute-start(f32[32,128,128]{2,1,0:T(8,128)} %get-tuple-element.8.refs_2_), channel_id=1, source_target_pairs={{0,112},{16,0},{32,16},{48,32},{64,48},{80,64},{96,80},{112,96},{1... | collective-permute-start | bytes 6291464 | tf_op jit(solution)/shard_map/ppermute | solution.py:20
  280.4 90.8 %collective-permute-start.5 = (f32[32,128,128]{2,1,0:T(8,128)}, f32[32,128,128]{2,1,0:T(8,128)S(1)}, u32[]{:S(2)}, u32[]{:S(2)}) collective-permute-start(f32[32,128,128]{2,1,0:T(8,128)} %get-tuple-element.7.refs_3_), channel_id=1, source_target_pairs={{0,16},{16,32},{32,48},{48,64},{64,80},{80,96},{96,112},{112,0},{1... | collective-permute-start | bytes 6291464 | tf_op jit(solution)/shard_map/ppermute | solution.py:20
  280.5 90.7 %collective-permute-start.6 = (f32[32,128,128]{2,1,0:T(8,128)}, f32[32,128,128]{2,1,0:T(8,128)S(1)}, u32[]{:S(2)}, u32[]{:S(2)}) collective-permute-start(f32[32,128,128]{2,1,0:T(8,128)} %get-tuple-element.7.refs_3_), channel_id=1, source_target_pairs={{0,112},{16,0},{32,16},{48,32},{64,48},{80,64},{96,80},{112,96},{1... | collective-permute-start | bytes 6291464 | tf_op jit(solution)/shard_map/ppermute | solution.py:20
  287.0 1.6 copy-start
  288.6 1.6 copy-start.1
  290.2 1.6 copy-start.2

commit v4 on v3

--- a/solution.py
+++ b/solution.py
@@ -25,55 +25,42 @@
     return lax.ppermute(value, axis, [(at, target(at) % count) for at in range(count)])
 
 
-def relay(count, load, store):
+def pack_kernel(pieces, dest, held, *refs):
+    labels = refs[0] if len(refs) > 3 else None
+    out, buf, sems = refs[-3:]
+    count, rows, _ = held.shape
+    devices = out.shape[0]
+    part = rows // pieces
+
+    def load(at):
+        return pltpu.make_async_copy(held.at[at], buf.at[at], sems.at[at])
+
+    def save(at, piece):
+        return pltpu.make_async_copy(
+            buf.at[at, pl.ds(piece * part, part)],
+            out.at[dest[piece, at], pl.ds(0, part)],
+            sems.at[(1 + piece) * count + at],
+        )
+
+    def mark(at):
+        return pltpu.make_async_copy(
+            labels, out.at[at, pl.ds(part, 8)], sems.at[(1 + pieces) * count + at]
+        )
+
     pl.loop(0, count)(lambda at: load(at).start())
+    if labels is not None:
+        pl.loop(0, devices)(lambda at: mark(at).start())
 
     def body(at):
         load(at).wait()
-        store(at)
+        for piece in range(pieces):
+            save(at, piece).start()
 
     pl.loop(0, count)(body)
-
-
-def pack_right_kernel(dest, held, out, buf, sems):
-    count = held.shape[0]
-
-    def load(at):
-        return pltpu.make_async_copy(held.at[at], buf.at[at], sems.at[0, at])
-
-    def save(at):
-        return pltpu.make_async_copy(buf.at[at], out.at[dest[at]], sems.at[1, at])
-
-    relay(count, load, lambda at: save(at).start())
-    pl.loop(0, count)(lambda at: save(at).wait())
-
-
-def pack_left_kernel(copies, part, dest, held, labels, out, buf, sems, mark_sems):
-    count = held.shape[0]
-    devices = out.shape[0]
-
-    def mark(at):
-        return pltpu.make_async_copy(labels, out.at[at, pl.ds(part, 8)], mark_sems.at[at])
-
-    def load(at):
-        return pltpu.make_async_copy(held.at[at], buf.at[at], sems.at[0, at])
-
-    def save(at, half):
-        return pltpu.make_async_copy(
-            buf.at[at, pl.ds(half * part, part)],
-            out.at[dest[half, at], pl.ds(0, part)],
-            sems.at[1 + half, at],
-        )
-
-    def store(at):
-        for half in range(copies):
-            save(at, half).start()
-
-    relay(count, load, store)
-    pl.loop(0, devices)(lambda at: mark(at).start())
-    for half in range(copies):
-        pl.loop(0, count)(lambda at: save(at, half).wait())
-    pl.loop(0, devices)(lambda at: mark(at).wait())
+    for piece in range(pieces):
+        pl.loop(0, count)(lambda at: save(at, piece).wait())
+    if labels is not None:
+        pl.loop(0, devices)(lambda at: mark(at).wait())
 
 
 def collect_kernel(source, recv, *refs):
@@ -102,36 +89,22 @@
 SMEM = pl.BlockSpec(memory_space=pltpu.SMEM)
 
 
-def pack_right(held, dest, devices):
+def pack(held, dest, devices, labels=None):
+    pieces = dest.shape[0]
+    count, rows, cols = held.shape
+    part = rows // pieces
+    marks = [] if labels is None else [labels]
     return pl.pallas_call(
-        pack_right_kernel,
-        out_shape=jax.ShapeDtypeStruct((devices,) + held.shape[1:], held.dtype),
-        in_specs=[SMEM, HBM],
+        functools.partial(pack_kernel, pieces),
+        out_shape=jax.ShapeDtypeStruct((devices, part + 8 * len(marks), cols), held.dtype),
+        in_specs=[SMEM, HBM] + [pl.BlockSpec(memory_space=pltpu.VMEM)] * len(marks),
         out_specs=HBM,
         scratch_shapes=[
             pltpu.VMEM(held.shape, held.dtype),
-            pltpu.SemaphoreType.DMA((2, held.shape[0])),
+            pltpu.SemaphoreType.DMA(((1 + pieces) * count + devices,)),
         ],
-        name="pack_right",
-    )(dest, held)
-
-
-def pack_left(held, dest, labels, devices):
-    copies = dest.shape[0]
-    count, rows, cols = held.shape
-    part = rows // copies
-    return pl.pallas_call(
-        functools.partial(pack_left_kernel, copies, part),
-        out_shape=jax.ShapeDtypeStruct((devices, part + 8, cols), held.dtype),
-        in_specs=[SMEM, HBM, pl.BlockSpec(memory_space=pltpu.VMEM)],
-        out_specs=HBM,
-        scratch_shapes=[
-            pltpu.VMEM(held.shape, held.dtype),
-            pltpu.SemaphoreType.DMA((1 + copies, count)),
-            pltpu.SemaphoreType.DMA((devices,)),
-        ],
-        name="pack_left",
-    )(dest, held, labels)
+        name="pack",
+    )(dest, held, *marks)
 
 
 def collect(recv, source, rows, chunks):
@@ -306,12 +279,13 @@
     edge = a_held.shape[1]
     labels = jnp.concatenate([a_slot, a_col, b_slot, b_col]).astype(jnp.float32)
     tile = jnp.pad(labels, (0, 8 * edge - labels.shape[0])).reshape(8, edge)
-    send_left = pack_left(a_held, dest_left, tile, devices)
-    send_right = pack_right(b_held, dest_right, devices)
+    send_right = pack(b_held, dest_right[None, :], devices, tile)
+    send_left = pack(a_held, dest_left, devices)
+    recv_right = lax.all_to_all(send_right, ("row", "col"), split_axis=0, concat_axis=0, tiled=True)
+    recv_right, send_left = lax.optimization_barrier((recv_right, send_left))
     recv_left = lax.all_to_all(send_left, ("row", "col"), split_axis=0, concat_axis=0, tiled=True)
-    recv_right = lax.all_to_all(send_right, ("row", "col"), split_axis=0, concat_axis=0, tiled=True)
-
-    labels = recv_left[:, edge // copies :, :].reshape(devices, -1)[:, : labels.shape[0]]
+
+    labels = recv_right[:, edge:, :].reshape(devices, -1)[:, : labels.shape[0]]
     labels = labels.astype(jnp.int32)
     parts = [hold_a, 2 * hold_a, 2 * hold_a + hold_b]
     all_a, all_acol, all_b, all_bcol = (part.reshape(-1) for part in jnp.split(labels, parts, axis=1))

time: 385 us -> 359 us (0.932)
  waiting for transfers between devices: 267 us -> 236 us
  starting transfers between devices: 41.4 us -> 47.7 us
    ppermute x6, waiting for transfers between devices: 219 us -> 70.7 us  [shifted(): return lax.ppermute(value, axis, pairs)]
    all_to_all x1, waiting for transfers between devices: 0.01 us -> 104 us  [on_device(): lax.all_to_all(send_right, ('row', 'col'), split_axis=0, concat_axis=0, t...]
    ppermute x3, waiting for transfers between devices: 0.01 us -> 24.6 us  [permuted(): lax.ppermute(value, axis, [(at, target(at) % count) for at in range(count)])]
    all_to_all x1, waiting for transfers between devices: 47.5 us -> 36 us  [on_device(): lax.all_to_all(send_left, ('row', 'col'), split_axis=0, concat_axis=0, ti...]
  transfers between devices with their start and end apart: 11 -> 11, of which waited for: 5 -> 5; matrix products, arithmetic and copies ran while one was open for 4% -> 3% of each run, Pallas kernels for 9% -> 9%
where the time goes in v4:
time: 359 us; the launch traced here: 356 us
  waiting for transfers between devices  236 us (66%)
  Pallas kernels  48.9 us (14%)
  starting transfers between devices  47.7 us (13%)
  local copies, waits for them, and re-layouts  11.7 us (3%)
  other arithmetic  9.27 us (3%)
    all_to_all x1, waiting for transfers between devices, on_device(): lax.all_to_all(send_right, ('row', 'col'), split_axis=0, concat_axis=0, t...  104 us
    ppermute x6, waiting for transfers between devices, shifted(): return lax.ppermute(value, axis, pairs)  70.7 us
    all_to_all x1, waiting for transfers between devices, on_device(): lax.all_to_all(send_left, ('row', 'col'), split_axis=0, concat_axis=0, ti...  36 us
    pallas_call x3, Pallas kernels, products(): pl.pallas_call(functools.partial(product_kernel, pieces, parts, first, UN...  26.7 us
    ppermute x3, waiting for transfers between devices, permuted(): lax.ppermute(value, axis, [(at, target(at) % count) for at in range(count)])  24.6 us
    ppermute x6, starting transfers between devices, shifted(): return lax.ppermute(value, axis, pairs)  19.3 us
    all_to_all x1, starting transfers between devices, on_device(): lax.all_to_all(send_left, ('row', 'col'), split_axis=0, concat_axis=0, ti...  14.3 us
    pallas_call x2, Pallas kernels, pack(): pl.pallas_call(functools.partial(pack_kernel, pieces), out_shape=jax.Shap...  13.3 us
  transfers between devices with their start and end apart: 11, of which 5 were waited for; matrix products, arithmetic and copies ran while one was open for 3% of the time, Pallas kernels for 9%

profile of v4, /device:TPU:26, one launch (start us, length us, event | category | flops | bytes accessed | tf_op | source)
XLA Modules:
  0.0 355.8 jit_solution(17172219847450691624)
XLA Ops:
  0.0 1.3 fusion.30.dest
  1.3 0.8 add_convert_fusion
  2.1 0.6 pad_bitcast_fusion.refs_0_
  2.7 8.2 %pack.2 = f32[128,136,128]{2,1,0:T(8,128)} custom-call(s32[1,64]{1,0:T(1,128)} %fusion.30.dest, f32[64,128,128]{2,1,0:T(8,128)} %held.2, f32[8,128]{1,0:T(8,128)} %pad_bitcast_fusion.refs_0_), custom_call_target="tpu_custom_call" | custom-call | tf_op jit(solution)/shard_map/pack/pallas_call | solution.py:97
  10.9 10.7 %all-to-all-start = ((f32[128,136,128]{2,1,0:T(8,128)}), f32[128,136,128]{2,1,0:T(8,128)}, u32[]{:S(2)}, u32[]{:S(2)}) async-start(f32[128,136,128]{2,1,0:T(8,128)} %pack.2), calls=%async_computation | async-start | bytes 17825792 | tf_op jit(solution)/shard_map/all_to_all | solution.py:284
  21.9 0.1 add.660
  22.1 0.1 add.652
  22.2 0.1 add.656
  22.5 0.7 broadcast_add_fusion.8.dest
  23.2 5.1 %pack.3 = f32[128,64,128]{2,1,0:T(8,128)} custom-call(s32[2,32]{1,0:T(2,128)} %broadcast_add_fusion.8.dest, f32[32,128,128]{2,1,0:T(8,128)} %held.3), custom_call_target="tpu_custom_call" | custom-call | tf_op jit(solution)/shard_map/pack/pallas_call | solution.py:97
  28.7 104.2 %all-to-all-done.recv = f32[128,136,128]{2,1,0:T(8,128)} async-done(((f32[128,136,128]{2,1,0:T(8,128)}), f32[128,136,128]{2,1,0:T(8,128)}, u32[]{:S(2)}, u32[]{:S(2)}) %all-to-all-start) | async-done | bytes 8912928 | tf_op jit(solution)/shard_map/all_to_all | solution.py:284
  132.9 1.1 slice.57
  134.5 0.9 select_reduce_fusion
  135.4 14.3 %all-to-all-start.1 = ((f32[128,64,128]{2,1,0:T(8,128)}), f32[128,64,128]{2,1,0:T(8,128)}, u32[]{:S(2)}, u32[]{:S(2)}) async-start(f32[128,64,128]{2,1,0:T(8,128)} %pack.3), calls=%async_computation.1 | async-start | bytes 8388608 | tf_op jit(solution)/shard_map/all_to_all | solution.py:286
  149.7 0.6 slice_bitcast_fusion.1.source
  150.3 4.8 %collect.3 = (f32[32,128,128]{2,1,0:T(8,128)}, f32[32,128,128]{2,1,0:T(8,128)}) custom-call(s32[64]{0:T(128)} %slice_bitcast_fusion.1.source, f32[128,136,128]{2,1,0:T(8,128)} %all-to-all-done.recv), custom_call_target="tpu_custom_call" | custom-call | tf_op jit(solution)/shard_map/collect/pallas_call | solution.py:113
  155.2 1.8 collective-permute-start.7
  157.0 3.9 %collective-permute-start.8 = (f32[32,128,128]{2,1,0:T(8,128)}, f32[32,128,128]{2,1,0:T(8,128)}, u32[]{:S(2)}, u32[]{:S(2)}) collective-permute-start(f32[32,128,128]{2,1,0:T(8,128)} %get-tuple-element.12.refs_2_), channel_id=1, source_target_pairs={{0,112},{16,0},{32,16},{48,32},{64,48},{80,64},{96,80},{112,96},{1... | collective-permute-start | bytes 6291464 | tf_op jit(solution)/shard_map/ppermute | solution.py:20
  161.5 0.5 select_reduce_fusion.1
  162.5 0.5 slice_bitcast_fusion.2.source
  163.0 36.0 %all-to-all-done.1.recv = f32[128,64,128]{2,1,0:T(8,128)} async-done(((f32[128,64,128]{2,1,0:T(8,128)}), f32[128,64,128]{2,1,0:T(8,128)}, u32[]{:S(2)}, u32[]{:S(2)}) %all-to-all-start.1) | async-done | bytes 4194336 | tf_op jit(solution)/shard_map/all_to_all | solution.py:286
  199.0 4.1 %collect.2.refs_0_ = f32[64,64,128]{2,1,0:T(8,128)} custom-call(s32[64]{0:T(128)} %slice_bitcast_fusion.2.source, f32[128,64,128]{2,1,0:T(8,128)} %all-to-all-done.1.recv), custom_call_target="tpu_custom_call" | custom-call | tf_op jit(solution)/shard_map/collect/pallas_call | solution.py:113
  203.2 4.0 %collective-permute-start.1 = (f32[64,64,128]{2,1,0:T(8,128)}, f32[64,64,128]{2,1,0:T(8,128)}, u32[]{:S(2)}, u32[]{:S(2)}) collective-permute-start(f32[64,64,128]{2,1,0:T(8,128)} %collect.2.refs_0_), channel_id=1, source_target_pairs={{0,8},{1,9},{2,10},{3,11},{4,12},{5,13},{6,14},{7,15},{8,0},{9,1},... | collective-permute-start | bytes 6291464 | tf_op jit(solution)/shard_map/ppermute | solution.py:20
  207.2 0.6 broadcast_add_fusion.2
  208.5 0.1 select_reduce_fusion.8
  208.6 0.1 copy.26
  208.7 0.6 convert_reduce_fusion
  210.0 0.1 copy.22
  210.2 0.6 convert_reduce_fusion.1
  211.5 0.1 copy.31
  211.6 0.1 reshape.612
  211.7 0.3 reduce-window.37
  212.2 0.1 sub.205
  212.4 0.1 add.654
  212.5 0.1 copy.27
  212.6 0.1 reshape.610
  212.8 0.3 reduce-window.29
  213.2 0.1 copy.28
  213.3 0.1 reshape.616
  213.4 0.1 reshape.609
  213.6 0.1 copy.23
  213.7 0.1 reshape.606
  213.8 0.3 reduce-window.25
  214.2 0.1 copy.24
  214.3 0.1 reshape.614
  214.4 0.1 reshape.605
  214.6 0.1 slice_reduce_fusion.2
  214.7 0.1 slice_reduce_fusion
  214.9 3.5 collective-permute-start
  218.4 43.9 %collective-permute-done.1.refs_1_ = f32[64,64,128]{2,1,0:T(8,128)} collective-permute-done((f32[64,64,128]{2,1,0:T(8,128)}, f32[64,64,128]{2,1,0:T(8,128)}, u32[]{:S(2)}, u32[]{:S(2)}) %collective-permute-start.1) | collective-permute-done | bytes 2097184 | tf_op jit(solution)/shard_map/ppermute | solution.py:20
  262.3 24.6 %collective-permute-done.3.refs_2_ = f32[64,64,128]{2,1,0:T(8,128)S(1)} collective-permute-done((f32[64,64,128]{2,1,0:T(8,128)}, f32[64,64,128]{2,1,0:T(8,128)S(1)}, u32[]{:S(2)}, u32[]{:S(2)}) %collective-permute-start.3) | collective-permute-done | bytes 2097184 | tf_op jit(solution)/shard_map/ppermute | solution.py:25
  286.9 3.9 %collective-permute-start.4 = (f32[64,64,128]{2,1,0:T(8,128)S(1)}, f32[64,64,128]{2,1,0:T(8,128)S(1)}, u32[]{:S(2)}, u32[]{:S(2)}) collective-permute-start(f32[64,64,128]{2,1,0:T(8,128)S(1)} %collective-permute-done.3.refs_2_), channel_id=1, source_target_pairs={{0,8},{1,9},{2,10},{3,11},{4,12},{5,13},{6,14},{7,15},{8,0},{9,1},... | collective-permute-start | bytes 6291464 | tf_op jit(solution)/shard_map/ppermute | solution.py:20
  290.8 0.1 slice_reduce_fusion.1
  291.0 5.6 %collective-permute-start.6 = (f32[32,128,128]{2,1,0:T(8,128)}, f32[32,128,128]{2,1,0:T(8,128)S(1)}, u32[]{:S(2)}, u32[]{:S(2)}) collective-permute-start(f32[32,128,128]{2,1,0:T(8,128)} %get-tuple-element.11.refs_3_), channel_id=1, source_target_pairs={{0,112},{16,0},{32,16},{48,32},{64,48},{80,64},{96,80},{112,96},{1... | collective-permute-start | bytes 6291464 | tf_op jit(solution)/shard_map/ppermute | solution.py:20
  296.6 0.1 select_reduce_fusion.4
  296.8 0.3 select_reduce_fusion.2
  297.2 0.3 select_reduce_fusion.3
  297.5 1.6 copy-done
  299.1 1.6 copy-done.1
  300.7 1.6 copy-done.2
  302.3 7.7 %products.3.refs_6_ = f32[96,128,128]{2,1,0:T(8,128)} custom-call(s32[1]{0:T(128)} %bitcast.15.counts, s32[256]{0:T(256)S(1)} %broadcast_add_fusion.6.items, s32[1]{0:T(128)S(1)} %bitcast.41, f32[64,64,128]{2,1,0:T(8,128)S(1)} %copy-done, f32[64,64,128]{2,1,0:T(8,128)} %collective-permute-done.1.refs_1_, f32[32,128,128]{2,1,0:T(8,128)S(1)} %copy-done.2, ...), custom_call_target="tpu_custom_call" | custom-call | flops 600000000 | bytes 8000000 | tf_op jit(solution)/shard_map/products/pallas_call | solution.py:213
  310.0 26.8 %collective-permute-done.4.refs_3_ = f32[64,64,128]{2,1,0:T(8,128)S(1)} collective-permute-done((f32[64,64,128]{2,1,0:T(8,128)S(1)}, f32[64,64,128]{2,1,0:T(8,128)S(1)}, u32[]{:S(2)}, u32[]{:S(2)}) %collective-permute-start.4) | collective-permute-done | bytes 2097184 | tf_op jit(solution)/shard_map/ppermute | solution.py:20
  336.8 10.5 %products.4.refs_6_ = f32[96,128,128]{2,1,0:T(8,128)} custom-call(s32[1]{0:T(128)} %bitcast.12.counts, s32[512]{0:T(512)S(1)} %broadcast_add_fusion.4.items, s32[2]{0:T(128)S(1)} %slice.63.order, f32[64,64,128]{2,1,0:T(8,128)S(1)} %collective-permute-done.refs_0_, f32[64,64,128]{2,1,0:T(8,128)S(1)} %collective-permute-done.2.refs_1_, ...), custom_call_target="tpu_custom_call" | custom-call | flops 1200000000 | bytes 16000000 | tf_op jit(solution)/shard_map/products/pallas_call | solution.py:213
  347.3 8.4 %products.5 = f32[96,128,128]{2,1,0:T(8,128)} custom-call(s32[1]{0:T(128)} %bitcast.4.counts, s32[512]{0:T(512)S(1)} %broadcast_add_fusion.5.items, s32[2]{0:T(128)S(1)} %slice.63.order, f32[64,64,128]{2,1,0:T(8,128)S(1)} %collective-permute-done.refs_0_, f32[64,64,128]{2,1,0:T(8,128)S(1)} %collective-permute-done.2.refs_1_, ...), custom_call_target="tpu_custom_call" | custom-call | flops 1200000000 | bytes 16000000 | tf_op jit(solution)/shard_map/products/pallas_call | solution.py:213
  (90 shorter events, 3.4 us)
Async XLA Ops:
  10.9 10.7 %copy-start.3 = (s32[16,6]{0,1:T(8,128)S(1)}, s32[16,6]{0,1:T(8,128)}, u32[]{:S(2)}) copy-start(s32[16,6]{0,1:T(8,128)} %param.13) | copy-start | bytes 1156
  10.9 11.6 %copy-start.4 = (s32[32]{0:T(128)S(1)}, s32[32]{0:T(128)}, u32[]{:S(2)}) copy-start(s32[32]{0:T(128)} %param.8) | copy-start | bytes 388
  10.9 122.0 %all-to-all-start = ((f32[128,136,128]{2,1,0:T(8,128)}), f32[128,136,128]{2,1,0:T(8,128)}, u32[]{:S(2)}, u32[]{:S(2)}) async-start(f32[128,136,128]{2,1,0:T(8,128)} %pack.2), calls=%async_computation | async-start | bytes 17825792 | tf_op jit(solution)/shard_map/all_to_all | solution.py:284
  135.4 63.6 %all-to-all-start.1 = ((f32[128,64,128]{2,1,0:T(8,128)}), f32[128,64,128]{2,1,0:T(8,128)}, u32[]{:S(2)}, u32[]{:S(2)}) async-start(f32[128,64,128]{2,1,0:T(8,128)} %pack.3), calls=%async_computation.1 | async-start | bytes 8388608 | tf_op jit(solution)/shard_map/all_to_all | solution.py:286
  155.2 135.7 %collective-permute-start.7 = (f32[32,128,128]{2,1,0:T(8,128)}, f32[32,128,128]{2,1,0:T(8,128)}, u32[]{:S(2)}, u32[]{:S(2)}) collective-permute-start(f32[32,128,128]{2,1,0:T(8,128)} %get-tuple-element.12.refs_2_), channel_id=1, source_target_pairs={{0,16},{16,32},{32,48},{48,64},{64,80},{80,96},{96,112},{112,0},{1... | collective-permute-start | bytes 6291464 | tf_op jit(solution)/shard_map/ppermute | solution.py:20
  157.0 134.0 %collective-permute-start.8 = (f32[32,128,128]{2,1,0:T(8,128)}, f32[32,128,128]{2,1,0:T(8,128)}, u32[]{:S(2)}, u32[]{:S(2)}) collective-permute-start(f32[32,128,128]{2,1,0:T(8,128)} %get-tuple-element.12.refs_2_), channel_id=1, source_target_pairs={{0,112},{16,0},{32,16},{48,32},{64,48},{80,64},{96,80},{112,96},{1... | collective-permute-start | bytes 6291464 | tf_op jit(solution)/shard_map/ppermute | solution.py:20
  203.2 59.1 %collective-permute-start.1 = (f32[64,64,128]{2,1,0:T(8,128)}, f32[64,64,128]{2,1,0:T(8,128)}, u32[]{:S(2)}, u32[]{:S(2)}) collective-permute-start(f32[64,64,128]{2,1,0:T(8,128)} %collect.2.refs_0_), channel_id=1, source_target_pairs={{0,8},{1,9},{2,10},{3,11},{4,12},{5,13},{6,14},{7,15},{8,0},{9,1},... | collective-permute-start | bytes 6291464 | tf_op jit(solution)/shard_map/ppermute | solution.py:20
  207.2 79.7 %collective-permute-start.3 = (f32[64,64,128]{2,1,0:T(8,128)}, f32[64,64,128]{2,1,0:T(8,128)S(1)}, u32[]{:S(2)}, u32[]{:S(2)}) collective-permute-start(f32[64,64,128]{2,1,0:T(8,128)} %collect.2.refs_0_), channel_id=1, source_target_pairs={{0,15},{1,2},{2,1},{3,4},{4,3},{5,6},{6,5},{7,8},{8,7},{9,10},{10,... | collective-permute-start | bytes 6291464 | tf_op jit(solution)/shard_map/ppermute | solution.py:25
  214.9 95.1 %collective-permute-start = (f32[64,64,128]{2,1,0:T(8,128)}, f32[64,64,128]{2,1,0:T(8,128)S(1)}, u32[]{:S(2)}, u32[]{:S(2)}) collective-permute-start(f32[64,64,128]{2,1,0:T(8,128)} %collect.2.refs_0_), channel_id=1, source_target_pairs={{0,1},{1,0},{2,3},{3,2},{4,5},{5,4},{6,7},{7,6},{8,9},{9,8},{10,11... | collective-permute-start | bytes 6291464 | tf_op jit(solution)/shard_map/ppermute | solution.py:25
  262.3 47.8 %collective-permute-start.2 = (f32[64,64,128]{2,1,0:T(8,128)}, f32[64,64,128]{2,1,0:T(8,128)S(1)}, u32[]{:S(2)}, u32[]{:S(2)}) collective-permute-start(f32[64,64,128]{2,1,0:T(8,128)} %collective-permute-done.1.refs_1_), channel_id=1, source_target_pairs={{0,1},{1,0},{2,3},{3,2},{4,5},{5,4},{6,7},{7,6},{8,9},{9,8},{10,11... | collective-permute-start | bytes 6291464 | tf_op jit(solution)/shard_map/ppermute | solution.py:25
  286.9 50.0 %collective-permute-start.4 = (f32[64,64,128]{2,1,0:T(8,128)S(1)}, f32[64,64,128]{2,1,0:T(8,128)S(1)}, u32[]{:S(2)}, u32[]{:S(2)}) collective-permute-start(f32[64,64,128]{2,1,0:T(8,128)S(1)} %collective-permute-done.3.refs_2_), channel_id=1, source_target_pairs={{0,8},{1,9},{2,10},{3,11},{4,12},{5,13},{6,14},{7,15},{8,0},{9,1},... | collective-permute-start | bytes 6291464 | tf_op jit(solution)/shard_map/ppermute | solution.py:20
  290.9 56.5 %collective-permute-start.5 = (f32[32,128,128]{2,1,0:T(8,128)}, f32[32,128,128]{2,1,0:T(8,128)S(1)}, u32[]{:S(2)}, u32[]{:S(2)}) collective-permute-start(f32[32,128,128]{2,1,0:T(8,128)} %get-tuple-element.11.refs_3_), channel_id=1, source_target_pairs={{0,16},{16,32},{32,48},{48,64},{64,80},{80,96},{96,112},{112,0},{1... | collective-permute-start | bytes 6291464 | tf_op jit(solution)/shard_map/ppermute | solution.py:20
  291.0 56.4 %collective-permute-start.6 = (f32[32,128,128]{2,1,0:T(8,128)}, f32[32,128,128]{2,1,0:T(8,128)S(1)}, u32[]{:S(2)}, u32[]{:S(2)}) collective-permute-start(f32[32,128,128]{2,1,0:T(8,128)} %get-tuple-element.11.refs_3_), channel_id=1, source_target_pairs={{0,112},{16,0},{32,16},{48,32},{64,48},{80,64},{96,80},{112,96},{1... | collective-permute-start | bytes 6291464 | tf_op jit(solution)/shard_map/ppermute | solution.py:20
  297.5 1.6 copy-start
  299.1 1.6 copy-start.1
  300.7 1.6 copy-start.2

commit v5 on v4

--- a/solution.py
+++ b/solution.py
@@ -26,10 +26,8 @@
 
 
 def pack_kernel(pieces, dest, held, *refs):
-    labels = refs[0] if len(refs) > 3 else None
-    out, buf, sems = refs[-3:]
+    outs, buf, sems = refs[:-2], refs[-2], refs[-1]
     count, rows, _ = held.shape
-    devices = out.shape[0]
     part = rows // pieces
 
     def load(at):
@@ -38,18 +36,11 @@
     def save(at, piece):
         return pltpu.make_async_copy(
             buf.at[at, pl.ds(piece * part, part)],
-            out.at[dest[piece, at], pl.ds(0, part)],
+            outs[piece % len(outs)].at[dest[piece, at]],
             sems.at[(1 + piece) * count + at],
         )
 
-    def mark(at):
-        return pltpu.make_async_copy(
-            labels, out.at[at, pl.ds(part, 8)], sems.at[(1 + pieces) * count + at]
-        )
-
     pl.loop(0, count)(lambda at: load(at).start())
-    if labels is not None:
-        pl.loop(0, devices)(lambda at: mark(at).start())
 
     def body(at):
         load(at).wait()
@@ -59,68 +50,308 @@
     pl.loop(0, count)(body)
     for piece in range(pieces):
         pl.loop(0, count)(lambda at: save(at, piece).wait())
-    if labels is not None:
-        pl.loop(0, devices)(lambda at: mark(at).wait())
-
-
-def collect_kernel(source, recv, *refs):
+
+
+SMEM = pl.BlockSpec(memory_space=pltpu.SMEM)
+VMEM = pl.BlockSpec(memory_space=pltpu.VMEM)
+
+
+def pack(held, dest, devices, outs):
+    pieces = dest.shape[0]
+    count, rows, cols = held.shape
+    shape = jax.ShapeDtypeStruct((devices, rows // pieces, cols), held.dtype)
+    return pl.pallas_call(
+        functools.partial(pack_kernel, pieces),
+        out_shape=[shape] * outs,
+        in_specs=[SMEM, HBM],
+        out_specs=[HBM] * outs,
+        scratch_shapes=[
+            pltpu.VMEM(held.shape, held.dtype),
+            pltpu.SemaphoreType.DMA(((1 + pieces) * count,)),
+        ],
+        name="pack",
+    )(dest, held)
+
+
+ORDERS = (("x", "y", "z"), ("y", "z", "x"), ("z", "x", "y"))
+STEPS_FIRST = (1, 2, 6, 3, 7, 4, 5)
+STEPS_LATER = (1, 3, 2)
+RING = 4
+CORES = 2
+
+
+def my_place():
+    row, col = lax.axis_index("row"), lax.axis_index("col")
+    return {
+        "x": row // RING * 2 + col // CORES % 2,
+        "y": col // RING,
+        "z": row % RING,
+        "core": col % CORES,
+    }
+
+
+def coords_of(place):
+    row = place["x"] // 2 * RING + place["z"]
+    col = place["y"] * RING + place["x"] % 2 * CORES + place["core"]
+    return row, col
+
+
+def exchange_kernel(*refs):
+    parts = len(ORDERS)
+    sends, refs = refs[:parts], refs[parts:]
+    tile, refs = refs[0], refs[1:]
+    stages = [refs[3 * part : 3 * part + 3] for part in range(parts)]
+    labels = refs[3 * parts]
+    first_recv, second_recv, third_recv, send_sems, label_send, label_recv = refs[3 * parts + 1 :]
+    place = my_place()
+
+    def moved(axis, steps, flip):
+        there = dict(place)
+        there[axis] = (place[axis] + steps) % RING
+        there["core"] = (place["core"] + flip) % CORES
+        return there
+
+    def copy(source, target, send_sem, recv_sem, there):
+        return pltpu.make_async_remote_copy(
+            src_ref=source,
+            dst_ref=target,
+            send_sem=send_sem,
+            recv_sem=recv_sem,
+            device_id=coords_of(there),
+            device_id_type=pl.DeviceIdType.MESH,
+        )
+
+    def spot(there, axis):
+        return there[axis] * CORES + there["core"]
+
+    def arrived(like, sem):
+        pltpu.make_async_copy(like, like, sem).wait()
+
+    peers = [moved("x", 0, 1)]
+    for axis in ("x", "y", "z"):
+        for steps in range(1, RING):
+            for flip in range(CORES):
+                peers.append(moved(axis, steps, flip))
+    barrier = pltpu.get_barrier_semaphore()
+    for there in peers:
+        pl.semaphore_signal(
+            barrier, inc=1, device_id=coords_of(there), device_id_type=pl.DeviceIdType.MESH
+        )
+    pl.semaphore_wait(barrier, len(peers))
+
+    x, y, z = spot(place, "x"), place["y"], place["z"]
+    labels[z, y, x] = tile[...]
+    for steps in STEPS_FIRST:
+        copy(
+            labels.at[z, y, x],
+            labels.at[z, y, x],
+            label_send.at[0],
+            label_recv.at[0],
+            moved("x", steps // CORES, steps % CORES),
+        ).start()
+    for steps in STEPS_FIRST:
+        for part, (one, two, three) in enumerate(ORDERS):
+            there = moved(one, steps // CORES, steps % CORES)
+            copy(
+                sends[part].at[spot(there, one)],
+                stages[part][0].at[spot(place, one)],
+                send_sems.at[part, 0],
+                first_recv.at[part, steps],
+                there,
+            ).start()
+    arrived(labels.at[0, 0, pl.ds(0, 7)], label_recv.at[0])
+    for steps in STEPS_LATER:
+        copy(
+            labels.at[z, y], labels.at[z, y], label_send.at[1], label_recv.at[1], moved("y", steps, 0)
+        ).start()
+    arrived(labels.at[0, pl.ds(0, 3)], label_recv.at[1])
+    for steps in STEPS_LATER:
+        copy(
+            labels.at[z], labels.at[z], label_send.at[2], label_recv.at[2], moved("z", steps, 0)
+        ).start()
+
+    for steps in (0,) + STEPS_FIRST:
+        for part, (one, two, three) in enumerate(ORDERS):
+            origin = spot(moved(one, RING - steps // CORES, steps % CORES), one)
+            if steps:
+                source = stages[part][0]
+                arrived(source.at[0], first_recv.at[part, steps])
+            else:
+                source = sends[part]
+            for later in STEPS_LATER:
+                there = moved(two, later, 0)
+                copy(
+                    source.at[origin, there[two]],
+                    stages[part][1].at[place[two], origin],
+                    send_sems.at[part, 1],
+                    second_recv.at[part, later],
+                    there,
+                ).start()
+
+    def last(part, source, target, there):
+        copy(source, target, send_sems.at[part, 2], third_recv.at[part], there).start()
+
+    for part, (one, two, three) in enumerate(ORDERS):
+        for steps in (0,) + STEPS_FIRST:
+            origin = spot(moved(one, RING - steps // CORES, steps % CORES), one)
+            source = stages[part][0] if steps else sends[part]
+            for later in STEPS_LATER:
+                there = moved(three, later, 0)
+                last(
+                    part,
+                    source.at[origin, place[two], there[three]],
+                    stages[part][2].at[place[three], place[two], origin],
+                    there,
+                )
+    for steps in STEPS_LATER:
+        for part, (one, two, three) in enumerate(ORDERS):
+            origin = moved(two, RING - steps, 0)[two]
+            arrived(stages[part][1].at[0], second_recv.at[part, steps])
+            for later in STEPS_LATER:
+                there = moved(three, later, 0)
+                last(
+                    part,
+                    stages[part][1].at[origin, :, there[three]],
+                    stages[part][2].at[place[three], origin],
+                    there,
+                )
+    for part in range(parts):
+        arrived(stages[part][2].at[pl.ds(0, 3)], third_recv.at[part])
+        arrived(sends[part].at[pl.ds(0, 7)], send_sems.at[part, 0])
+        arrived(stages[part][2].at[pl.ds(0, 3)], send_sems.at[part, 1])
+        arrived(stages[part][2].at[pl.ds(0, 3)], send_sems.at[part, 2])
+    arrived(labels.at[pl.ds(0, 3)], label_recv.at[2])
+    arrived(labels.at[0, 0, pl.ds(0, 7)], label_send.at[0])
+    arrived(labels.at[0, pl.ds(0, 3)], label_send.at[1])
+    arrived(labels.at[pl.ds(0, 3)], label_send.at[2])
+
+
+def exchange(sends, tile):
+    parts = len(sends)
+    _, rows, cols = sends[0].shape
+    kind = sends[0].dtype
+    block = (rows, cols)
+    eight = RING * CORES
+    shapes = [
+        (eight, RING, RING) + block,
+        (RING, eight, RING) + block,
+        (RING, RING, eight) + block,
+    ]
+    outs = pl.pallas_call(
+        exchange_kernel,
+        out_shape=[jax.ShapeDtypeStruct(shape, kind) for shape in shapes] * parts
+        + [jax.ShapeDtypeStruct((RING, RING, eight) + tile.shape, tile.dtype)],
+        in_specs=[HBM] * parts + [VMEM],
+        out_specs=[HBM] * (3 * parts) + [VMEM],
+        scratch_shapes=[
+            pltpu.SemaphoreType.DMA((parts, eight)),
+            pltpu.SemaphoreType.DMA((parts, RING)),
+            pltpu.SemaphoreType.DMA((parts,)),
+            pltpu.SemaphoreType.DMA((parts, 3)),
+            pltpu.SemaphoreType.DMA((3,)),
+            pltpu.SemaphoreType.DMA((3,)),
+        ],
+        compiler_params=pltpu.CompilerParams(
+            collective_id=0, has_side_effects=True, vmem_limit_bytes=40 * 1024 * 1024
+        ),
+        name="exchange",
+    )(*(send.reshape((eight, RING, RING) + block) for send in sends), tile)
+    flat = [out.reshape((-1,) + block) for out in outs[: 3 * parts]]
+    groups = [
+        [sends[part]] + flat[3 * part : 3 * part + 3] for part in range(parts)
+    ]
+    return groups, outs[-1]
+
+
+def place_in_send(place, order):
+    one, two, three = (place[axis] for axis in order)
+    return ((one * CORES + place["core"]) * RING + two) * RING + three
+
+
+def place_received(origin, here, order):
+    one, two, three = ((origin[axis], here[axis]) for axis in order)
+    first = one[0] * CORES + origin["core"]
+    same_first = (one[0] == one[1]) & (origin["core"] == here["core"])
+    same_two, same_three = two[0] == two[1], three[0] == three[1]
+    early = (first * RING + two[0]) * RING + three[0]
+    middle = (two[0] * RING * CORES + first) * RING + three[0]
+    late = (three[0] * RING + two[0]) * RING * CORES + first
+    buffer = jnp.where(
+        same_three, jnp.where(same_two, jnp.where(same_first, 0, 1), 2), 3
+    )
+    at = jnp.where(buffer == 3, late, jnp.where(buffer == 2, middle, early))
+    return buffer * 128 + at
+
+
+def place_of(device):
+    row, col = device // (RING * RING), device % (RING * RING)
+    return {
+        "x": row // RING * 2 + col // CORES % 2,
+        "y": col // RING,
+        "z": row % RING,
+        "core": col % CORES,
+    }
+
+
+def collect_kernel(pieces, source, *refs):
+    groups = [refs[4 * piece : 4 * piece + 4] for piece in range(pieces)]
     buf, sems = refs[-2:]
+    outs = refs[4 * pieces : -2]
     count, rows, _ = buf.shape
-    outs = refs[:-2]
+    part = rows // pieces
     chunk = count // len(outs)
 
+    def target(at, piece):
+        return buf.at[at, pl.ds(piece * part, part)]
+
     def load(at):
-        return pltpu.make_async_copy(
-            recv.at[source[at], pl.ds(0, rows)], buf.at[at], sems.at[at]
+        for piece, group in enumerate(groups):
+            code = source[piece, at]
+            for which, ref in enumerate(group):
+
+                @pl.when(code // 128 == which)
+                def _():
+                    pltpu.make_async_copy(
+                        ref.at[code % 128], target(at, piece), sems.at[piece * count + at]
+                    ).start()
+
+    def loaded(at):
+        for piece, group in enumerate(groups):
+            pltpu.make_async_copy(
+                group[3].at[0], target(at, piece), sems.at[piece * count + at]
+            ).wait()
+
+    pl.loop(0, count)(load)
+    saves = [
+        pltpu.make_async_copy(
+            buf.at[pl.ds(part * chunk, chunk)], out, sems.at[pieces * count + part]
         )
-
-    pl.loop(0, count)(lambda at: load(at).start())
-    saves = [
-        pltpu.make_async_copy(buf.at[pl.ds(part * chunk, chunk)], out, sems.at[count + part])
         for part, out in enumerate(outs)
     ]
-    for part, save in enumerate(saves):
-        pl.loop(part * chunk, (part + 1) * chunk)(lambda at: load(at).wait())
+    for at, save in enumerate(saves):
+        pl.loop(at * chunk, (at + 1) * chunk)(loaded)
         save.start()
     for save in saves:
         save.wait()
 
 
-SMEM = pl.BlockSpec(memory_space=pltpu.SMEM)
-
-
-def pack(held, dest, devices, labels=None):
-    pieces = dest.shape[0]
-    count, rows, cols = held.shape
-    part = rows // pieces
-    marks = [] if labels is None else [labels]
+def collect(groups, source, chunks):
+    pieces = len(groups)
+    count = source.shape[1]
+    _, rows, cols = groups[0][0].shape
+    kind = groups[0][0].dtype
+    part = jax.ShapeDtypeStruct((count // chunks, pieces * rows, cols), kind)
     return pl.pallas_call(
-        functools.partial(pack_kernel, pieces),
-        out_shape=jax.ShapeDtypeStruct((devices, part + 8 * len(marks), cols), held.dtype),
-        in_specs=[SMEM, HBM] + [pl.BlockSpec(memory_space=pltpu.VMEM)] * len(marks),
-        out_specs=HBM,
-        scratch_shapes=[
-            pltpu.VMEM(held.shape, held.dtype),
-            pltpu.SemaphoreType.DMA(((1 + pieces) * count + devices,)),
-        ],
-        name="pack",
-    )(dest, held, *marks)
-
-
-def collect(recv, source, rows, chunks):
-    count, cols = source.shape[0], recv.shape[2]
-    part = jax.ShapeDtypeStruct((count // chunks, rows, cols), recv.dtype)
-    return pl.pallas_call(
-        collect_kernel,
+        functools.partial(collect_kernel, pieces),
         out_shape=[part] * chunks,
-        in_specs=[SMEM, HBM],
+        in_specs=[SMEM] + [HBM] * (4 * pieces),
         out_specs=[HBM] * chunks,
         scratch_shapes=[
-            pltpu.VMEM((count, rows, cols), recv.dtype),
-            pltpu.SemaphoreType.DMA((count + chunks,)),
+            pltpu.VMEM((count, pieces * rows, cols), kind),
+            pltpu.SemaphoreType.DMA((pieces * count + chunks,)),
         ],
         name="collect",
-    )(source, recv)
+    )(source, *(ref for group in groups for ref in group))
 
 
 def split(value):
@@ -279,13 +510,14 @@
     edge = a_held.shape[1]
     labels = jnp.concatenate([a_slot, a_col, b_slot, b_col]).astype(jnp.float32)
     tile = jnp.pad(labels, (0, 8 * edge - labels.shape[0])).reshape(8, edge)
-    send_right = pack(b_held, dest_right[None, :], devices, tile)
-    send_left = pack(a_held, dest_left, devices)
-    recv_right = lax.all_to_all(send_right, ("row", "col"), split_axis=0, concat_axis=0, tiled=True)
-    recv_right, send_left = lax.optimization_barrier((recv_right, send_left))
-    recv_left = lax.all_to_all(send_left, ("row", "col"), split_axis=0, concat_axis=0, tiled=True)
-
-    labels = recv_right[:, edge:, :].reshape(devices, -1)[:, : labels.shape[0]]
+    to_right, to_left = place_of(dest_right), place_of(dest_left)
+    spots = jnp.stack([place_in_send(to_right, order) for order in ORDERS[:2]])
+    sends = pack(b_held, spots, devices, 2)
+    sends += pack(a_held, place_in_send(to_left, ORDERS[2]), devices, 1)
+    received, labels = exchange(sends, tile)
+
+    labels = labels.reshape(RING, RING, 2, 2, CORES, -1)[..., : 2 * (hold_a + hold_b)]
+    labels = labels.transpose(2, 0, 1, 3, 4, 5).reshape(devices, -1)
     labels = labels.astype(jnp.int32)
     parts = [hold_a, 2 * hold_a, 2 * hold_a + hold_b]
     all_a, all_acol, all_b, all_bcol = (part.reshape(-1) for part in jnp.split(labels, parts, axis=1))
@@ -304,8 +536,11 @@
     src_left, col_left = look_up(i * grid_rows + k, slots_a, all_a, all_acol, hold_a)
     src_right, col_right = look_up(k * grid_cols + c, slots_b, all_b, all_bcol, hold_b)
 
-    (own,) = collect(recv_left, src_left[0], edge // copies, 1)
-    right = collect(recv_right, src_right[0], edge, CHUNKS)
+    here = place_of(i * grid_cols + c)
+    origin = place_of(src_right[0])
+    source = jnp.stack([place_received(origin, here, order) for order in ORDERS[:2]])
+    right = collect(received[:2], source, CHUNKS)
+    (own,) = collect(received[2:], place_received(place_of(src_left[0]), here, ORDERS[2])[None], 1)
     other = shifted(own, "col", grid_rows)
     cross = permuted(own, "col", lambda at: ((at - 1) ^ 1) + 1)
     mate_first = permuted(own, "col", lambda at: at ^ 1)

time: 359 us -> 335 us (0.933)
  Pallas kernels: 48.9 us -> 201 us
  waiting for transfers between devices: 236 us -> 91.5 us
  starting transfers between devices: 47.7 us -> 11.8 us
    pallas_call x4 -> x5, Pallas kernels: 22.3 us -> 173 us  [the longest x1 152 us: exchange(): pl.pallas_call(exchange_kernel, out_shape=[jax.ShapeDtypeStruct(shape, ki...]
    all_to_all x2 -> x0, waiting for transfers between devices: 140 us -> none  [the longest x1 104 us: on_device(): lax.all_to_all(send_right, ('row', 'col'), split_axis=0, concat_axis=0, t...]
    all_to_all x2 -> x0, starting transfers between devices: 24.9 us -> none  [the longest x1 14.3 us: on_device(): lax.all_to_all(send_left, ('row', 'col'), split_axis=0, concat_axis=0, ti...]
    ppermute x3, waiting for transfers between devices: 24.6 us -> 0.01 us  [permuted(): lax.ppermute(value, axis, [(at, target(at) % count) for at in range(count)])]
    ppermute x6, waiting for transfers between devices: 70.7 us -> 91.5 us  [shifted(): return lax.ppermute(value, axis, pairs)]
    ppermute x6, starting transfers between devices: 19.3 us -> 10.5 us  [shifted(): return lax.ppermute(value, axis, pairs)]
    unnamed x11 -> x14, local copies, waits for them, and re-layouts: 4.87 us -> 10.6 us
  transfers between devices with their start and end apart: 11 -> 9, of which waited for: 5 -> 5; matrix products, arithmetic and copies ran while one was open for 3% -> 3% of each run, Pallas kernels for 9% -> 7%
where the time goes in v5:
time: 335 us; the launch traced here: 333 us
  Pallas kernels  201 us (60%)
  waiting for transfers between devices  91.5 us (27%)
  local copies, waits for them, and re-layouts  15.1 us (5%)
  starting transfers between devices  11.8 us (4%)
  other arithmetic  11.1 us (3%)
    pallas_call x1, Pallas kernels, exchange(): pl.pallas_call(exchange_kernel, out_shape=[jax.ShapeDtypeStruct(shape, ki...  152 us
    ppermute x6, waiting for transfers between devices, shifted(): return lax.ppermute(value, axis, pairs)  91.5 us
    pallas_call x3, Pallas kernels, products(): pl.pallas_call(functools.partial(product_kernel, pieces, parts, first, UN...  27.9 us
    pallas_call x2, Pallas kernels, pack(): pl.pallas_call(functools.partial(pack_kernel, pieces), out_shape=[shape]...  10.7 us
    unnamed x14, local copies, waits for them, and re-layouts  10.6 us
    ppermute x6, starting transfers between devices, shifted(): return lax.ppermute(value, axis, pairs)  10.5 us
    pallas_call x2, Pallas kernels, collect(): pl.pallas_call(functools.partial(collect_kernel, pieces), out_shape=[part...  10.5 us
  transfers between devices with their start and end apart: 9, of which 5 were waited for; matrix products, arithmetic and copies ran while one was open for 3% of the time, Pallas kernels for 7%

profile of v5, /device:TPU:26, one launch (start us, length us, event | category | flops | bytes accessed | tf_op | source)
XLA Modules:
  0.0 332.6 jit_solution(11420297032514330072)
XLA Ops:
  0.0 0.7 add_bitcast_fusion.4
  0.7 0.7 fusion.30
  1.4 0.8 add_convert_fusion
  2.2 0.6 pad_add_fusion.dest
  2.8 6.8 %pack.2 = (f32[128,64,128]{2,1,0:T(8,128)}, f32[128,64,128]{2,1,0:T(8,128)}) custom-call(s32[2,64]{1,0:T(2,128)} %pad_add_fusion.dest, f32[64,128,128]{2,1,0:T(8,128)} %held.2), custom_call_target="tpu_custom_call" | custom-call | tf_op jit(solution)/shard_map/pack/pallas_call | solution.py:63
  9.6 0.7 fusion.27.dest
  10.3 3.9 %pack.3.refs_0_ = f32[128,64,128]{2,1,0:T(8,128)} custom-call(s32[2,32]{1,0:T(2,128)} %fusion.27.dest, f32[32,128,128]{2,1,0:T(8,128)} %held.3), custom_call_target="tpu_custom_call" | custom-call | tf_op jit(solution)/shard_map/pack/pallas_call | solution.py:63
  14.2 151.7 %exchange.1 = (f32[8,4,4,64,128]{4,3,2,1,0:T(8,128)S(1)}, f32[4,8,4,64,128]{4,3,2,1,0:T(8,128)S(1)}, f32[4,4,8,64,128]{4,3,2,1,0:T(8,128)S(1)}, f32[8,4,4,64,128...) custom-call(f32[8,4,4,64,128]{4,3,2,1,0:T(8,128)} %bitcast.56, ...), custom_call_target="tpu_custom_call" | custom-call | tf_op jit(solution)/shard_map/exchange/pallas_call | solution.py:240
  165.9 1.9 copy-done.1
  167.8 2.0 copy-done.2
  169.8 2.0 copy-done.3
  171.8 0.3 reshape.638
  172.6 0.5 select_reduce_fusion.1
  173.2 0.6 fusion.36.source
  173.8 4.5 %collect.2.refs_0_ = f32[64,64,128]{2,1,0:T(8,128)} custom-call(s32[1,64]{1,0:T(1,128)} %fusion.36.source, f32[128,64,128]{2,1,0:T(8,128)} %pack.3.refs_0_, f32[128,64,128]{2,1,0:T(8,128)} %bitcast.61, f32[128,64,128]{2,1,0:T(8,128)} %bitcast.62, f32[128,64,128]{2,1,0:T(8,128)} %bitcast.63), custom_call_target="tpu_custom_call" | custom-call | tf_op jit(solution)/shard_map/collect/pallas_call | solution.py:344
  178.4 2.0 collective-permute-start.1
  180.4 1.2 collective-permute-start.3
  181.9 0.9 select_reduce_fusion
  182.9 0.5 pad_add_fusion.1.source
  183.4 6.0 %collect.3 = (f32[32,128,128]{2,1,0:T(8,128)}, f32[32,128,128]{2,1,0:T(8,128)}) custom-call(s32[2,64]{1,0:T(2,128)} %pad_add_fusion.1.source, f32[128,64,128]{2,1,0:T(8,128)} %get-tuple-element.19.refs_0_, f32[128,64,128]{2,1,0:T(8,128)} %bitcast.51, f32[128,64,128]{2,1,0:T(8,128)} %bitcast.52, f32[128,64,128]{2,1,0:T(8,128)} %bitcast.53, ...), custom_call_target="tpu_custom_call" | custom-call | tf_op jit(solution)/shard_map/collect/pallas_call | solution.py:344
  189.4 1.0 collective-permute-start.7
  190.4 4.7 %collective-permute-start.8 = (f32[32,128,128]{2,1,0:T(8,128)}, f32[32,128,128]{2,1,0:T(8,128)}, u32[]{:S(2)}, u32[]{:S(2)}) collective-permute-start(f32[32,128,128]{2,1,0:T(8,128)} %get-tuple-element.32.refs_2_), channel_id=1, source_target_pairs={{0,112},{16,0},{32,16},{48,32},{64,48},{80,64},{96,80},{112,96},{1... | collective-permute-start | bytes 6291464 | tf_op jit(solution)/shard_map/ppermute | solution.py:20
  196.2 0.6 convert_reduce_fusion.1
  197.5 0.1 copy.25
  197.6 0.6 convert_reduce_fusion
  198.8 0.1 copy.29
  199.3 0.6 broadcast_add_fusion.2
  200.6 0.1 copy.27
  200.7 0.1 reshape.664
  200.8 0.1 copy.26
  200.9 0.1 reshape.656
  201.1 0.3 reduce-window.25
  201.5 0.1 reshape.655
  201.9 0.1 reshape.666
  202.0 0.1 copy.30
  202.1 0.1 reshape.660
  202.2 0.3 reduce-window.29
  202.6 0.1 reshape.659
  202.9 0.1 sub.303
  203.0 0.1 add.982
  203.2 0.1 add.974
  203.4 0.1 add.976
  203.6 0.1 add.978
  203.8 0.1 reshape.662
  203.9 0.3 reduce-window.37
  204.3 0.1 slice_reduce_fusion.2
  204.4 0.1 slice_reduce_fusion.1
  204.6 46.3 %collective-permute-done.1.refs_1_ = f32[64,64,128]{2,1,0:T(8,128)} collective-permute-done((f32[64,64,128]{2,1,0:T(8,128)}, f32[64,64,128]{2,1,0:T(8,128)}, u32[]{:S(2)}, u32[]{:S(2)}) %collective-permute-start.1) | collective-permute-done | bytes 2097184 | tf_op jit(solution)/shard_map/ppermute | solution.py:20
  250.9 1.7 collective-permute-start.4
  252.7 0.1 slice_reduce_fusion
  252.8 1.0 collective-permute-start.5
  253.8 22.1 %collective-permute-done.7.refs_4_ = f32[32,128,128]{2,1,0:T(8,128)} collective-permute-done((f32[32,128,128]{2,1,0:T(8,128)}, f32[32,128,128]{2,1,0:T(8,128)}, u32[]{:S(2)}, u32[]{:S(2)}) %collective-permute-start.7) | collective-permute-done | bytes 2097184 | tf_op jit(solution)/shard_map/ppermute | solution.py:20
  275.9 0.1 select_reduce_fusion.4
  276.1 0.3 select_reduce_fusion.3
  276.5 0.3 select_reduce_fusion.2
  276.8 1.6 copy-done
  278.4 1.6 copy-done.4
  280.0 1.6 copy-done.5
  281.6 7.7 %products.3.refs_6_ = f32[96,128,128]{2,1,0:T(8,128)} custom-call(s32[1]{0:T(128)} %bitcast.27.counts, s32[256]{0:T(256)S(1)} %broadcast_add_fusion.6.items, s32[1]{0:T(128)S(1)} %bitcast.54, f32[64,64,128]{2,1,0:T(8,128)S(1)} %copy-done, f32[64,64,128]{2,1,0:T(8,128)} %collective-permute-done.1.refs_1_, f32[32,128,128]{2,1,0:T(8,128)S(1)} %copy-done.5, ...), custom_call_target="tpu_custom_call" | custom-call | flops 600000000 | bytes 8000000 | tf_op jit(solution)/shard_map/products/pallas_call | solution.py:444
  289.4 11.3 %collective-permute-done.4.refs_3_ = f32[64,64,128]{2,1,0:T(8,128)S(1)} collective-permute-done((f32[64,64,128]{2,1,0:T(8,128)}, f32[64,64,128]{2,1,0:T(8,128)S(1)}, u32[]{:S(2)}, u32[]{:S(2)}) %collective-permute-start.4) | collective-permute-done | bytes 2097184 | tf_op jit(solution)/shard_map/ppermute | solution.py:20
  300.7 11.1 %products.4.refs_6_ = f32[96,128,128]{2,1,0:T(8,128)} custom-call(s32[1]{0:T(128)} %bitcast.24.counts, s32[512]{0:T(512)S(1)} %broadcast_add_fusion.4.items, s32[2]{0:T(128)S(1)} %slice.59.order, f32[64,64,128]{2,1,0:T(8,128)S(1)} %collective-permute-done.refs_0_, f32[64,64,128]{2,1,0:T(8,128)S(1)} %collective-permute-done.2.refs_1_, ...), custom_call_target="tpu_custom_call" | custom-call | flops 1200000000 | bytes 16000000 | tf_op jit(solution)/shard_map/products/pallas_call | solution.py:444
  311.7 8.9 %collective-permute-done.5.refs_4_ = f32[32,128,128]{2,1,0:T(8,128)S(1)} collective-permute-done((f32[32,128,128]{2,1,0:T(8,128)}, f32[32,128,128]{2,1,0:T(8,128)S(1)}, u32[]{:S(2)}, u32[]{:S(2)}) %collective-permute-start.5) | collective-permute-done | bytes 2097184 | tf_op jit(solution)/shard_map/ppermute | solution.py:20
  320.6 2.9 collective-permute-done.6.refs_5_
  323.5 9.1 %products.5 = f32[96,128,128]{2,1,0:T(8,128)} custom-call(s32[1]{0:T(128)} %bitcast.9.counts, s32[512]{0:T(512)S(1)} %broadcast_add_fusion.5.items, s32[2]{0:T(128)S(1)} %slice.59.order, f32[64,64,128]{2,1,0:T(8,128)S(1)} %collective-permute-done.refs_0_, f32[64,64,128]{2,1,0:T(8,128)S(1)} %collective-permute-done.2.refs_1_, ...), custom_call_target="tpu_custom_call" | custom-call | flops 1200000000 | bytes 16000000 | tf_op jit(solution)/shard_map/products/pallas_call | solution.py:444
  (95 shorter events, 3.8 us)
Async XLA Ops:
  165.9 1.9 copy-start.1
  167.8 2.0 copy-start.2
  169.8 2.0 copy-start.3
  178.3 74.5 %collective-permute-start = (f32[64,64,128]{2,1,0:T(8,128)}, f32[64,64,128]{2,1,0:T(8,128)S(1)}, u32[]{:S(2)}, u32[]{:S(2)}) collective-permute-start(f32[64,64,128]{2,1,0:T(8,128)} %collect.2.refs_0_), channel_id=1, source_target_pairs={{0,1},{1,0},{2,3},{3,2},{4,5},{5,4},{6,7},{7,6},{8,9},{9,8},{10,11... | collective-permute-start | bytes 6291464 | tf_op jit(solution)/shard_map/ppermute | solution.py:25
  178.4 72.6 %collective-permute-start.1 = (f32[64,64,128]{2,1,0:T(8,128)}, f32[64,64,128]{2,1,0:T(8,128)}, u32[]{:S(2)}, u32[]{:S(2)}) collective-permute-start(f32[64,64,128]{2,1,0:T(8,128)} %collect.2.refs_0_), channel_id=1, source_target_pairs={{0,8},{1,9},{2,10},{3,11},{4,12},{5,13},{6,14},{7,15},{8,0},{9,1},... | collective-permute-start | bytes 6291464 | tf_op jit(solution)/shard_map/ppermute | solution.py:20
  180.4 70.5 %collective-permute-start.3 = (f32[64,64,128]{2,1,0:T(8,128)}, f32[64,64,128]{2,1,0:T(8,128)}, u32[]{:S(2)}, u32[]{:S(2)}) collective-permute-start(f32[64,64,128]{2,1,0:T(8,128)} %collect.2.refs_0_), channel_id=1, source_target_pairs={{0,15},{1,2},{2,1},{3,4},{4,3},{5,6},{6,5},{7,8},{8,7},{9,10},{10,... | collective-permute-start | bytes 6291464 | tf_op jit(solution)/shard_map/ppermute | solution.py:25
  183.4 12.4 %copy-start.6 = (s32[16,6]{0,1:T(8,128)S(1)}, s32[16,6]{0,1:T(8,128)}, u32[]{:S(2)}) copy-start(s32[16,6]{0,1:T(8,128)} %param.13) | copy-start | bytes 1156
  189.4 86.5 %collective-permute-start.7 = (f32[32,128,128]{2,1,0:T(8,128)}, f32[32,128,128]{2,1,0:T(8,128)}, u32[]{:S(2)}, u32[]{:S(2)}) collective-permute-start(f32[32,128,128]{2,1,0:T(8,128)} %get-tuple-element.32.refs_2_), channel_id=1, source_target_pairs={{0,16},{16,32},{32,48},{48,64},{64,80},{80,96},{96,112},{112,0},{1... | collective-permute-start | bytes 6291464 | tf_op jit(solution)/shard_map/ppermute | solution.py:20
  190.4 98.9 %collective-permute-start.8 = (f32[32,128,128]{2,1,0:T(8,128)}, f32[32,128,128]{2,1,0:T(8,128)}, u32[]{:S(2)}, u32[]{:S(2)}) collective-permute-start(f32[32,128,128]{2,1,0:T(8,128)} %get-tuple-element.32.refs_2_), channel_id=1, source_target_pairs={{0,112},{16,0},{32,16},{48,32},{64,48},{80,64},{96,80},{112,96},{1... | collective-permute-start | bytes 6291464 | tf_op jit(solution)/shard_map/ppermute | solution.py:20
  250.9 38.4 %collective-permute-start.2 = (f32[64,64,128]{2,1,0:T(8,128)}, f32[64,64,128]{2,1,0:T(8,128)S(1)}, u32[]{:S(2)}, u32[]{:S(2)}) collective-permute-start(f32[64,64,128]{2,1,0:T(8,128)} %collective-permute-done.1.refs_1_), channel_id=1, source_target_pairs={{0,1},{1,0},{2,3},{3,2},{4,5},{5,4},{6,7},{7,6},{8,9},{9,8},{10,11... | collective-permute-start | bytes 6291464 | tf_op jit(solution)/shard_map/ppermute | solution.py:25
  250.9 49.8 %collective-permute-start.4 = (f32[64,64,128]{2,1,0:T(8,128)}, f32[64,64,128]{2,1,0:T(8,128)S(1)}, u32[]{:S(2)}, u32[]{:S(2)}) collective-permute-start(f32[64,64,128]{2,1,0:T(8,128)} %collective-permute-done.3.refs_2_), channel_id=1, source_target_pairs={{0,8},{1,9},{2,10},{3,11},{4,12},{5,13},{6,14},{7,15},{8,0},{9,1},... | collective-permute-start | bytes 6291464 | tf_op jit(solution)/shard_map/ppermute | solution.py:20
  252.8 67.8 %collective-permute-start.5 = (f32[32,128,128]{2,1,0:T(8,128)}, f32[32,128,128]{2,1,0:T(8,128)S(1)}, u32[]{:S(2)}, u32[]{:S(2)}) collective-permute-start(f32[32,128,128]{2,1,0:T(8,128)} %get-tuple-element.31.refs_3_), channel_id=1, source_target_pairs={{0,16},{16,32},{32,48},{48,64},{64,80},{80,96},{96,112},{112,0},{1... | collective-permute-start | bytes 6291464 | tf_op jit(solution)/shard_map/ppermute | solution.py:20
  275.9 47.6 %collective-permute-start.6 = (f32[32,128,128]{2,1,0:T(8,128)}, f32[32,128,128]{2,1,0:T(8,128)S(1)}, u32[]{:S(2)}, u32[]{:S(2)}) collective-permute-start(f32[32,128,128]{2,1,0:T(8,128)} %get-tuple-element.31.refs_3_), channel_id=1, source_target_pairs={{0,112},{16,0},{32,16},{48,32},{64,48},{80,64},{96,80},{112,96},{1... | collective-permute-start | bytes 6291464 | tf_op jit(solution)/shard_map/ppermute | solution.py:20
  276.8 1.6 copy-start
  278.4 1.6 copy-start.4
  280.0 1.6 copy-start.5

commit v6 on v5

--- a/solution.py
+++ b/solution.py
@@ -11,18 +11,7 @@
 WA = 4
 WB = 4
 STEPS = 3
-HBM = pl.BlockSpec(memory_space=pl.ANY)
-
-
-def shifted(value, axis, steps):
-    count = lax.axis_size(axis)
-    pairs = [(source, (source + steps) % count) for source in range(count)]
-    return lax.ppermute(value, axis, pairs)
-
-
-def permuted(value, axis, target):
-    count = lax.axis_size(axis)
-    return lax.ppermute(value, axis, [(at, target(at) % count) for at in range(count)])
+HBM = pl.BlockSpec(memory_space=pltpu.HBM)
 
 
 def pack_kernel(pieces, dest, held, *refs):
@@ -52,6 +41,7 @@
         pl.loop(0, count)(lambda at: save(at, piece).wait())
 
 
+GRANT = 60 * 1024 * 1024
 SMEM = pl.BlockSpec(memory_space=pltpu.SMEM)
 VMEM = pl.BlockSpec(memory_space=pltpu.VMEM)
 
@@ -69,6 +59,7 @@
             pltpu.VMEM(held.shape, held.dtype),
             pltpu.SemaphoreType.DMA(((1 + pieces) * count,)),
         ],
+        compiler_params=pltpu.CompilerParams(vmem_limit_bytes=GRANT),
         name="pack",
     )(dest, held)
 
@@ -252,7 +243,7 @@
             pltpu.SemaphoreType.DMA((3,)),
         ],
         compiler_params=pltpu.CompilerParams(
-            collective_id=0, has_side_effects=True, vmem_limit_bytes=40 * 1024 * 1024
+            collective_id=0, has_side_effects=True, vmem_limit_bytes=GRANT
         ),
         name="exchange",
     )(*(send.reshape((eight, RING, RING) + block) for send in sends), tile)
@@ -293,21 +284,21 @@
     }
 
 
-def collect_kernel(pieces, source, *refs):
-    groups = [refs[4 * piece : 4 * piece + 4] for piece in range(pieces)]
-    buf, sems = refs[-2:]
-    outs = refs[4 * pieces : -2]
-    count, rows, _ = buf.shape
-    part = rows // pieces
-    chunk = count // len(outs)
+def collect_kernel(source, lefts, rights, kept, *refs):
+    groups = [refs[4 * piece : 4 * piece + 4] for piece in range(3)]
+    right_out, left_out, items, counts, right_buf, left_buf, sems = refs[12:]
+    count = right_buf.shape[0]
+    part = left_buf.shape[1]
 
     def target(at, piece):
-        return buf.at[at, pl.ds(piece * part, part)]
-
-    def load(at):
-        for piece, group in enumerate(groups):
-            code = source[piece, at]
-            for which, ref in enumerate(group):
+        if piece == 2:
+            return left_buf.at[at]
+        return right_buf.at[at, pl.ds(piece * part, part)]
+
+    def load(piece):
+        def body(at):
+            code = source[piece * count + at]
+            for which, ref in enumerate(groups[piece]):
 
                 @pl.when(code // 128 == which)
                 def _():
@@ -315,43 +306,235 @@
                         ref.at[code % 128], target(at, piece), sems.at[piece * count + at]
                     ).start()
 
-    def loaded(at):
-        for piece, group in enumerate(groups):
+        pl.loop(0, count)(body)
+
+    def loaded(piece):
+        def body(at):
             pltpu.make_async_copy(
-                group[3].at[0], target(at, piece), sems.at[piece * count + at]
+                groups[piece][3].at[0], target(at, piece), sems.at[piece * count + at]
             ).wait()
 
-    pl.loop(0, count)(load)
-    saves = [
-        pltpu.make_async_copy(
-            buf.at[pl.ds(part * chunk, chunk)], out, sems.at[pieces * count + part]
-        )
-        for part, out in enumerate(outs)
-    ]
-    for at, save in enumerate(saves):
-        pl.loop(at * chunk, (at + 1) * chunk)(loaded)
-        save.start()
-    for save in saves:
-        save.wait()
-
-
-def collect(groups, source, chunks):
-    pieces = len(groups)
-    count = source.shape[1]
+        pl.loop(0, count)(body)
+
+    for piece in (2, 0, 1):
+        load(piece)
+    for step in range(STEPS):
+
+        def body(slot, found):
+            column = lefts[step * count + slot]
+            inner = jnp.maximum(column, 0)
+            for way in range(WB):
+                other = rights[step * count + inner * WB + way]
+                out = kept[slot // WA * (KPB + 1) + other + 1]
+                items[step, found] = slot * 16384 + (inner * WB + way) * 128 + jnp.maximum(out, 0)
+                found += ((column >= 0) & (out >= 0)).astype(jnp.int32)
+            return found
+
+        found = lax.fori_loop(0, count, body, jnp.int32(0))
+        for lane in range(UNROLL):
+            items[step, found + lane] = SPARE
+        counts[step] = (found + UNROLL - 1) // UNROLL
+    loaded(2)
+    save_left = pltpu.make_async_copy(left_buf, left_out, sems.at[3 * count])
+    save_left.start()
+    loaded(0)
+    loaded(1)
+    save_right = pltpu.make_async_copy(right_buf, right_out, sems.at[3 * count + 1])
+    save_right.start()
+    save_left.wait()
+    save_right.wait()
+
+
+def collect(groups, source, lefts, rights, kept):
+    count = source.shape[0] // 3
     _, rows, cols = groups[0][0].shape
     kind = groups[0][0].dtype
-    part = jax.ShapeDtypeStruct((count // chunks, pieces * rows, cols), kind)
+    right, left = (count, 2 * rows, cols), (count, rows, cols)
     return pl.pallas_call(
-        functools.partial(collect_kernel, pieces),
-        out_shape=[part] * chunks,
-        in_specs=[SMEM] + [HBM] * (4 * pieces),
-        out_specs=[HBM] * chunks,
+        collect_kernel,
+        out_shape=[
+            jax.ShapeDtypeStruct(right, kind),
+            jax.ShapeDtypeStruct(left, kind),
+            jax.ShapeDtypeStruct((STEPS, count * WB + UNROLL), jnp.int32),
+            jax.ShapeDtypeStruct((STEPS,), jnp.int32),
+        ],
+        in_specs=[SMEM] * 4 + [HBM] * 12,
+        out_specs=[HBM, HBM, SMEM, SMEM],
         scratch_shapes=[
-            pltpu.VMEM((count, pieces * rows, cols), kind),
-            pltpu.SemaphoreType.DMA((pieces * count + chunks,)),
+            pltpu.VMEM(right, kind),
+            pltpu.VMEM(left, kind),
+            pltpu.SemaphoreType.DMA((3 * count + 2,)),
         ],
+        compiler_params=pltpu.CompilerParams(vmem_limit_bytes=GRANT),
         name="collect",
-    )(source, *(ref for group in groups for ref in group))
+    )(source, lefts, rights, kept, *(ref for group in groups for ref in group))
+
+
+RIGHT_CHUNKS = 8
+RELAYED = 3
+LEFT_CHUNKS = 4
+
+
+def spread_kernel(own, right, other, mate_one, mate_two, cross_one, cross_two, before, after, *sems):
+    send_sems, before_sems, after_sems, other_sems, cross_sems, late_sems = sems
+    row, col = lax.axis_index("row"), lax.axis_index("col")
+    rows, cols = lax.axis_size("row"), lax.axis_size("col")
+    half = row % RING
+    up, down = ((row + 1) % rows, col), ((row + rows - 1) % rows, col)
+    up_two, down_two = ((row + 2) % rows, col), ((row + rows - 2) % rows, col)
+    twin = (row, (col + cols // 2) % cols)
+    mate = (row, col + 1 - 2 * (col % 2))
+    cross = (row, (col + cols - 1 + 2 * (col % 2)) % cols)
+
+    barrier = pltpu.get_barrier_semaphore()
+    peers = (up, down, up_two, down_two, twin, mate, cross)
+    for there in peers:
+        pl.semaphore_signal(
+            barrier, inc=1, device_id=there, device_id_type=pl.DeviceIdType.MESH
+        )
+    pl.semaphore_wait(barrier, len(peers))
+
+    right_size = right.shape[0] // RIGHT_CHUNKS
+    left_size = own.shape[0] // LEFT_CHUNKS
+
+    def cut(ref, at, size):
+        return ref.at[pl.ds(at * size, size)]
+
+    def send(source, target, at, size, send_sem, recv_sem, there):
+        return pltpu.make_async_remote_copy(
+            src_ref=cut(source, at, size),
+            dst_ref=cut(target, at, size),
+            send_sem=send_sem,
+            recv_sem=recv_sem,
+            device_id=there,
+            device_id_type=pl.DeviceIdType.MESH,
+        )
+
+    def raise_chunk(at):
+        return send(right, before, at, right_size, send_sems.at[0, at], before_sems.at[at], up)
+
+    def lower_chunk(at):
+        return send(right, after, at, right_size, send_sems.at[1, at], after_sems.at[at], down)
+
+    def relay_up(at):
+        return send(after, before, at, right_size, send_sems.at[2, at], before_sems.at[at], up_two)
+
+    def relay_down(at):
+        return send(before, after, at, right_size, send_sems.at[2, at], after_sems.at[at], down_two)
+
+    def to_twin(at):
+        return send(own, other, at, left_size, send_sems.at[3, at], other_sems.at[at], twin)
+
+    def to_cross(at):
+        return send(own, cross_one, at, left_size, send_sems.at[4, at], cross_sems.at[at], cross)
+
+    def to_mate(at):
+        return send(own, mate_one, at, left_size, send_sems.at[5, at], late_sems.at[0, at], mate)
+
+    def pass_mate(at):
+        return send(other, mate_two, at, left_size, send_sems.at[6, at], late_sems.at[1, at], mate)
+
+    def pass_twin(at):
+        return send(
+            cross_one, cross_two, at, left_size, send_sems.at[7, at], late_sems.at[2, at], twin
+        )
+
+    last = half == RING - 1
+    first = half == 0
+    for at in range(RELAYED):
+
+        @pl.when(jnp.logical_not(last))
+        def _():
+            raise_chunk(at).start()
+
+        @pl.when(jnp.logical_not(first))
+        def _():
+            lower_chunk(at).start()
+
+    for at in range(LEFT_CHUNKS):
+        to_cross(at).start()
+        to_twin(at).start()
+        to_mate(at).start()
+    for at in range(RELAYED, RIGHT_CHUNKS):
+        raise_chunk(at).start()
+        lower_chunk(at).start()
+    for at in range(RELAYED):
+
+        @pl.when(half == RING - 2)
+        def _():
+            lower_chunk(at).wait_recv()
+            relay_up(at).start()
+
+        @pl.when(half == 1)
+        def _():
+            raise_chunk(at).wait_recv()
+            relay_down(at).start()
+
+    for at in range(LEFT_CHUNKS):
+        to_cross(at).wait_recv()
+        pass_twin(at).start()
+        to_twin(at).wait_recv()
+        pass_mate(at).start()
+
+    for at in range(RELAYED):
+
+        @pl.when(half != 1)
+        def _():
+            raise_chunk(at).wait_recv()
+
+        @pl.when(half != RING - 2)
+        def _():
+            lower_chunk(at).wait_recv()
+
+        @pl.when(jnp.logical_not(last))
+        def _():
+            raise_chunk(at).wait_send()
+
+        @pl.when(jnp.logical_not(first))
+        def _():
+            lower_chunk(at).wait_send()
+
+        @pl.when(half == RING - 2)
+        def _():
+            relay_up(at).wait_send()
+
+        @pl.when(half == 1)
+        def _():
+            relay_down(at).wait_send()
+
+    for at in range(RELAYED, RIGHT_CHUNKS):
+        raise_chunk(at).wait()
+        lower_chunk(at).wait()
+    for at in range(LEFT_CHUNKS):
+        to_mate(at).wait()
+        pass_mate(at).wait()
+        pass_twin(at).wait()
+        to_twin(at).wait_send()
+        to_cross(at).wait_send()
+
+
+def spread(own, right):
+    left_shape = jax.ShapeDtypeStruct(own.shape, own.dtype)
+    right_shape = jax.ShapeDtypeStruct(right.shape, right.dtype)
+    dma = pltpu.SemaphoreType.DMA
+    return pl.pallas_call(
+        spread_kernel,
+        out_shape=[left_shape] * 5 + [right_shape] * 2,
+        in_specs=[HBM] * 2,
+        out_specs=[HBM] * 7,
+        scratch_shapes=[
+            dma((8, RIGHT_CHUNKS)),
+            dma((RIGHT_CHUNKS,)),
+            dma((RIGHT_CHUNKS,)),
+            dma((LEFT_CHUNKS,)),
+            dma((LEFT_CHUNKS,)),
+            dma((3, LEFT_CHUNKS)),
+        ],
+        compiler_params=pltpu.CompilerParams(
+            collective_id=1, has_side_effects=True, vmem_limit_bytes=GRANT
+        ),
+        name="spread",
+    )(own, right)
 
 
 def split(value):
@@ -360,132 +543,95 @@
     return high, low
 
 
-def product_kernel(pieces, parts, first, unroll, counts, items, order, *refs):
-    lefts = refs[: 2 * pieces]
-    rights = refs[2 * pieces : 2 * pieces + parts]
-    refs = refs[2 * pieces + parts :]
-    if not first:
-        before, refs = refs[0], refs[1:]
-    out, left_buf, right_buf, total, load_sems, out_sem = refs
+UNROLL = 8
+SPARE = 96
+
+
+def product_kernel(counts, items, order, places, *refs):
+    lefts = refs[: 2 * STEPS]
+    right, before, after, out, left_buf, right_buf, total, load_sems, out_sem = refs[2 * STEPS :]
     outs, edge, _ = out.shape
-    slots_a = lefts[0].shape[0]
-    slots_b = rights[0].shape[0]
-
-    loads = [
+
+    def right_load(step, source):
+        return pltpu.make_async_copy(source, right_buf.at[step], load_sems.at[2 * STEPS + step])
+
+    left_loads = [
         pltpu.make_async_copy(source, left_buf.at[at], load_sems.at[at])
         for at, source in enumerate(lefts)
-    ] + [
-        pltpu.make_async_copy(
-            source, right_buf.at[pl.ds(at * slots_b, slots_b)], load_sems.at[2 * pieces + at]
-        )
-        for at, source in enumerate(rights)
     ]
-    if not first:
-        restore = pltpu.make_async_copy(before, total.at[pl.ds(0, outs)], out_sem)
-        restore.start()
-    for load in loads:
-        load.start()
-    if first:
-
-        def clear(at):
-            total[at] = jnp.zeros((edge, edge), jnp.float32)
-
-        pl.loop(0, outs)(clear)
-    else:
-        restore.wait()
-    for load in loads:
-        load.wait()
-
-    def step(at):
-        codes = [items[at * unroll + lane] for lane in range(unroll)]
-        sums = []
-        for code in codes:
-            slot_a = code // 16384
-            slot_b = (code // 128) % 128
-            piece = slot_a // slots_a
-            swap = order[piece]
-            slot_a = slot_a % slots_a
-            left = jnp.concatenate(
-                [
-                    left_buf[2 * piece + swap, slot_a],
-                    left_buf[2 * piece + 1 - swap, slot_a],
-                ],
-                axis=0,
-            )
-            a_hi, a_lo = split(left)
-            b_hi, b_lo = split(right_buf[slot_b])
-            sums.append(
-                jnp.dot(
-                    jnp.concatenate([a_hi, a_lo], axis=1),
-                    jnp.concatenate([b_hi, b_hi], axis=0),
-                    preferred_element_type=jnp.float32,
+    for step in range(STEPS):
+        left_loads[2 * step].start()
+        left_loads[2 * step + 1].start()
+        if step == 0:
+            right_load(0, right).start()
+        else:
+            for place, source in enumerate((before, after)):
+
+                @pl.when(places[step - 1] == place)
+                def _():
+                    right_load(step, source).start()
+
+    def clear(at):
+        total[at] = jnp.zeros((edge, edge), jnp.float32)
+
+    pl.loop(0, outs + 1)(clear)
+
+    for step in range(STEPS):
+        left_loads[2 * step].wait()
+        left_loads[2 * step + 1].wait()
+        right_load(step, right).wait()
+        swap = order[step]
+
+        def body(at):
+            codes = [items[step, at * UNROLL + lane] for lane in range(UNROLL)]
+            sums = []
+            for code in codes:
+                slot_a = lax.shift_right_logical(code, 14)
+                slot_b = lax.shift_right_logical(code, 7) & 127
+                left = jnp.concatenate(
+                    [
+                        left_buf[2 * step + swap, slot_a],
+                        left_buf[2 * step + 1 - swap, slot_a],
+                    ],
+                    axis=0,
                 )
-                + jnp.dot(a_hi, b_lo, preferred_element_type=jnp.float32)
-            )
-        for code, value in zip(codes, sums):
-            total[code % 128] += value
-
-    pl.loop(0, counts[0])(step)
+                a_hi, a_lo = split(left)
+                b_hi, b_lo = split(right_buf[step, slot_b])
+                sums.append(
+                    jnp.dot(
+                        jnp.concatenate([a_hi, a_lo], axis=1),
+                        jnp.concatenate([b_hi, b_hi], axis=0),
+                        preferred_element_type=jnp.float32,
+                    )
+                    + jnp.dot(a_hi, b_lo, preferred_element_type=jnp.float32)
+                )
+            for code, value in zip(codes, sums):
+                total[code & 127] += value
+
+        pl.loop(0, counts[step])(body)
     save = pltpu.make_async_copy(total.at[pl.ds(0, outs)], out, out_sem)
     save.start()
     save.wait()
 
 
-UNROLL = 8
-CHUNKS = 2
-
-
-def products(counts, items, order, halves, rights, before, outs):
-    pieces, parts = len(halves) // 2, len(rights)
+def products(counts, items, order, places, lefts, rights, outs):
     slots_b, edge, _ = rights[0].shape
-    slots_a, part, _ = halves[0].shape
-    first = before is None
-    extra = [] if first else [before]
+    slots_a, part, _ = lefts[0].shape
     return pl.pallas_call(
-        functools.partial(product_kernel, pieces, parts, first, UNROLL),
+        product_kernel,
         out_shape=jax.ShapeDtypeStruct((outs, edge, edge), jnp.float32),
-        in_specs=[SMEM] * 3 + [HBM] * (2 * pieces + parts + len(extra)),
+        in_specs=[SMEM] * 4 + [HBM] * (len(lefts) + len(rights)),
         out_specs=HBM,
         scratch_shapes=[
-            pltpu.VMEM((2 * pieces, slots_a, part, edge), jnp.float32),
-            pltpu.VMEM((parts * slots_b, edge, edge), jnp.float32),
+            pltpu.VMEM((2 * STEPS, slots_a, part, edge), jnp.float32),
+            pltpu.VMEM((STEPS, slots_b, edge, edge), jnp.float32),
             pltpu.VMEM((outs + 1, edge, edge), jnp.float32),
-            pltpu.SemaphoreType.DMA((2 * pieces + parts,)),
+            pltpu.SemaphoreType.DMA((3 * STEPS,)),
             pltpu.SemaphoreType.DMA,
         ],
-        compiler_params=pltpu.CompilerParams(vmem_limit_bytes=40 * 1024 * 1024),
-        cost_estimate=pl.CostEstimate(
-            flops=pieces * 600_000_000, bytes_accessed=pieces * 8_000_000, transcendentals=0
-        ),
+        compiler_params=pltpu.CompilerParams(vmem_limit_bytes=GRANT),
         name="products",
-    )(counts, items, order, *halves, *rights, *extra)
-
-
-def work_list(lefts, rights, places, kept, first_row):
-    rows, width = kept.shape
-    pieces, inner, _ = rights.shape
-    outs = rows * width
-    slots = rows * WA
-    rel = lefts - first_row
-    here = rel[:, :, None] == jnp.arange(inner, dtype=jnp.int32)
-    chosen = (
-        jnp.sum(jnp.where(here[:, :, :, None], rights[:, None, :, :] + 1, 0), axis=2) - 1
-    )
-    at_row = jnp.repeat(kept, WA, axis=0)
-    match = (chosen[:, :, :, None] == at_row[None, :, None, :]) & (chosen >= 0)[:, :, :, None]
-    target = jnp.sum(jnp.where(match, jnp.arange(width, dtype=jnp.int32) + 1, 0), axis=3) - 1
-    live = target >= 0
-    slot = jnp.arange(slots, dtype=jnp.int32)[None, :, None]
-    slot_a = slot + slots * jnp.arange(pieces, dtype=jnp.int32)[:, None, None]
-    slot_b = (places[:, None, None] * inner + rel[:, :, None]) * WB + jnp.arange(WB, dtype=jnp.int32)
-    code = slot_a * 16384 + slot_b * 128 + slot // WA * width + target
-    live, code = live.reshape(-1), code.reshape(-1)
-    spot = jnp.cumsum(live.astype(jnp.int32)) - 1
-    place = jnp.arange(live.shape[0], dtype=jnp.int32)
-    here = live[None, :] & (spot[None, :] == place[:, None])
-    packed = jnp.sum(jnp.where(here, code[None, :] - outs, 0), axis=1) + outs
-    count = (jnp.sum(live.astype(jnp.int32)) + UNROLL - 1) // UNROLL
-    return count[None], packed
+    )(counts, items, order, places, *lefts, *rights)
 
 
 def on_device(a_held, a_slot, a_col, b_held, b_slot, b_col, c_col):
@@ -538,29 +684,26 @@
 
     here = place_of(i * grid_cols + c)
     origin = place_of(src_right[0])
-    source = jnp.stack([place_received(origin, here, order) for order in ORDERS[:2]])
-    right = collect(received[:2], source, CHUNKS)
-    (own,) = collect(received[2:], place_received(place_of(src_left[0]), here, ORDERS[2])[None], 1)
-    other = shifted(own, "col", grid_rows)
-    cross = permuted(own, "col", lambda at: ((at - 1) ^ 1) + 1)
-    mate_first = permuted(own, "col", lambda at: at ^ 1)
-    mate_second = permuted(other, "col", lambda at: at ^ 1)
-    cross_second = shifted(cross, "col", grid_rows)
+    source = [place_received(origin, here, order) for order in ORDERS[:2]]
+    source.append(place_received(place_of(src_left[0]), here, ORDERS[2]))
+    hit = c_col[:, :, None] == jnp.arange(-1, KPB, dtype=jnp.int32)
+    hit &= (c_col >= 0)[:, :, None]
+    outs = jnp.arange(rows * width, dtype=jnp.int32).reshape(rows, width, 1)
+    kept = jnp.sum(jnp.where(hit, outs + 1, 0), axis=1) - 1
+    right, own, items, counts = collect(
+        received,
+        jnp.concatenate(source),
+        col_left.reshape(-1),
+        col_right.reshape(-1),
+        kept.reshape(-1),
+    )
+    other, mate_one, mate_two, cross_one, cross_two, before, after = spread(own, right)
+
     homes = (c + jnp.stack([jnp.int32(0), -side, side])) % grid_cols
     order = (homes >= grid_rows).astype(jnp.int32)
-
-    outs = rows * width
-    tables = col_right.reshape(STEPS, KPB, WB)
-    count, items = work_list(col_left[:1], tables[:1], jnp.zeros((1,), jnp.int32), c_col, 0)
-    total = products(count, items, order[:1], [own, other], right, None, outs)
     places = jnp.stack([(1 - side) // 2, (1 + side) // 2])
-    lefts = [mate_first, mate_second, cross, cross_second]
-    chunk = slots_b // CHUNKS
-    for at in range(CHUNKS):
-        shifts = [shifted(right[at], "row", 1), shifted(right[at], "row", -1)]
-        first, last = at * chunk // WB, (at + 1) * chunk // WB
-        count, items = work_list(col_left[1:], tables[1:, first:last], places, c_col, first)
-        total = products(count, items, order[1:], lefts, shifts, total, outs)
+    lefts = [own, other, mate_one, mate_two, cross_one, cross_two]
+    total = products(counts, items, order, places, lefts, [right, before, after], rows * width)
     return total.reshape(rows, width, edge, edge)
 
 

time: 335 us -> 350 us (1.045)
  Pallas kernels: 201 us -> 335 us
  waiting for transfers between devices: 91.5 us -> 0 us
  local copies, waits for them, and re-layouts: 15.1 us -> 3.26 us
  starting transfers between devices: 11.8 us -> 0 us
    pallas_call x5 -> x3, Pallas kernels: 38.4 us -> 172 us  [the longest x1 141 us: spread(): pl.pallas_call(spread_kernel, out_shape=[left_shape] * 5 + [right_shape]...]
    ppermute x9 -> x0, waiting for transfers between devices: 91.5 us -> none  [the longest x6 91.5 us: shifted(): return lax.ppermute(value, axis, pairs)]
    ppermute x9 -> x0, starting transfers between devices: 11.8 us -> none  [the longest x6 10.5 us: shifted(): return lax.ppermute(value, axis, pairs)]
    unnamed x14 -> x0, local copies, waits for them, and re-layouts: 10.6 us -> none
  transfers between devices with their start and end apart: 9 -> 0, of which waited for: 5 -> 0; matrix products, arithmetic and copies ran while one was open for 3% -> 0% of each run, Pallas kernels for 7% -> 0%
where the time goes in v6:
time: 350 us; the launch traced here: 348 us
  Pallas kernels  335 us (96%)
  other arithmetic  9.25 us (3%)
    pallas_call x1, Pallas kernels, exchange(): pl.pallas_call(exchange_kernel, out_shape=[jax.ShapeDtypeStruct(shape, ki...  153 us
    pallas_call x1, Pallas kernels, spread(): pl.pallas_call(spread_kernel, out_shape=[left_shape] * 5 + [right_shape]...  141 us
    pallas_call x1, Pallas kernels, collect(): pl.pallas_call(collect_kernel, out_shape=[jax.ShapeDtypeStruct(right, kin...  16 us
    pallas_call x1, Pallas kernels, products(): pl.pallas_call(product_kernel, out_shape=jax.ShapeDtypeStruct((outs, edge...  14.4 us
    pallas_call x2, Pallas kernels, pack(): pl.pallas_call(functools.partial(pack_kernel, pieces), out_shape=[shape]...  10.8 us

profile of v6, /device:TPU:26, one launch (start us, length us, event | category | flops | bytes accessed | tf_op | source)
XLA Modules:
  0.0 348.1 jit_solution(1871042868187655867)
XLA Ops:
  0.0 0.6 pad_add_fusion.2.places
  0.6 0.1 add_multiply_fusion.1
  0.7 0.7 compare_convert_fusion.order
  1.4 0.7 fusion.29
  2.1 0.7 fusion.26.dest
  2.7 0.8 add_convert_fusion
  3.5 0.7 broadcast_compare_fusion
  4.2 0.1 iota_add_fusion
  4.3 0.1 iota_add_fusion.1
  4.4 0.7 add_bitcast_fusion.1
  5.1 0.6 pad_add_fusion.dest
  5.7 0.6 pad_bitcast_fusion.refs_3_
  6.3 0.8 select_reduce_fusion.2
  7.1 0.6 sub.197.kept
  7.7 4.0 %pack.3.refs_8_ = f32[128,64,128]{2,1,0:T(8,128)} custom-call(s32[2,32]{1,0:T(2,128)} %fusion.26.dest, f32[32,128,128]{2,1,0:T(8,128)} %held.3), custom_call_target="tpu_custom_call" | custom-call | tf_op jit(solution)/shard_map/pack/pallas_call | solution.py:53
  11.7 6.8 %pack.2 = (f32[128,64,128]{2,1,0:T(8,128)}, f32[128,64,128]{2,1,0:T(8,128)}) custom-call(s32[2,64]{1,0:T(2,128)} %pad_add_fusion.dest, f32[64,128,128]{2,1,0:T(8,128)} %held.2), custom_call_target="tpu_custom_call" | custom-call | tf_op jit(solution)/shard_map/pack/pallas_call | solution.py:53
  18.5 153.0 %exchange.1 = (f32[8,4,4,64,128]{4,3,2,1,0:T(8,128)}, f32[4,8,4,64,128]{4,3,2,1,0:T(8,128)}, f32[4,4,8,64,128]{4,3,2,1,0:T(8,128)}, f32[8,4,4,64,128]{4,3,2,1,0:...) custom-call(f32[8,4,4,64,128]{4,3,2,1,0:T(8,128)} %bitcast.56, ...), custom_call_target="tpu_custom_call" | custom-call | tf_op jit(solution)/shard_map/exchange/pallas_call | solution.py:231
  171.5 1.3 reshape.196
  172.8 0.1 fusion
  172.9 0.1 convert_element_type.20
  173.0 0.1 fusion.47
  173.1 0.1 eq.160
  173.1 0.1 fusion.46
  173.2 0.1 eq.144
  173.3 0.1 reshape.198
  173.4 0.5 select_reduce_fusion.1
  173.9 0.1 reduce_sum.33
  174.0 0.1 reshape.197
  174.1 0.9 select_reduce_fusion
  175.0 0.1 reduce_sum.34
  175.2 0.7 pad_add_fusion.1.source
  175.8 0.6 fusion.21
  176.4 16.0 %collect.1 = (f32[64,128,128]{2,1,0:T(8,128)}, f32[64,64,128]{2,1,0:T(8,128)}, s32[3,264]{1,0:T(4,128)}, s32[3]{0:T(128)}) custom-call(s32[192]{0:T(256)} %pad_add_fusion.1.source, s32[192]{0:T(256)} %get-tuple-element.68.lefts, s32[192]{0:T(256)} %get-tuple-element.69.rights, s32[272]{0:T(512)} %sub.197.kept, f32[128,64,128]{2,1,0:T(8,128)} %get-tuple-element.28.refs_0_, ...), custom_call_target="tpu_custom_call" | custom-call | tf_op jit(solution)/shard_map/collect/pallas_call | solution.py:353
  192.4 141.3 %spread.1 = (f32[64,64,128]{2,1,0:T(8,128)}, f32[64,64,128]{2,1,0:T(8,128)}, f32[64,64,128]{2,1,0:T(8,128)}, f32[64,64,128]{2,1,0:T(8,128)}, f32[64,64,128]{2,1,...) custom-call(f32[64,64,128]{2,1,0:T(8,128)} %get-tuple-element.42.own.refs_0_, ...), custom_call_target="tpu_custom_call" | custom-call | tf_op jit(solution)/shard_map/spread/pallas_call | solution.py:520
  333.7 14.4 %products.1 = f32[96,128,128]{2,1,0:T(8,128)} custom-call(s32[3]{0:T(128)} %get-tuple-element.40.counts, s32[3,264]{1,0:T(4,128)} %get-tuple-element.41.items, s32[3]{0:T(128)} %compare_convert_fusion.order, s32[2]{0:T(128)} %pad_add_fusion.2.places, f32[64,64,128]{2,1,0:T(8,128)} %get-tuple-element.42.own.refs_0_, ...), custom_call_target="tpu_custom_call" | custom-call | tf_op jit(solution)/shard_map/products/pallas_call | solution.py:620
  (12 shorter events, 0.1 us)

commit v7 on v6

--- a/solution.py
+++ b/solution.py
@@ -14,31 +14,73 @@
 HBM = pl.BlockSpec(memory_space=pltpu.HBM)
 
 
-def pack_kernel(pieces, dest, held, *refs):
-    outs, buf, sems = refs[:-2], refs[-2], refs[-1]
-    count, rows, _ = held.shape
-    part = rows // pieces
-
-    def load(at):
-        return pltpu.make_async_copy(held.at[at], buf.at[at], sems.at[at])
-
-    def save(at, piece):
+def pack_kernel(
+    grid, a_slot, b_slot, c_col, a_held, b_held, upper, lower, halves, kept, a_buf, b_buf, sems
+):
+    grid_rows, grid_cols = grid
+    hold_a, hold_b = a_held.shape[0], b_held.shape[0]
+    rows, width = c_col.shape
+    part = halves.shape[1]
+    base = hold_a + hold_b
+
+    def load_a(at):
+        return pltpu.make_async_copy(a_held.at[at], a_buf.at[at], sems.at[at])
+
+    def load_b(at):
+        return pltpu.make_async_copy(b_held.at[at], b_buf.at[at], sems.at[hold_a + at])
+
+    def save_a(at, half, spot):
         return pltpu.make_async_copy(
-            buf.at[at, pl.ds(piece * part, part)],
-            outs[piece % len(outs)].at[dest[piece, at]],
-            sems.at[(1 + piece) * count + at],
+            a_buf.at[at, pl.ds(half * part, part)], halves.at[spot], sems.at[base + 2 * at + half]
         )
 
-    pl.loop(0, count)(lambda at: load(at).start())
-
-    def body(at):
-        load(at).wait()
-        for piece in range(pieces):
-            save(at, piece).start()
-
-    pl.loop(0, count)(body)
-    for piece in range(pieces):
-        pl.loop(0, count)(lambda at: save(at, piece).wait())
+    def save_b(at, half, spot):
+        return pltpu.make_async_copy(
+            b_buf.at[at, pl.ds(half * part, part)],
+            (upper, lower)[half].at[spot],
+            sems.at[base + 2 * (hold_a + at) + half],
+        )
+
+    pl.loop(0, hold_b)(lambda at: load_b(at).start())
+    pl.loop(0, hold_a)(lambda at: load_a(at).start())
+
+    def send_b(at):
+        panel = lax.div(b_slot[at], KPB * WB)
+        inner, col = lax.div(panel, grid_cols), lax.rem(panel, grid_cols)
+        row = lax.rem(inner - col - 1 + grid_rows + grid_cols, grid_rows)
+        place = place_of(row * grid_cols + col)
+        load_b(at).wait()
+        for half, order in enumerate(ORDERS[:2]):
+            save_b(at, half, place_in_send(place, order)).start()
+
+    pl.loop(0, hold_b)(send_b)
+
+    def send_a(at):
+        panel = lax.div(a_slot[at], rows * WA)
+        row, inner = lax.div(panel, grid_rows), lax.rem(panel, grid_rows)
+        col = lax.rem(inner - row - 1 + 2 * grid_rows, grid_rows)
+        load_a(at).wait()
+        for half in range(2):
+            place = place_of(row * grid_cols + col + half * grid_rows)
+            save_a(at, half, place_in_send(place, ORDERS[2])).start()
+
+    pl.loop(0, hold_a)(send_a)
+
+    def empty(row):
+        for column in range(KPB + 1):
+            kept[row * (KPB + 1) + column] = -1
+
+    pl.loop(0, rows)(empty)
+
+    def keep(row):
+        for at in range(width):
+            column = c_col[row, at]
+            kept[row * (KPB + 1) + column + 1] = jnp.where(column >= 0, row * width + at, -1)
+
+    pl.loop(0, rows)(keep)
+    for half in range(2):
+        pl.loop(0, hold_b)(lambda at: save_b(at, half, 0).wait())
+        pl.loop(0, hold_a)(lambda at: save_a(at, half, 0).wait())
 
 
 GRANT = 60 * 1024 * 1024
@@ -46,22 +88,25 @@
 VMEM = pl.BlockSpec(memory_space=pltpu.VMEM)
 
 
-def pack(held, dest, devices, outs):
-    pieces = dest.shape[0]
-    count, rows, cols = held.shape
-    shape = jax.ShapeDtypeStruct((devices, rows // pieces, cols), held.dtype)
-    return pl.pallas_call(
-        functools.partial(pack_kernel, pieces),
-        out_shape=[shape] * outs,
-        in_specs=[SMEM, HBM],
-        out_specs=[HBM] * outs,
+def pack(grid, a_slot, b_slot, c_col, a_held, b_held):
+    devices = grid[0] * grid[1]
+    edge, cols = a_held.shape[1:]
+    send = jax.ShapeDtypeStruct((devices, edge // 2, cols), a_held.dtype)
+    kept = jax.ShapeDtypeStruct((c_col.shape[0] * (KPB + 1),), jnp.int32)
+    *sends, kept = pl.pallas_call(
+        functools.partial(pack_kernel, grid),
+        out_shape=[send] * 3 + [kept],
+        in_specs=[SMEM] * 3 + [HBM] * 2,
+        out_specs=[HBM] * 3 + [SMEM],
         scratch_shapes=[
-            pltpu.VMEM(held.shape, held.dtype),
-            pltpu.SemaphoreType.DMA(((1 + pieces) * count,)),
+            pltpu.VMEM(a_held.shape, a_held.dtype),
+            pltpu.VMEM(b_held.shape, b_held.dtype),
+            pltpu.SemaphoreType.DMA((3 * (a_held.shape[0] + b_held.shape[0]),)),
         ],
         compiler_params=pltpu.CompilerParams(vmem_limit_bytes=GRANT),
         name="pack",
-    )(dest, held)
+    )(a_slot, b_slot, c_col, a_held, b_held)
+    return sends, kept
 
 
 ORDERS = (("x", "y", "z"), ("y", "z", "x"), ("z", "x", "y"))
@@ -275,12 +320,12 @@
 
 
 def place_of(device):
-    row, col = device // (RING * RING), device % (RING * RING)
+    row, col = lax.div(device, RING * RING), lax.rem(device, RING * RING)
     return {
-        "x": row // RING * 2 + col // CORES % 2,
-        "y": col // RING,
-        "z": row % RING,
-        "core": col % CORES,
+        "x": lax.div(row, RING) * 2 + lax.rem(lax.div(col, CORES), 2),
+        "y": lax.div(col, RING),
+        "z": lax.rem(row, RING),
+        "core": lax.rem(col, CORES),
     }
 
 
@@ -373,6 +418,7 @@
 RIGHT_CHUNKS = 8
 RELAYED = 3
 LEFT_CHUNKS = 4
+AHEAD = 2
 
 
 def spread_kernel(own, right, other, mate_one, mate_two, cross_one, cross_two, before, after, *sems):
@@ -441,41 +487,59 @@
 
     last = half == RING - 1
     first = half == 0
-    for at in range(RELAYED):
-
-        @pl.when(jnp.logical_not(last))
-        def _():
-            raise_chunk(at).start()
-
-        @pl.when(jnp.logical_not(first))
-        def _():
-            lower_chunk(at).start()
-
-    for at in range(LEFT_CHUNKS):
-        to_cross(at).start()
-        to_twin(at).start()
-        to_mate(at).start()
-    for at in range(RELAYED, RIGHT_CHUNKS):
-        raise_chunk(at).start()
-        lower_chunk(at).start()
-    for at in range(RELAYED):
-
-        @pl.when(half == RING - 2)
-        def _():
-            lower_chunk(at).wait_recv()
-            relay_up(at).start()
-
-        @pl.when(half == 1)
-        def _():
-            raise_chunk(at).wait_recv()
-            relay_down(at).start()
-
-    for at in range(LEFT_CHUNKS):
-        to_cross(at).wait_recv()
-        pass_twin(at).start()
-        to_twin(at).wait_recv()
-        pass_mate(at).start()
-
+
+    def on_right(at, action):
+        if at >= RELAYED:
+            action(raise_chunk(at))
+            action(lower_chunk(at))
+        else:
+
+            @pl.when(jnp.logical_not(last))
+            def _():
+                action(raise_chunk(at))
+
+            @pl.when(jnp.logical_not(first))
+            def _():
+                action(lower_chunk(at))
+
+    def start(copy):
+        copy.start()
+
+    def sent(copy):
+        copy.wait_send()
+
+    for at in range(RIGHT_CHUNKS):
+        if at >= AHEAD:
+            on_right(at - AHEAD, sent)
+            if at - AHEAD < LEFT_CHUNKS:
+                to_twin(at - AHEAD).wait_send()
+        if at < LEFT_CHUNKS:
+            to_cross(at).start()
+            to_twin(at).start()
+            to_mate(at).start()
+        else:
+            to_cross(at - LEFT_CHUNKS).wait_recv()
+            pass_twin(at - LEFT_CHUNKS).start()
+        on_right(at, start)
+        relay = at - AHEAD
+        if 0 <= relay < RELAYED:
+
+            @pl.when(half == RING - 2)
+            def _():
+                lower_chunk(relay).wait_recv()
+                relay_up(relay).start()
+
+            @pl.when(half == 1)
+            def _():
+                raise_chunk(relay).wait_recv()
+                relay_down(relay).start()
+
+        if at >= LEFT_CHUNKS:
+            to_twin(at - LEFT_CHUNKS).wait_recv()
+            pass_mate(at - LEFT_CHUNKS).start()
+
+    for at in range(RIGHT_CHUNKS - AHEAD, RIGHT_CHUNKS):
+        on_right(at, sent)
     for at in range(RELAYED):
 
         @pl.when(half != 1)
@@ -486,14 +550,6 @@
         def _():
             lower_chunk(at).wait_recv()
 
-        @pl.when(jnp.logical_not(last))
-        def _():
-            raise_chunk(at).wait_send()
-
-        @pl.when(jnp.logical_not(first))
-        def _():
-            lower_chunk(at).wait_send()
-
         @pl.when(half == RING - 2)
         def _():
             relay_up(at).wait_send()
@@ -503,14 +559,15 @@
             relay_down(at).wait_send()
 
     for at in range(RELAYED, RIGHT_CHUNKS):
-        raise_chunk(at).wait()
-        lower_chunk(at).wait()
+        raise_chunk(at).wait_recv()
+        lower_chunk(at).wait_recv()
     for at in range(LEFT_CHUNKS):
         to_mate(at).wait()
         pass_mate(at).wait()
         pass_twin(at).wait()
-        to_twin(at).wait_send()
         to_cross(at).wait_send()
+        if at + AHEAD >= RIGHT_CHUNKS:
+            to_twin(at).wait_send()
 
 
 def spread(own, right):
@@ -547,10 +604,15 @@
 SPARE = 96
 
 
-def product_kernel(counts, items, order, places, *refs):
+def product_kernel(counts, items, *refs):
     lefts = refs[: 2 * STEPS]
     right, before, after, out, left_buf, right_buf, total, load_sems, out_sem = refs[2 * STEPS :]
     outs, edge, _ = out.shape
+    col, cols = lax.axis_index("col"), lax.axis_size("col")
+    side = 2 * lax.rem(col, 2) - 1
+    places = (lax.rem(col + 1, 2), lax.rem(col, 2))
+    homes = (col, col - side, lax.rem(col + side + cols, cols))
+    order = [lax.div(home, cols // 2) for home in homes]
 
     def right_load(step, source):
         return pltpu.make_async_copy(source, right_buf.at[step], load_sems.at[2 * STEPS + step])
@@ -614,13 +676,13 @@
     save.wait()
 
 
-def products(counts, items, order, places, lefts, rights, outs):
+def products(counts, items, lefts, rights, outs):
     slots_b, edge, _ = rights[0].shape
     slots_a, part, _ = lefts[0].shape
     return pl.pallas_call(
         product_kernel,
         out_shape=jax.ShapeDtypeStruct((outs, edge, edge), jnp.float32),
-        in_specs=[SMEM] * 4 + [HBM] * (len(lefts) + len(rights)),
+        in_specs=[SMEM] * 2 + [HBM] * (len(lefts) + len(rights)),
         out_specs=HBM,
         scratch_shapes=[
             pltpu.VMEM((2 * STEPS, slots_a, part, edge), jnp.float32),
@@ -631,7 +693,7 @@
         ],
         compiler_params=pltpu.CompilerParams(vmem_limit_bytes=GRANT),
         name="products",
-    )(counts, items, order, places, *lefts, *rights)
+    )(counts, items, *lefts, *rights)
 
 
 def on_device(a_held, a_slot, a_col, b_held, b_slot, b_col, c_col):
@@ -645,26 +707,14 @@
     hold_a, hold_b = a_slot.shape[0], b_slot.shape[0]
     slots_a, slots_b = rows * WA, KPB * WB
 
-    panel = a_slot // slots_a
-    at_row, inner = panel // grid_rows, panel % grid_rows
-    dest = at_row * grid_cols + (inner - at_row - 1) % grid_rows
-    dest_left = dest[None, :] + grid_rows * jnp.arange(copies, dtype=jnp.int32)[:, None]
-    panel = b_slot // slots_b
-    inner, at_col = panel // grid_cols, panel % grid_cols
-    dest_right = ((inner - at_col - 1) % grid_rows) * grid_cols + at_col
-
     edge = a_held.shape[1]
-    labels = jnp.concatenate([a_slot, a_col, b_slot, b_col]).astype(jnp.float32)
+    labels = jnp.concatenate([a_slot, a_col, b_slot, b_col])
     tile = jnp.pad(labels, (0, 8 * edge - labels.shape[0])).reshape(8, edge)
-    to_right, to_left = place_of(dest_right), place_of(dest_left)
-    spots = jnp.stack([place_in_send(to_right, order) for order in ORDERS[:2]])
-    sends = pack(b_held, spots, devices, 2)
-    sends += pack(a_held, place_in_send(to_left, ORDERS[2]), devices, 1)
+    sends, kept = pack((grid_rows, grid_cols), a_slot, b_slot, c_col, a_held, b_held)
     received, labels = exchange(sends, tile)
 
     labels = labels.reshape(RING, RING, 2, 2, CORES, -1)[..., : 2 * (hold_a + hold_b)]
     labels = labels.transpose(2, 0, 1, 3, 4, 5).reshape(devices, -1)
-    labels = labels.astype(jnp.int32)
     parts = [hold_a, 2 * hold_a, 2 * hold_a + hold_b]
     all_a, all_acol, all_b, all_bcol = (part.reshape(-1) for part in jnp.split(labels, parts, axis=1))
 
@@ -686,24 +736,17 @@
     origin = place_of(src_right[0])
     source = [place_received(origin, here, order) for order in ORDERS[:2]]
     source.append(place_received(place_of(src_left[0]), here, ORDERS[2]))
-    hit = c_col[:, :, None] == jnp.arange(-1, KPB, dtype=jnp.int32)
-    hit &= (c_col >= 0)[:, :, None]
-    outs = jnp.arange(rows * width, dtype=jnp.int32).reshape(rows, width, 1)
-    kept = jnp.sum(jnp.where(hit, outs + 1, 0), axis=1) - 1
     right, own, items, counts = collect(
         received,
         jnp.concatenate(source),
         col_left.reshape(-1),
         col_right.reshape(-1),
-        kept.reshape(-1),
+        kept,
     )
     other, mate_one, mate_two, cross_one, cross_two, before, after = spread(own, right)
 
-    homes = (c + jnp.stack([jnp.int32(0), -side, side])) % grid_cols
-    order = (homes >= grid_rows).astype(jnp.int32)
-    places = jnp.stack([(1 - side) // 2, (1 + side) // 2])
     lefts = [own, other, mate_one, mate_two, cross_one, cross_two]
-    total = products(counts, items, order, places, lefts, [right, before, after], rows * width)
+    total = products(counts, items, lefts, [right, before, after], rows * width)
     return total.reshape(rows, width, edge, edge)
 
 

time: 350 us -> 347 us (level); the launches traced: 348 us -> 340 us
  other arithmetic: 9.25 us -> 3.75 us
    pallas_call x2 -> x1, Pallas kernels: 10.8 us -> 10.6 us  [pack(): pl.pallas_call(functools.partial(pack_kernel, grid), out_shape=[send] * 3...]
where the time goes in v7:
time: 347 us; the launch traced here: 340 us
  Pallas kernels  333 us (96%)
  local copies, waits for them, and re-layouts  4.02 us (1%)
  other arithmetic  3.75 us (1%)
    pallas_call x1, Pallas kernels, exchange(): pl.pallas_call(exchange_kernel, out_shape=[jax.ShapeDtypeStruct(shape, ki...  153 us
    pallas_call x1, Pallas kernels, spread(): pl.pallas_call(spread_kernel, out_shape=[left_shape] * 5 + [right_shape]...  139 us
    pallas_call x1, Pallas kernels, collect(): pl.pallas_call(collect_kernel, out_shape=[jax.ShapeDtypeStruct(right, kin...  16 us
    pallas_call x1, Pallas kernels, products(): pl.pallas_call(product_kernel, out_shape=jax.ShapeDtypeStruct((outs, edge...  13.8 us
    pallas_call x1, Pallas kernels, pack(): pl.pallas_call(functools.partial(pack_kernel, grid), out_shape=[send] * 3...  10.6 us

profile of v7, /device:TPU:26, one launch (start us, length us, event | category | flops | bytes accessed | tf_op | source)
XLA Modules:
  0.0 340.5 jit_solution(5711447523874061362)
XLA Ops:
  0.0 0.1 add_multiply_fusion.1
  0.1 0.8 pad_add_fusion
  0.9 0.1 iota_add_fusion
  0.9 0.1 iota_add_fusion.1
  1.0 0.6 pad_bitcast_fusion.refs_3_
  1.6 1.4 copy.11.c_col
  3.0 10.6 %pack.1 = (f32[128,64,128]{2,1,0:T(8,128)}, f32[128,64,128]{2,1,0:T(8,128)}, f32[128,64,128]{2,1,0:T(8,128)}, s32[272]{0:T(512)}) custom-call(s32[32]{0:T(128)} %a_slot.1, s32[64]{0:T(128)} %b_slot.1, s32[16,6]{1,0:T(8,128)} %copy.11.c_col, f32[32,128,128]{2,1,0:T(8,128)} %a_held.1, f32[64,128,128]{2,1,0:T(8,128)} %b_held.1), custom_call_target="tpu_custom_call" | custom-call | tf_op jit(solution)/shard_map/pack/pallas_call | solution.py:96
  13.6 153.0 %exchange.1 = (f32[8,4,4,64,128]{4,3,2,1,0:T(8,128)}, f32[4,8,4,64,128]{4,3,2,1,0:T(8,128)}, f32[4,4,8,64,128]{4,3,2,1,0:T(8,128)}, f32[8,4,4,64,128]{4,3,2,1,0:...) custom-call(f32[8,4,4,64,128]{4,3,2,1,0:T(8,128)} %bitcast.52, ...), custom_call_target="tpu_custom_call" | custom-call | tf_op jit(solution)/shard_map/exchange/pallas_call | solution.py:276
  166.6 1.3 reshape.162
  168.0 0.1 reshape.163
  168.1 0.1 fusion.30
  168.2 0.1 eq.119
  168.2 0.1 fusion.29
  168.3 0.1 eq.103
  168.4 0.1 reshape.165
  168.5 0.5 select_reduce_fusion.1
  169.0 0.1 reduce_sum.24
  169.1 0.1 reshape.164
  169.2 0.9 select_reduce_fusion
  170.1 0.1 reduce_sum.25
  170.2 0.7 pad_add_fusion.1.source
  170.9 0.6 fusion.16
  171.5 16.0 %collect.1 = (f32[64,128,128]{2,1,0:T(8,128)}, f32[64,64,128]{2,1,0:T(8,128)}, s32[3,264]{1,0:T(4,128)}, s32[3]{0:T(128)}) custom-call(s32[192]{0:T(256)} %pad_add_fusion.1.source, s32[192]{0:T(256)} %get-tuple-element.64.lefts, s32[192]{0:T(256)} %get-tuple-element.65.rights, s32[272]{0:T(512)} %get-tuple-element.34.kept, ...), custom_call_target="tpu_custom_call" | custom-call | tf_op jit(solution)/shard_map/collect/pallas_call | solution.py:398
  187.5 139.2 %spread.1 = (f32[64,64,128]{2,1,0:T(8,128)}, f32[64,64,128]{2,1,0:T(8,128)}, f32[64,64,128]{2,1,0:T(8,128)}, f32[64,64,128]{2,1,0:T(8,128)}, f32[64,64,128]{2,1,...) custom-call(f32[64,64,128]{2,1,0:T(8,128)} %get-tuple-element.46.own.refs_0_, ...), custom_call_target="tpu_custom_call" | custom-call | tf_op jit(solution)/shard_map/spread/pallas_call | solution.py:577
  326.6 13.8 %products.1 = f32[96,128,128]{2,1,0:T(8,128)} custom-call(s32[3]{0:T(128)} %get-tuple-element.44.counts, s32[3,264]{1,0:T(4,128)} %get-tuple-element.45.items, f32[64,64,128]{2,1,0:T(8,128)} %get-tuple-element.46.own.refs_0_, f32[64,64,128]{2,1,0:T(8,128)} %get-tuple-element.48.refs_1_, f32[64,64,128]{2,1,0:T(8,128)} %get-tuple-element.49.refs_2_, ...), custom_call_target="tpu_custom_call" | custom-call | tf_op jit(solution)/shard_map/products/pallas_call | solution.py:682
  (8 shorter events, 0.1 us)

commit v8 on v5

--- a/solution.py
+++ b/solution.py
@@ -11,7 +11,7 @@
 WA = 4
 WB = 4
 STEPS = 3
-HBM = pl.BlockSpec(memory_space=pl.ANY)
+HBM = pl.BlockSpec(memory_space=pltpu.HBM)
 
 
 def shifted(value, axis, steps):
@@ -25,52 +25,84 @@
     return lax.ppermute(value, axis, [(at, target(at) % count) for at in range(count)])
 
 
-def pack_kernel(pieces, dest, held, *refs):
-    outs, buf, sems = refs[:-2], refs[-2], refs[-1]
-    count, rows, _ = held.shape
-    part = rows // pieces
-
-    def load(at):
-        return pltpu.make_async_copy(held.at[at], buf.at[at], sems.at[at])
-
-    def save(at, piece):
+def pack_kernel(
+    grid, slots, a_slot, b_slot, a_held, b_held, upper, lower, halves, a_buf, b_buf, sems
+):
+    grid_rows, grid_cols = grid
+    hold_a, hold_b = a_held.shape[0], b_held.shape[0]
+    part = halves.shape[1]
+    base = hold_a + hold_b
+
+    def load_a(at):
+        return pltpu.make_async_copy(a_held.at[at], a_buf.at[at], sems.at[at])
+
+    def load_b(at):
+        return pltpu.make_async_copy(b_held.at[at], b_buf.at[at], sems.at[hold_a + at])
+
+    def save_a(at, half, spot):
         return pltpu.make_async_copy(
-            buf.at[at, pl.ds(piece * part, part)],
-            outs[piece % len(outs)].at[dest[piece, at]],
-            sems.at[(1 + piece) * count + at],
+            a_buf.at[at, pl.ds(half * part, part)], halves.at[spot], sems.at[base + 2 * at + half]
         )
 
-    pl.loop(0, count)(lambda at: load(at).start())
-
-    def body(at):
-        load(at).wait()
-        for piece in range(pieces):
-            save(at, piece).start()
-
-    pl.loop(0, count)(body)
-    for piece in range(pieces):
-        pl.loop(0, count)(lambda at: save(at, piece).wait())
-
-
+    def save_b(at, half, spot):
+        return pltpu.make_async_copy(
+            b_buf.at[at, pl.ds(half * part, part)],
+            (upper, lower)[half].at[spot],
+            sems.at[base + 2 * (hold_a + at) + half],
+        )
+
+    pl.loop(0, hold_b)(lambda at: load_b(at).start())
+    pl.loop(0, hold_a)(lambda at: load_a(at).start())
+
+    def send_b(at):
+        panel = lax.div(b_slot[at], slots[1])
+        inner, col = lax.div(panel, grid_cols), lax.rem(panel, grid_cols)
+        row = lax.rem(inner - col - 1 + grid_rows + grid_cols, grid_rows)
+        place = place_of(row * grid_cols + col)
+        load_b(at).wait()
+        for half, order in enumerate(ORDERS[:2]):
+            save_b(at, half, place_in_send(place, order)).start()
+
+    pl.loop(0, hold_b, unroll=4)(send_b)
+
+    def send_a(at):
+        panel = lax.div(a_slot[at], slots[0])
+        row, inner = lax.div(panel, grid_rows), lax.rem(panel, grid_rows)
+        col = lax.rem(inner - row - 1 + 2 * grid_rows, grid_rows)
+        load_a(at).wait()
+        for half in range(2):
+            place = place_of(row * grid_cols + col + half * grid_rows)
+            save_a(at, half, place_in_send(place, ORDERS[2])).start()
+
+    pl.loop(0, hold_a, unroll=4)(send_a)
+
+    for half in range(2):
+        pl.loop(0, hold_b)(lambda at: save_b(at, half, 0).wait())
+        pl.loop(0, hold_a)(lambda at: save_a(at, half, 0).wait())
+
+
+GRANT = 60 * 1024 * 1024
 SMEM = pl.BlockSpec(memory_space=pltpu.SMEM)
 VMEM = pl.BlockSpec(memory_space=pltpu.VMEM)
 
 
-def pack(held, dest, devices, outs):
-    pieces = dest.shape[0]
-    count, rows, cols = held.shape
-    shape = jax.ShapeDtypeStruct((devices, rows // pieces, cols), held.dtype)
+def pack(grid, slots, a_slot, b_slot, a_held, b_held):
+    devices = grid[0] * grid[1]
+    edge, cols = a_held.shape[1:]
+    send = jax.ShapeDtypeStruct((devices, edge // 2, cols), a_held.dtype)
     return pl.pallas_call(
-        functools.partial(pack_kernel, pieces),
-        out_shape=[shape] * outs,
-        in_specs=[SMEM, HBM],
-        out_specs=[HBM] * outs,
+        functools.partial(pack_kernel, grid, slots),
+        out_shape=[send] * 3,
+        in_specs=[SMEM] * 2 + [HBM] * 2,
+        out_specs=[HBM] * 3,
         scratch_shapes=[
-            pltpu.VMEM(held.shape, held.dtype),
-            pltpu.SemaphoreType.DMA(((1 + pieces) * count,)),
+            pltpu.VMEM(a_held.shape, a_held.dtype),
+            pltpu.VMEM(b_held.shape, b_held.dtype),
+            pltpu.SemaphoreType.DMA((3 * (a_held.shape[0] + b_held.shape[0]),)),
         ],
+        compiler_params=pltpu.CompilerParams(vmem_limit_bytes=GRANT),
         name="pack",
-    )(dest, held)
+    )(a_slot, b_slot, a_held, b_held)
 
 
 ORDERS = (("x", "y", "z"), ("y", "z", "x"), ("z", "x", "y"))
@@ -252,7 +284,7 @@
             pltpu.SemaphoreType.DMA((3,)),
         ],
         compiler_params=pltpu.CompilerParams(
-            collective_id=0, has_side_effects=True, vmem_limit_bytes=40 * 1024 * 1024
+            collective_id=0, has_side_effects=True, vmem_limit_bytes=GRANT
         ),
         name="exchange",
     )(*(send.reshape((eight, RING, RING) + block) for send in sends), tile)
@@ -284,12 +316,12 @@
 
 
 def place_of(device):
-    row, col = device // (RING * RING), device % (RING * RING)
+    row, col = lax.div(device, RING * RING), lax.rem(device, RING * RING)
     return {
-        "x": row // RING * 2 + col // CORES % 2,
-        "y": col // RING,
-        "z": row % RING,
-        "core": col % CORES,
+        "x": lax.div(row, RING) * 2 + lax.rem(lax.div(col, CORES), 2),
+        "y": lax.div(col, RING),
+        "z": lax.rem(row, RING),
+        "core": lax.rem(col, CORES),
     }
 
 
@@ -321,7 +353,7 @@
                 group[3].at[0], target(at, piece), sems.at[piece * count + at]
             ).wait()
 
-    pl.loop(0, count)(load)
+    pl.loop(0, count, unroll=2)(load)
     saves = [
         pltpu.make_async_copy(
             buf.at[pl.ds(part * chunk, chunk)], out, sems.at[pieces * count + part]
@@ -350,6 +382,7 @@
             pltpu.VMEM((count, pieces * rows, cols), kind),
             pltpu.SemaphoreType.DMA((pieces * count + chunks,)),
         ],
+        compiler_params=pltpu.CompilerParams(vmem_limit_bytes=GRANT),
         name="collect",
     )(source, *(ref for group in groups for ref in group))
 
@@ -453,7 +486,7 @@
             pltpu.SemaphoreType.DMA((2 * pieces + parts,)),
             pltpu.SemaphoreType.DMA,
         ],
-        compiler_params=pltpu.CompilerParams(vmem_limit_bytes=40 * 1024 * 1024),
+        compiler_params=pltpu.CompilerParams(vmem_limit_bytes=GRANT),
         cost_estimate=pl.CostEstimate(
             flops=pieces * 600_000_000, bytes_accessed=pieces * 8_000_000, transcendentals=0
         ),
@@ -499,26 +532,15 @@
     hold_a, hold_b = a_slot.shape[0], b_slot.shape[0]
     slots_a, slots_b = rows * WA, KPB * WB
 
-    panel = a_slot // slots_a
-    at_row, inner = panel // grid_rows, panel % grid_rows
-    dest = at_row * grid_cols + (inner - at_row - 1) % grid_rows
-    dest_left = dest[None, :] + grid_rows * jnp.arange(copies, dtype=jnp.int32)[:, None]
-    panel = b_slot // slots_b
-    inner, at_col = panel // grid_cols, panel % grid_cols
-    dest_right = ((inner - at_col - 1) % grid_rows) * grid_cols + at_col
-
     edge = a_held.shape[1]
-    labels = jnp.concatenate([a_slot, a_col, b_slot, b_col]).astype(jnp.float32)
+    labels = jnp.concatenate([a_slot, a_col, b_slot, b_col])
     tile = jnp.pad(labels, (0, 8 * edge - labels.shape[0])).reshape(8, edge)
-    to_right, to_left = place_of(dest_right), place_of(dest_left)
-    spots = jnp.stack([place_in_send(to_right, order) for order in ORDERS[:2]])
-    sends = pack(b_held, spots, devices, 2)
-    sends += pack(a_held, place_in_send(to_left, ORDERS[2]), devices, 1)
+    grid, slots = (grid_rows, grid_cols), (slots_a, slots_b)
+    sends = pack(grid, slots, a_slot, b_slot, a_held, b_held)
     received, labels = exchange(sends, tile)
 
     labels = labels.reshape(RING, RING, 2, 2, CORES, -1)[..., : 2 * (hold_a + hold_b)]
     labels = labels.transpose(2, 0, 1, 3, 4, 5).reshape(devices, -1)
-    labels = labels.astype(jnp.int32)
     parts = [hold_a, 2 * hold_a, 2 * hold_a + hold_b]
     all_a, all_acol, all_b, all_bcol = (part.reshape(-1) for part in jnp.split(labels, parts, axis=1))
 

time: 335 us -> 330 us (0.985)
  local copies, waits for them, and re-layouts: 15.1 us -> 6.7 us
  Pallas kernels: 201 us -> 208 us
    unnamed x14 -> x6, local copies, waits for them, and re-layouts: 10.6 us -> 0.01 us
    pallas_call x3, Pallas kernels: 27.9 us -> 35.6 us  [products(): pl.pallas_call(functools.partial(product_kernel, pieces, parts, first, UN...]
    pallas_call x2 -> x1, Pallas kernels: 10.7 us -> 9.25 us  [pack(): pl.pallas_call(functools.partial(pack_kernel, grid, slots), out_shape=[se...]
  transfers between devices with their start and end apart: 9 -> 9, of which waited for: 5 -> 5; matrix products, arithmetic and copies ran while one was open for 3% -> 4% of each run, Pallas kernels for 7% -> 9%
where the time goes in v8:
time: 330 us; the launch traced here: 329 us
  Pallas kernels  208 us (63%)
  waiting for transfers between devices  89.2 us (27%)
  starting transfers between devices  12 us (4%)
  other arithmetic  10.1 us (3%)
  local copies, waits for them, and re-layouts  6.7 us (2%)
    pallas_call x1, Pallas kernels, exchange(): pl.pallas_call(exchange_kernel, out_shape=[jax.ShapeDtypeStruct(shape, ki...  153 us
    ppermute x6, waiting for transfers between devices, shifted(): return lax.ppermute(value, axis, pairs)  89.2 us
    pallas_call x3, Pallas kernels, products(): pl.pallas_call(functools.partial(product_kernel, pieces, parts, first, UN...  35.6 us
    ppermute x6, starting transfers between devices, shifted(): return lax.ppermute(value, axis, pairs)  10.7 us
    pallas_call x2, Pallas kernels, collect(): pl.pallas_call(functools.partial(collect_kernel, pieces), out_shape=[part...  10.3 us
    pallas_call x1, Pallas kernels, pack(): pl.pallas_call(functools.partial(pack_kernel, grid, slots), out_shape=[se...  9.25 us
  transfers between devices with their start and end apart: 9, of which 5 were waited for; matrix products, arithmetic and copies ran while one was open for 4% of the time, Pallas kernels for 9%

profile of v8, /device:TPU:26, one launch (start us, length us, event | category | flops | bytes accessed | tf_op | source)
XLA Modules:
  0.0 328.5 jit_solution(11134773472576385099)
XLA Ops:
  0.0 0.8 pad_add_fusion
  0.8 0.6 pad_bitcast_fusion.refs_3_
  1.4 9.2 %pack.1 = (f32[128,64,128]{2,1,0:T(8,128)}, f32[128,64,128]{2,1,0:T(8,128)}, f32[128,64,128]{2,1,0:T(8,128)}) custom-call(s32[32]{0:T(128)} %a_slot.1, s32[64]{0:T(128)} %b_slot.1, f32[32,128,128]{2,1,0:T(8,128)} %a_held.1, f32[64,128,128]{2,1,0:T(8,128)} %b_held.1), custom_call_target="tpu_custom_call" | custom-call | tf_op jit(solution)/shard_map/pack/pallas_call | solution.py:93
  10.6 153.0 %exchange.1 = (f32[8,4,4,64,128]{4,3,2,1,0:T(8,128)}, f32[4,8,4,64,128]{4,3,2,1,0:T(8,128)}, f32[4,4,8,64,128]{4,3,2,1,0:T(8,128)}, f32[8,4,4,64,128]{4,3,2,1,0:...) custom-call(f32[8,4,4,64,128]{4,3,2,1,0:T(8,128)} %bitcast.47, ...), custom_call_target="tpu_custom_call" | custom-call | tf_op jit(solution)/shard_map/exchange/pallas_call | solution.py:272
  163.7 1.3 reshape.633
  165.5 0.5 select_reduce_fusion.1
  166.1 0.6 fusion.22.source
  166.6 4.4 %collect.2.refs_0_ = f32[64,64,128]{2,1,0:T(8,128)} custom-call(s32[1,64]{1,0:T(1,128)} %fusion.22.source, f32[128,64,128]{2,1,0:T(8,128)} %get-tuple-element.22.refs_0_, f32[128,64,128]{2,1,0:T(8,128)} %bitcast.56, f32[128,64,128]{2,1,0:T(8,128)} %bitcast.57, f32[128,64,128]{2,1,0:T(8,128)} %bitcast.58), custom_call_target="tpu_custom_call" | custom-call | tf_op jit(solution)/shard_map/collect/pallas_call | solution.py:376
  171.1 2.1 collective-permute-start.1
  173.3 1.2 collective-permute-start.3
  174.8 0.9 select_reduce_fusion
  175.8 0.5 pad_add_fusion.1.source
  176.3 5.9 %collect.3 = (f32[32,128,128]{2,1,0:T(8,128)}, f32[32,128,128]{2,1,0:T(8,128)}) custom-call(s32[2,64]{1,0:T(2,128)} %pad_add_fusion.1.source, f32[128,64,128]{2,1,0:T(8,128)} %get-tuple-element.20.refs_0_, f32[128,64,128]{2,1,0:T(8,128)} %bitcast.50, f32[128,64,128]{2,1,0:T(8,128)} %bitcast.51, f32[128,64,128]{2,1,0:T(8,128)} %bitcast.52, ...), custom_call_target="tpu_custom_call" | custom-call | tf_op jit(solution)/shard_map/collect/pallas_call | solution.py:376
  182.2 1.0 collective-permute-start.7
  183.3 4.7 %collective-permute-start.8 = (f32[32,128,128]{2,1,0:T(8,128)}, f32[32,128,128]{2,1,0:T(8,128)}, u32[]{:S(2)}, u32[]{:S(2)}) collective-permute-start(f32[32,128,128]{2,1,0:T(8,128)} %get-tuple-element.34.refs_2_), channel_id=1, source_target_pairs={{0,112},{16,0},{32,16},{48,32},{64,48},{80,64},{96,80},{112,96},{1... | collective-permute-start | bytes 6291464 | tf_op jit(solution)/shard_map/ppermute | solution.py:20
  188.6 0.1 select_reduce_fusion.7
  188.9 0.1 select_reduce_fusion.8
  189.0 0.6 convert_reduce_fusion.1
  190.3 0.1 copy.25
  190.4 0.6 convert_reduce_fusion
  191.6 0.1 copy.29
  191.9 0.1 select_reduce_fusion.5
  192.1 0.6 broadcast_add_fusion.2
  193.4 0.1 copy.27
  193.5 0.1 reshape.660
  193.6 0.1 copy.26
  193.8 0.1 reshape.652
  193.9 0.3 reduce-window.25
  194.3 0.1 reshape.651
  194.5 0.7 slice.59.order
  195.2 0.1 copy.31
  195.3 0.1 reshape.662
  195.4 0.1 copy.30
  195.5 0.1 reshape.656
  195.6 0.3 reduce-window.29
  196.0 0.1 reshape.655
  196.2 0.1 copy.33
  196.3 0.1 sub.163
  196.4 0.1 add.742
  196.6 0.1 add.734
  196.8 0.1 add.736
  197.0 0.1 add.738
  197.1 0.1 copy.34
  197.2 0.1 reshape.658
  197.3 0.3 reduce-window.37
  197.7 0.1 slice_reduce_fusion.2
  197.8 0.1 slice_reduce_fusion.1
  198.0 45.7 %collective-permute-done.1.refs_1_ = f32[64,64,128]{2,1,0:T(8,128)} collective-permute-done((f32[64,64,128]{2,1,0:T(8,128)}, f32[64,64,128]{2,1,0:T(8,128)}, u32[]{:S(2)}, u32[]{:S(2)}) %collective-permute-start.1) | collective-permute-done | bytes 2097184 | tf_op jit(solution)/shard_map/ppermute | solution.py:20
  243.8 1.8 collective-permute-start.4
  245.6 0.1 slice_reduce_fusion
  245.7 1.0 collective-permute-start.5
  246.7 22.0 %collective-permute-done.7.refs_4_ = f32[32,128,128]{2,1,0:T(8,128)} collective-permute-done((f32[32,128,128]{2,1,0:T(8,128)}, f32[32,128,128]{2,1,0:T(8,128)}, u32[]{:S(2)}, u32[]{:S(2)}) %collective-permute-start.7) | collective-permute-done | bytes 2097184 | tf_op jit(solution)/shard_map/ppermute | solution.py:20
  268.7 0.1 select_reduce_fusion.4
  268.9 0.3 select_reduce_fusion.3
  269.3 0.3 select_reduce_fusion.2
  269.6 0.6 broadcast_add_fusion.6.items
  270.2 0.6 broadcast_add_fusion.5.items
  270.8 0.6 broadcast_add_fusion.4.items
  271.3 10.1 %products.3.refs_6_ = f32[96,128,128]{2,1,0:T(8,128)} custom-call(s32[1]{0:T(128)} %bitcast.25.counts, s32[256]{0:T(256)} %broadcast_add_fusion.6.items, s32[1]{0:T(128)} %bitcast.59, f32[64,64,128]{2,1,0:T(8,128)} %collect.2.refs_0_, f32[64,64,128]{2,1,0:T(8,128)} %collective-permute-done.1.refs_1_, f32[32,128,128]{2,1,0:T(8,128)} %get-tuple-element.34.refs_2_, ...), custom_call_target="tpu_custom_call" | custom-call | flops 600000000 | bytes 8000000 | tf_op jit(solution)/shard_map/products/pallas_call | solution.py:477
  281.5 12.1 %collective-permute-done.4.refs_3_ = f32[64,64,128]{2,1,0:T(8,128)} collective-permute-done((f32[64,64,128]{2,1,0:T(8,128)}, f32[64,64,128]{2,1,0:T(8,128)}, u32[]{:S(2)}, u32[]{:S(2)}) %collective-permute-start.4) | collective-permute-done | bytes 2097184 | tf_op jit(solution)/shard_map/ppermute | solution.py:20
  293.6 13.3 %products.4.refs_6_ = f32[96,128,128]{2,1,0:T(8,128)} custom-call(s32[1]{0:T(128)} %bitcast.22.counts, s32[512]{0:T(512)} %broadcast_add_fusion.4.items, s32[2]{0:T(128)} %slice.59.order, f32[64,64,128]{2,1,0:T(8,128)} %copy-done, f32[64,64,128]{2,1,0:T(8,128)} %collective-permute-done.2.refs_1_, f32[64,64,128]{2,1,0:T(8,128)} %collective-permute-done.3.refs_2_, ...), custom_call_target="tpu_custom_call" | custom-call | flops 1200000000 | bytes 16000000 | tf_op jit(solution)/shard_map/products/pallas_call | solution.py:477
  306.9 6.5 %collective-permute-done.5.refs_4_ = f32[32,128,128]{2,1,0:T(8,128)} collective-permute-done((f32[32,128,128]{2,1,0:T(8,128)}, f32[32,128,128]{2,1,0:T(8,128)}, u32[]{:S(2)}, u32[]{:S(2)}) %collective-permute-start.5) | collective-permute-done | bytes 2097184 | tf_op jit(solution)/shard_map/ppermute | solution.py:20
  313.5 2.9 collective-permute-done.6.refs_5_
  316.3 12.2 %products.5 = f32[96,128,128]{2,1,0:T(8,128)} custom-call(s32[1]{0:T(128)} %bitcast.7.counts, s32[512]{0:T(512)} %broadcast_add_fusion.5.items, s32[2]{0:T(128)} %slice.59.order, f32[64,64,128]{2,1,0:T(8,128)} %copy-done, f32[64,64,128]{2,1,0:T(8,128)} %collective-permute-done.2.refs_1_, f32[64,64,128]{2,1,0:T(8,128)} %collective-permute-done.3.refs_2_, ...), custom_call_target="tpu_custom_call" | custom-call | flops 1200000000 | bytes 16000000 | tf_op jit(solution)/shard_map/products/pallas_call | solution.py:477
  (80 shorter events, 3.0 us)
Async XLA Ops:
  171.1 74.6 %collective-permute-start = (f32[64,64,128]{2,1,0:T(8,128)}, f32[64,64,128]{2,1,0:T(8,128)S(1)}, u32[]{:S(2)}, u32[]{:S(2)}) collective-permute-start(f32[64,64,128]{2,1,0:T(8,128)} %collect.2.refs_0_), channel_id=1, source_target_pairs={{0,1},{1,0},{2,3},{3,2},{4,5},{5,4},{6,7},{7,6},{8,9},{9,8},{10,11... | collective-permute-start | bytes 6291464 | tf_op jit(solution)/shard_map/ppermute | solution.py:25
  171.1 72.6 %collective-permute-start.1 = (f32[64,64,128]{2,1,0:T(8,128)}, f32[64,64,128]{2,1,0:T(8,128)}, u32[]{:S(2)}, u32[]{:S(2)}) collective-permute-start(f32[64,64,128]{2,1,0:T(8,128)} %collect.2.refs_0_), channel_id=1, source_target_pairs={{0,8},{1,9},{2,10},{3,11},{4,12},{5,13},{6,14},{7,15},{8,0},{9,1},... | collective-permute-start | bytes 6291464 | tf_op jit(solution)/shard_map/ppermute | solution.py:20
  173.3 70.5 %collective-permute-start.3 = (f32[64,64,128]{2,1,0:T(8,128)}, f32[64,64,128]{2,1,0:T(8,128)}, u32[]{:S(2)}, u32[]{:S(2)}) collective-permute-start(f32[64,64,128]{2,1,0:T(8,128)} %collect.2.refs_0_), channel_id=1, source_target_pairs={{0,15},{1,2},{2,1},{3,4},{4,3},{5,6},{6,5},{7,8},{8,7},{9,10},{10,... | collective-permute-start | bytes 6291464 | tf_op jit(solution)/shard_map/ppermute | solution.py:25
  176.3 12.4 %copy-start.1 = (s32[16,6]{0,1:T(8,128)S(1)}, s32[16,6]{0,1:T(8,128)}, u32[]{:S(2)}) copy-start(s32[16,6]{0,1:T(8,128)} %param.13) | copy-start | bytes 1156
  182.2 86.4 %collective-permute-start.7 = (f32[32,128,128]{2,1,0:T(8,128)}, f32[32,128,128]{2,1,0:T(8,128)}, u32[]{:S(2)}, u32[]{:S(2)}) collective-permute-start(f32[32,128,128]{2,1,0:T(8,128)} %get-tuple-element.34.refs_2_), channel_id=1, source_target_pairs={{0,16},{16,32},{32,48},{48,64},{64,80},{80,96},{96,112},{112,0},{1... | collective-permute-start | bytes 6291464 | tf_op jit(solution)/shard_map/ppermute | solution.py:20
  183.3 98.2 %collective-permute-start.8 = (f32[32,128,128]{2,1,0:T(8,128)}, f32[32,128,128]{2,1,0:T(8,128)}, u32[]{:S(2)}, u32[]{:S(2)}) collective-permute-start(f32[32,128,128]{2,1,0:T(8,128)} %get-tuple-element.34.refs_2_), channel_id=1, source_target_pairs={{0,112},{16,0},{32,16},{48,32},{64,48},{80,64},{96,80},{112,96},{1... | collective-permute-start | bytes 6291464 | tf_op jit(solution)/shard_map/ppermute | solution.py:20
  194.5 76.8 %copy-start.2 = (s32[3]{0:T(128)}, s32[3]{0:T(128)S(1)}, u32[]{:S(2)}) copy-start(s32[3]{0:T(128)S(1)} %compare_convert_fusion.1) | copy-start | bytes 40
  243.8 37.8 %collective-permute-start.2 = (f32[64,64,128]{2,1,0:T(8,128)}, f32[64,64,128]{2,1,0:T(8,128)}, u32[]{:S(2)}, u32[]{:S(2)}) collective-permute-start(f32[64,64,128]{2,1,0:T(8,128)} %collective-permute-done.1.refs_1_), channel_id=1, source_target_pairs={{0,1},{1,0},{2,3},{3,2},{4,5},{5,4},{6,7},{7,6},{8,9},{9,8},{10,11... | collective-permute-start | bytes 6291464 | tf_op jit(solution)/shard_map/ppermute | solution.py:25
  243.8 49.9 %collective-permute-start.4 = (f32[64,64,128]{2,1,0:T(8,128)}, f32[64,64,128]{2,1,0:T(8,128)}, u32[]{:S(2)}, u32[]{:S(2)}) collective-permute-start(f32[64,64,128]{2,1,0:T(8,128)} %collective-permute-done.3.refs_2_), channel_id=1, source_target_pairs={{0,8},{1,9},{2,10},{3,11},{4,12},{5,13},{6,14},{7,15},{8,0},{9,1},... | collective-permute-start | bytes 6291464 | tf_op jit(solution)/shard_map/ppermute | solution.py:20
  245.7 35.8 %copy-start = (f32[64,64,128]{2,1,0:T(8,128)}, f32[64,64,128]{2,1,0:T(8,128)S(1)}, u32[]{:S(2)}) copy-start(f32[64,64,128]{2,1,0:T(8,128)S(1)} %collective-permute-done.refs_0_) | copy-start | bytes 6291460
  245.7 67.8 %collective-permute-start.5 = (f32[32,128,128]{2,1,0:T(8,128)}, f32[32,128,128]{2,1,0:T(8,128)}, u32[]{:S(2)}, u32[]{:S(2)}) collective-permute-start(f32[32,128,128]{2,1,0:T(8,128)} %get-tuple-element.33.refs_3_), channel_id=1, source_target_pairs={{0,16},{16,32},{32,48},{48,64},{64,80},{80,96},{96,112},{112,0},{1... | collective-permute-start | bytes 6291464 | tf_op jit(solution)/shard_map/ppermute | solution.py:20
  268.7 47.6 %collective-permute-start.6 = (f32[32,128,128]{2,1,0:T(8,128)}, f32[32,128,128]{2,1,0:T(8,128)}, u32[]{:S(2)}, u32[]{:S(2)}) collective-permute-start(f32[32,128,128]{2,1,0:T(8,128)} %get-tuple-element.33.refs_3_), channel_id=1, source_target_pairs={{0,112},{16,0},{32,16},{48,32},{64,48},{80,64},{96,80},{112,96},{1... | collective-permute-start | bytes 6291464 | tf_op jit(solution)/shard_map/ppermute | solution.py:20

commit v9 on v8

--- a/solution.py
+++ b/solution.py
@@ -55,9 +55,8 @@
     pl.loop(0, hold_a)(lambda at: load_a(at).start())
 
     def send_b(at):
-        panel = lax.div(b_slot[at], slots[1])
-        inner, col = lax.div(panel, grid_cols), lax.rem(panel, grid_cols)
-        row = lax.rem(inner - col - 1 + grid_rows + grid_cols, grid_rows)
+        inner, col = over(over(b_slot[at], slots[1])[0], grid_cols)
+        row = (inner - col - 1 + grid_rows + grid_cols) & (grid_rows - 1)
         place = place_of(row * grid_cols + col)
         load_b(at).wait()
         for half, order in enumerate(ORDERS[:2]):
@@ -66,9 +65,8 @@
     pl.loop(0, hold_b, unroll=4)(send_b)
 
     def send_a(at):
-        panel = lax.div(a_slot[at], slots[0])
-        row, inner = lax.div(panel, grid_rows), lax.rem(panel, grid_rows)
-        col = lax.rem(inner - row - 1 + 2 * grid_rows, grid_rows)
+        row, inner = over(over(a_slot[at], slots[0])[0], grid_rows)
+        col = (inner - row - 1 + 2 * grid_rows) & (grid_rows - 1)
         load_a(at).wait()
         for half in range(2):
             place = place_of(row * grid_cols + col + half * grid_rows)
@@ -315,14 +313,16 @@
     return buffer * 128 + at
 
 
+def over(value, size):
+    return lax.shift_right_logical(value, jnp.int32(size.bit_length() - 1)), value & (size - 1)
+
+
 def place_of(device):
-    row, col = lax.div(device, RING * RING), lax.rem(device, RING * RING)
-    return {
-        "x": lax.div(row, RING) * 2 + lax.rem(lax.div(col, CORES), 2),
-        "y": lax.div(col, RING),
-        "z": lax.rem(row, RING),
-        "core": lax.rem(col, CORES),
-    }
+    row, col = over(device, RING * RING)
+    x_high, z = over(row, RING)
+    y, rest = over(col, RING)
+    x_low, core = over(rest, CORES)
+    return {"x": x_high * 2 + x_low, "y": y, "z": z, "core": core}
 
 
 def collect_kernel(pieces, source, *refs):
@@ -494,6 +494,114 @@
     )(counts, items, order, *halves, *rights, *extra)
 
 
+def matched_kernel(counts, items, order, *refs):
+    lefts, rights = (refs[0:2], refs[2:4]), refs[4:6]
+    before, out, left_buf, right_buf, total, load_sems, io_sem = refs[6:]
+    outs = out.shape[0]
+    slots_a, part, _ = lefts[0][0].shape
+    slots_b = rights[0].shape[0]
+    batches = counts[0]
+    restore = pltpu.make_async_copy(before, total.at[pl.ds(0, outs)], io_sem)
+    restore.start()
+
+    def fetch(at):
+        buffer = at & 1
+        for lane in range(UNROLL):
+            code = items[at * UNROLL + lane]
+            slot_a = lax.shift_right_logical(code, 14)
+            slot_b = lax.shift_right_logical(code, 7) & 127
+            for piece, halves in enumerate(lefts):
+
+                @pl.when(lax.div(slot_a, slots_a) == piece)
+                def _():
+                    swap = order[piece]
+                    for half, source in enumerate(halves):
+                        rows = pl.multiple_of((swap if half == 0 else 1 - swap) * part, part)
+                        pltpu.make_async_copy(
+                            source.at[slot_a - piece * slots_a],
+                            left_buf.at[buffer, lane, pl.ds(rows, part)],
+                            load_sems.at[buffer, lane, half],
+                        ).start()
+
+            for which, source in enumerate(rights):
+
+                @pl.when(lax.div(slot_b, slots_b) == which)
+                def _():
+                    pltpu.make_async_copy(
+                        source.at[slot_b - which * slots_b],
+                        right_buf.at[buffer, lane],
+                        load_sems.at[buffer, lane, 2],
+                    ).start()
+
+    def fetched(at):
+        buffer = at & 1
+        for lane in range(UNROLL):
+            for half in range(2):
+                pltpu.make_async_copy(
+                    lefts[0][0].at[0],
+                    left_buf.at[buffer, lane, pl.ds(0, part)],
+                    load_sems.at[buffer, lane, half],
+                ).wait()
+            pltpu.make_async_copy(
+                rights[0].at[0], right_buf.at[buffer, lane], load_sems.at[buffer, lane, 2]
+            ).wait()
+
+    @pl.when(batches > 0)
+    def _():
+        fetch(jnp.int32(0))
+
+    restore.wait()
+
+    def step(at):
+        @pl.when(at + 1 < batches)
+        def _():
+            fetch(at + 1)
+
+        fetched(at)
+        buffer = at & 1
+        sums = []
+        for lane in range(UNROLL):
+            a_hi, a_lo = split(left_buf[buffer, lane])
+            b_hi, b_lo = split(right_buf[buffer, lane])
+            sums.append(
+                jnp.dot(
+                    jnp.concatenate([a_hi, a_lo], axis=1),
+                    jnp.concatenate([b_hi, b_hi], axis=0),
+                    preferred_element_type=jnp.float32,
+                )
+                + jnp.dot(a_hi, b_lo, preferred_element_type=jnp.float32)
+            )
+        for lane, value in enumerate(sums):
+            total[items[at * UNROLL + lane] & 127] += value
+
+    pl.loop(0, batches)(step)
+    save = pltpu.make_async_copy(total.at[pl.ds(0, outs)], out, io_sem)
+    save.start()
+    save.wait()
+
+
+def add_matched(counts, items, order, lefts, rights, before):
+    outs, edge, _ = before.shape
+    return pl.pallas_call(
+        matched_kernel,
+        out_shape=jax.ShapeDtypeStruct(before.shape, jnp.float32),
+        in_specs=[SMEM] * 3 + [HBM] * (len(lefts) + len(rights) + 1),
+        out_specs=HBM,
+        scratch_shapes=[
+            pltpu.VMEM((2, UNROLL, edge, edge), jnp.float32),
+            pltpu.VMEM((2, UNROLL, edge, edge), jnp.float32),
+            pltpu.VMEM((outs + 1, edge, edge), jnp.float32),
+            pltpu.SemaphoreType.DMA((2, UNROLL, 3)),
+            pltpu.SemaphoreType.DMA,
+        ],
+        compiler_params=pltpu.CompilerParams(vmem_limit_bytes=GRANT),
+        cost_estimate=pl.CostEstimate(
+            flops=600_000_000, bytes_accessed=16_000_000, transcendentals=0
+        ),
+        name="add_matched",
+    )(counts, items, order, *lefts, *rights, before)
+
+
 def work_list(lefts, rights, places, kept, first_row):
     rows, width = kept.shape
     pieces, inner, _ = rights.shape
@@ -582,7 +690,7 @@
         shifts = [shifted(right[at], "row", 1), shifted(right[at], "row", -1)]
         first, last = at * chunk // WB, (at + 1) * chunk // WB
         count, items = work_list(col_left[1:], tables[1:, first:last], places, c_col, first)
-        total = products(count, items, order[1:], lefts, shifts, total, outs)
+        total = add_matched(count, items, order[1:], lefts, shifts, total)
     return total.reshape(rows, width, edge, edge)
 
 

time: 330 us -> 392 us (1.19); the launches traced: 329 us -> 385 us
  waiting for transfers between devices: 89.2 us -> 147 us
  Pallas kernels: 208 us -> 204 us
    ppermute x6, waiting for transfers between devices: 89.2 us -> 147 us  [shifted(): return lax.ppermute(value, axis, pairs)]
    pallas_call x3 -> x1, Pallas kernels: 35.6 us -> 9.36 us  [products(): pl.pallas_call(functools.partial(product_kernel, pieces, parts, first, UN...]
    pallas_call x0 -> x2, Pallas kernels: none -> 22.1 us  [add_matched(): pl.pallas_call(matched_kernel, out_shape=jax.ShapeDtypeStruct(before.shap...]
  transfers between devices with their start and end apart: 9 -> 9, of which waited for: 5 -> 3; matrix products, arithmetic and copies ran while one was open for 4% -> 3% of each run, Pallas kernels for 9% -> 7%
where the time goes in v9:
time: 392 us; the launch traced here: 385 us
  Pallas kernels  204 us (52%)
  waiting for transfers between devices  147 us (38%)
  starting transfers between devices  14 us (4%)
  other arithmetic  10.2 us (3%)
  local copies, waits for them, and re-layouts  6.7 us (2%)
    pallas_call x1, Pallas kernels, exchange(): pl.pallas_call(exchange_kernel, out_shape=[jax.ShapeDtypeStruct(shape, ki...  153 us
    ppermute x6, waiting for transfers between devices, shifted(): return lax.ppermute(value, axis, pairs)  147 us
    pallas_call x2, Pallas kernels, add_matched(): pl.pallas_call(matched_kernel, out_shape=jax.ShapeDtypeStruct(before.shap...  22.1 us
    ppermute x6, starting transfers between devices, shifted(): return lax.ppermute(value, axis, pairs)  12.7 us
    pallas_call x2, Pallas kernels, collect(): pl.pallas_call(functools.partial(collect_kernel, pieces), out_shape=[part...  10.3 us
    pallas_call x1, Pallas kernels, products(): pl.pallas_call(functools.partial(product_kernel, pieces, parts, first, UN...  9.36 us
    pallas_call x1, Pallas kernels, pack(): pl.pallas_call(functools.partial(pack_kernel, grid, slots), out_shape=[se...  9.09 us
  transfers between devices with their start and end apart: 9, of which 3 were waited for; matrix products, arithmetic and copies ran while one was open for 3% of the time, Pallas kernels for 7%

profile of v9, /device:TPU:26, one launch (start us, length us, event | category | flops | bytes accessed | tf_op | source)
XLA Modules:
  0.0 384.7 jit_solution(605834611668823601)
XLA Ops:
  0.0 0.8 pad_add_fusion
  0.8 0.6 pad_bitcast_fusion.refs_3_
  1.4 9.1 %pack.1 = (f32[128,64,128]{2,1,0:T(8,128)}, f32[128,64,128]{2,1,0:T(8,128)}, f32[128,64,128]{2,1,0:T(8,128)}) custom-call(s32[32]{0:T(128)} %a_slot.1, s32[64]{0:T(128)} %b_slot.1, f32[32,128,128]{2,1,0:T(8,128)} %a_held.1, f32[64,128,128]{2,1,0:T(8,128)} %b_held.1), custom_call_target="tpu_custom_call" | custom-call | tf_op jit(solution)/shard_map/pack/pallas_call | solution.py:91
  10.5 153.0 %exchange.1 = (f32[8,4,4,64,128]{4,3,2,1,0:T(8,128)}, f32[4,8,4,64,128]{4,3,2,1,0:T(8,128)}, f32[4,4,8,64,128]{4,3,2,1,0:T(8,128)}, f32[8,4,4,64,128]{4,3,2,1,0:...) custom-call(f32[8,4,4,64,128]{4,3,2,1,0:T(8,128)} %bitcast.47, ...), custom_call_target="tpu_custom_call" | custom-call | tf_op jit(solution)/shard_map/exchange/pallas_call | solution.py:270
  163.5 1.3 reshape.633
  164.8 0.1 reshape.634
  165.4 0.5 select_reduce_fusion.1
  165.9 0.6 fusion.22.source
  166.5 4.4 %collect.2.refs_0_ = f32[64,64,128]{2,1,0:T(8,128)} custom-call(s32[1,64]{1,0:T(1,128)} %fusion.22.source, f32[128,64,128]{2,1,0:T(8,128)} %get-tuple-element.22.refs_0_, f32[128,64,128]{2,1,0:T(8,128)} %bitcast.56, f32[128,64,128]{2,1,0:T(8,128)} %bitcast.57, f32[128,64,128]{2,1,0:T(8,128)} %bitcast.58), custom_call_target="tpu_custom_call" | custom-call | tf_op jit(solution)/shard_map/collect/pallas_call | solution.py:376
  171.0 2.1 collective-permute-start.1
  173.1 1.2 collective-permute-start.3
  174.6 0.9 select_reduce_fusion
  175.5 0.5 pad_add_fusion.1.source
  176.1 5.9 %collect.3 = (f32[32,128,128]{2,1,0:T(8,128)}, f32[32,128,128]{2,1,0:T(8,128)}) custom-call(s32[2,64]{1,0:T(2,128)} %pad_add_fusion.1.source, f32[128,64,128]{2,1,0:T(8,128)} %get-tuple-element.20.refs_0_, f32[128,64,128]{2,1,0:T(8,128)} %bitcast.50, f32[128,64,128]{2,1,0:T(8,128)} %bitcast.51, f32[128,64,128]{2,1,0:T(8,128)} %bitcast.52, ...), custom_call_target="tpu_custom_call" | custom-call | tf_op jit(solution)/shard_map/collect/pallas_call | solution.py:376
  182.0 1.0 collective-permute-start.5
  183.7 0.1 select_reduce_fusion.7
  184.0 0.1 select_reduce_fusion.5
  184.2 0.1 eq.275
  184.3 0.1 select_reduce_fusion.8
  184.6 0.7 broadcast_add_fusion.2
  185.3 0.1 copy.26
  185.4 0.1 reshape.652
  185.5 0.3 reduce-window.25
  185.9 0.1 copy.30
  186.0 0.1 reshape.656
  186.1 0.3 reduce-window.29
  186.6 0.1 copy.33
  186.7 0.1 sub.163
  186.8 0.1 copy.34
  186.9 0.1 reshape.658
  187.0 0.3 reduce-window.37
  187.4 0.1 slice_reduce_fusion.2
  187.5 0.1 slice_reduce_fusion.1
  187.6 0.1 slice_reduce_fusion
  187.8 0.6 convert_reduce_fusion.1
  188.4 0.7 convert_reduce_fusion
  189.2 5.6 %collective-permute-start.6 = (f32[32,128,128]{2,1,0:T(8,128)}, f32[32,128,128]{2,1,0:T(8,128)}, u32[]{:S(2)}, u32[]{:S(2)}) collective-permute-start(f32[32,128,128]{2,1,0:T(8,128)} %get-tuple-element.33.refs_3_), channel_id=1, source_target_pairs={{0,112},{16,0},{32,16},{48,32},{64,48},{80,64},{96,80},{112,96},{1... | collective-permute-start | bytes 6291464 | tf_op jit(solution)/shard_map/ppermute | solution.py:20
  194.8 48.8 %collective-permute-done.1.refs_1_ = f32[64,64,128]{2,1,0:T(8,128)} collective-permute-done((f32[64,64,128]{2,1,0:T(8,128)}, f32[64,64,128]{2,1,0:T(8,128)}, u32[]{:S(2)}, u32[]{:S(2)}) %collective-permute-start.1) | collective-permute-done | bytes 2097184 | tf_op jit(solution)/shard_map/ppermute | solution.py:20
  243.6 3.2 collective-permute-start.8
  246.7 66.5 %collective-permute-done.7.refs_4_ = f32[32,128,128]{2,1,0:T(8,128)} collective-permute-done((f32[32,128,128]{2,1,0:T(8,128)}, f32[32,128,128]{2,1,0:T(8,128)}, u32[]{:S(2)}, u32[]{:S(2)}) %collective-permute-start.7) | collective-permute-done | bytes 2097184 | tf_op jit(solution)/shard_map/ppermute | solution.py:20
  313.3 0.7 collective-permute-start.4
  314.7 0.1 copy.25
  315.5 0.1 copy.29
  316.4 0.1 copy.27
  316.5 0.1 reshape.660
  316.6 0.1 reshape.651
  316.7 0.7 slice.59.order
  317.4 0.1 copy.31
  317.5 0.1 reshape.662
  317.6 0.1 reshape.655
  317.8 0.1 add.742
  318.0 0.1 add.734
  318.2 0.1 add.736
  318.3 0.1 add.738
  318.5 0.1 select_reduce_fusion.4
  318.7 0.3 select_reduce_fusion.3
  319.1 0.3 select_reduce_fusion.2
  319.4 0.6 broadcast_add_fusion.6.items
  320.0 0.6 broadcast_add_fusion.5.items
  320.6 0.6 broadcast_add_fusion.4.items
  321.2 9.4 %products.1.refs_6_ = f32[96,128,128]{2,1,0:T(8,128)} custom-call(s32[1]{0:T(128)} %bitcast.25.counts, s32[256]{0:T(256)} %broadcast_add_fusion.6.items, s32[1]{0:T(128)} %bitcast.59, f32[64,64,128]{2,1,0:T(8,128)} %collect.2.refs_0_, f32[64,64,128]{2,1,0:T(8,128)} %collective-permute-done.1.refs_1_, f32[32,128,128]{2,1,0:T(8,128)} %get-tuple-element.34.refs_2_, ...), custom_call_target="tpu_custom_call" | custom-call | flops 600000000 | bytes 8000000 | tf_op jit(solution)/shard_map/products/pallas_call | solution.py:477
  330.6 32.0 %collective-permute-done.4.refs_3_ = f32[64,64,128]{2,1,0:T(8,128)} collective-permute-done((f32[64,64,128]{2,1,0:T(8,128)}, f32[64,64,128]{2,1,0:T(8,128)}, u32[]{:S(2)}, u32[]{:S(2)}) %collective-permute-start.4) | collective-permute-done | bytes 2097184 | tf_op jit(solution)/shard_map/ppermute | solution.py:20
  362.6 11.4 %add_matched.2.refs_6_ = f32[96,128,128]{2,1,0:T(8,128)} custom-call(s32[1]{0:T(128)} %bitcast.22.counts, s32[512]{0:T(512)} %broadcast_add_fusion.4.items, s32[2]{0:T(128)} %slice.59.order, f32[64,64,128]{2,1,0:T(8,128)} %copy-done, f32[64,64,128]{2,1,0:T(8,128)} %collective-permute-done.2.refs_1_, f32[64,64,128]{2,1,0:T(8,128)} %collective-permute-done.3.refs_2_, ...), custom_call_target="tpu_custom_call" | custom-call | flops 600000000 | bytes 16000000 | tf_op jit(solution)/shard_map/add_matched/pallas_call | solution.py:585
  374.0 10.7 %add_matched.3 = f32[96,128,128]{2,1,0:T(8,128)} custom-call(s32[1]{0:T(128)} %bitcast.7.counts, s32[512]{0:T(512)} %broadcast_add_fusion.5.items, s32[2]{0:T(128)} %slice.59.order, f32[64,64,128]{2,1,0:T(8,128)} %copy-done, f32[64,64,128]{2,1,0:T(8,128)} %collective-permute-done.2.refs_1_, f32[64,64,128]{2,1,0:T(8,128)} %collective-permute-done.3.refs_2_, ...), custom_call_target="tpu_custom_call" | custom-call | flops 600000000 | bytes 16000000 | tf_op jit(solution)/shard_map/add_matched/pallas_call | solution.py:585
  (79 shorter events, 2.9 us)
Async XLA Ops:
  170.9 18.3 %collective-permute-start = (f32[64,64,128]{2,1,0:T(8,128)}, f32[64,64,128]{2,1,0:T(8,128)S(1)}, u32[]{:S(2)}, u32[]{:S(2)}) collective-permute-start(f32[64,64,128]{2,1,0:T(8,128)} %collect.2.refs_0_), channel_id=1, source_target_pairs={{0,1},{1,0},{2,3},{3,2},{4,5},{5,4},{6,7},{7,6},{8,9},{9,8},{10,11... | collective-permute-start | bytes 6291464 | tf_op jit(solution)/shard_map/ppermute | solution.py:25
  171.0 72.6 %collective-permute-start.1 = (f32[64,64,128]{2,1,0:T(8,128)}, f32[64,64,128]{2,1,0:T(8,128)}, u32[]{:S(2)}, u32[]{:S(2)}) collective-permute-start(f32[64,64,128]{2,1,0:T(8,128)} %collect.2.refs_0_), channel_id=1, source_target_pairs={{0,8},{1,9},{2,10},{3,11},{4,12},{5,13},{6,14},{7,15},{8,0},{9,1},... | collective-permute-start | bytes 6291464 | tf_op jit(solution)/shard_map/ppermute | solution.py:20
  173.1 73.6 %collective-permute-start.3 = (f32[64,64,128]{2,1,0:T(8,128)}, f32[64,64,128]{2,1,0:T(8,128)}, u32[]{:S(2)}, u32[]{:S(2)}) collective-permute-start(f32[64,64,128]{2,1,0:T(8,128)} %collect.2.refs_0_), channel_id=1, source_target_pairs={{0,15},{1,2},{2,1},{3,4},{4,3},{5,6},{6,5},{7,8},{8,7},{9,10},{10,... | collective-permute-start | bytes 6291464 | tf_op jit(solution)/shard_map/ppermute | solution.py:25
  176.1 8.1 %copy-start.1 = (s32[16,6]{0,1:T(8,128)S(1)}, s32[16,6]{0,1:T(8,128)}, u32[]{:S(2)}) copy-start(s32[16,6]{0,1:T(8,128)} %param.13) | copy-start | bytes 1156
  182.0 192.0 %collective-permute-start.5 = (f32[32,128,128]{2,1,0:T(8,128)}, f32[32,128,128]{2,1,0:T(8,128)}, u32[]{:S(2)}, u32[]{:S(2)}) collective-permute-start(f32[32,128,128]{2,1,0:T(8,128)} %get-tuple-element.33.refs_3_), channel_id=1, source_target_pairs={{0,16},{16,32},{32,48},{48,64},{64,80},{80,96},{96,112},{112,0},{1... | collective-permute-start | bytes 6291464 | tf_op jit(solution)/shard_map/ppermute | solution.py:20
  183.0 130.2 %collective-permute-start.7 = (f32[32,128,128]{2,1,0:T(8,128)}, f32[32,128,128]{2,1,0:T(8,128)}, u32[]{:S(2)}, u32[]{:S(2)}) collective-permute-start(f32[32,128,128]{2,1,0:T(8,128)} %get-tuple-element.34.refs_2_), channel_id=1, source_target_pairs={{0,16},{16,32},{32,48},{48,64},{64,80},{80,96},{96,112},{112,0},{1... | collective-permute-start | bytes 6291464 | tf_op jit(solution)/shard_map/ppermute | solution.py:20
  189.2 141.4 %copy-start = (f32[64,64,128]{2,1,0:T(8,128)}, f32[64,64,128]{2,1,0:T(8,128)S(1)}, u32[]{:S(2)}) copy-start(f32[64,64,128]{2,1,0:T(8,128)S(1)} %collective-permute-done.refs_0_) | copy-start | bytes 6291460
  189.2 184.9 %collective-permute-start.6 = (f32[32,128,128]{2,1,0:T(8,128)}, f32[32,128,128]{2,1,0:T(8,128)}, u32[]{:S(2)}, u32[]{:S(2)}) collective-permute-start(f32[32,128,128]{2,1,0:T(8,128)} %get-tuple-element.33.refs_3_), channel_id=1, source_target_pairs={{0,112},{16,0},{32,16},{48,32},{64,48},{80,64},{96,80},{112,96},{1... | collective-permute-start | bytes 6291464 | tf_op jit(solution)/shard_map/ppermute | solution.py:20
  243.6 87.0 %collective-permute-start.8 = (f32[32,128,128]{2,1,0:T(8,128)}, f32[32,128,128]{2,1,0:T(8,128)}, u32[]{:S(2)}, u32[]{:S(2)}) collective-permute-start(f32[32,128,128]{2,1,0:T(8,128)} %get-tuple-element.34.refs_2_), channel_id=1, source_target_pairs={{0,112},{16,0},{32,16},{48,32},{64,48},{80,64},{96,80},{112,96},{1... | collective-permute-start | bytes 6291464 | tf_op jit(solution)/shard_map/ppermute | solution.py:20
  246.7 83.8 %collective-permute-start.2 = (f32[64,64,128]{2,1,0:T(8,128)}, f32[64,64,128]{2,1,0:T(8,128)}, u32[]{:S(2)}, u32[]{:S(2)}) collective-permute-start(f32[64,64,128]{2,1,0:T(8,128)} %collective-permute-done.1.refs_1_), channel_id=1, source_target_pairs={{0,1},{1,0},{2,3},{3,2},{4,5},{5,4},{6,7},{7,6},{8,9},{9,8},{10,11... | collective-permute-start | bytes 6291464 | tf_op jit(solution)/shard_map/ppermute | solution.py:25
  313.3 49.3 %collective-permute-start.4 = (f32[64,64,128]{2,1,0:T(8,128)}, f32[64,64,128]{2,1,0:T(8,128)}, u32[]{:S(2)}, u32[]{:S(2)}) collective-permute-start(f32[64,64,128]{2,1,0:T(8,128)} %collective-permute-done.3.refs_2_), channel_id=1, source_target_pairs={{0,8},{1,9},{2,10},{3,11},{4,12},{5,13},{6,14},{7,15},{8,0},{9,1},... | collective-permute-start | bytes 6291464 | tf_op jit(solution)/shard_map/ppermute | solution.py:20
  314.1 7.1 %copy-start.2 = (s32[3]{0:T(128)}, s32[3]{0:T(128)S(1)}, u32[]{:S(2)}) copy-start(s32[3]{0:T(128)S(1)} %compare_convert_fusion.1) | copy-start | bytes 40

commit v10 on v8

--- a/solution.py
+++ b/solution.py
@@ -486,7 +486,7 @@
             pltpu.SemaphoreType.DMA((2 * pieces + parts,)),
             pltpu.SemaphoreType.DMA,
         ],
-        compiler_params=pltpu.CompilerParams(vmem_limit_bytes=GRANT),
+        compiler_params=pltpu.CompilerParams(vmem_limit_bytes=24 * 1024 * 1024),
         cost_estimate=pl.CostEstimate(
             flops=pieces * 600_000_000, bytes_accessed=pieces * 8_000_000, transcendentals=0
         ),

time: 330 us -> 327 us (level)
  Pallas kernels: 208 us -> 193 us
  waiting for transfers between devices: 89.2 us -> 98 us
  local copies, waits for them, and re-layouts: 6.7 us -> 10.9 us
    pallas_call x3, Pallas kernels: 35.6 us -> 20 us  [products(): pl.pallas_call(functools.partial(product_kernel, pieces, parts, first, UN...]
    ppermute x6, waiting for transfers between devices: 89.2 us -> 98 us  [shifted(): return lax.ppermute(value, axis, pairs)]
    unnamed x6 -> x8, local copies, waits for them, and re-layouts: 0.01 us -> 4.77 us
  transfers between devices with their start and end apart: 9 -> 9, of which waited for: 5 -> 5; matrix products, arithmetic and copies ran while one was open for 4% -> 3% of each run, Pallas kernels for 9% -> 6%
where the time goes in v10:
time: 327 us; the launch traced here: 324 us
  Pallas kernels  193 us (59%)
  waiting for transfers between devices  98 us (30%)
  starting transfers between devices  12 us (4%)
  local copies, waits for them, and re-layouts  10.9 us (3%)
  other arithmetic  8.33 us (3%)
    pallas_call x1, Pallas kernels, exchange(): pl.pallas_call(exchange_kernel, out_shape=[jax.ShapeDtypeStruct(shape, ki...  153 us
    ppermute x6, waiting for transfers between devices, shifted(): return lax.ppermute(value, axis, pairs)  98 us
    pallas_call x3, Pallas kernels, products(): pl.pallas_call(functools.partial(product_kernel, pieces, parts, first, UN...  20 us
    ppermute x6, starting transfers between devices, shifted(): return lax.ppermute(value, axis, pairs)  10.7 us
    pallas_call x2, Pallas kernels, collect(): pl.pallas_call(functools.partial(collect_kernel, pieces), out_shape=[part...  10.3 us
    pallas_call x1, Pallas kernels, pack(): pl.pallas_call(functools.partial(pack_kernel, grid, slots), out_shape=[se...  9.25 us
  transfers between devices with their start and end apart: 9, of which 5 were waited for; matrix products, arithmetic and copies ran while one was open for 3% of the time, Pallas kernels for 6%

profile of v10, /device:TPU:26, one launch (start us, length us, event | category | flops | bytes accessed | tf_op | source)
XLA Modules:
  0.0 324.1 jit_solution(9648439141090819826)
XLA Ops:
  0.0 0.8 pad_add_fusion
  0.8 0.6 pad_bitcast_fusion.refs_3_
  1.4 9.2 %pack.1 = (f32[128,64,128]{2,1,0:T(8,128)}, f32[128,64,128]{2,1,0:T(8,128)}, f32[128,64,128]{2,1,0:T(8,128)}) custom-call(s32[32]{0:T(128)} %a_slot.1, s32[64]{0:T(128)} %b_slot.1, f32[32,128,128]{2,1,0:T(8,128)} %a_held.1, f32[64,128,128]{2,1,0:T(8,128)} %b_held.1), custom_call_target="tpu_custom_call" | custom-call | tf_op jit(solution)/shard_map/pack/pallas_call | solution.py:93
  10.6 153.0 %exchange.1 = (f32[8,4,4,64,128]{4,3,2,1,0:T(8,128)}, f32[4,8,4,64,128]{4,3,2,1,0:T(8,128)}, f32[4,4,8,64,128]{4,3,2,1,0:T(8,128)}, f32[8,4,4,64,128]{4,3,2,1,0:...) custom-call(f32[8,4,4,64,128]{4,3,2,1,0:T(8,128)} %bitcast.48, ...), custom_call_target="tpu_custom_call" | custom-call | tf_op jit(solution)/shard_map/exchange/pallas_call | solution.py:272
  163.7 1.3 reshape.633
  165.0 0.1 reshape.634
  165.5 0.5 select_reduce_fusion.1
  166.1 0.6 fusion.22.source
  166.6 4.4 %collect.2.refs_0_ = f32[64,64,128]{2,1,0:T(8,128)} custom-call(s32[1,64]{1,0:T(1,128)} %fusion.22.source, f32[128,64,128]{2,1,0:T(8,128)} %get-tuple-element.22.refs_0_, f32[128,64,128]{2,1,0:T(8,128)} %bitcast.57, f32[128,64,128]{2,1,0:T(8,128)} %bitcast.58, f32[128,64,128]{2,1,0:T(8,128)} %bitcast.59), custom_call_target="tpu_custom_call" | custom-call | tf_op jit(solution)/shard_map/collect/pallas_call | solution.py:376
  171.1 2.2 collective-permute-start.1
  173.3 1.2 collective-permute-start.3
  174.8 0.9 select_reduce_fusion
  175.8 0.5 pad_add_fusion.1.source
  176.3 5.9 %collect.3 = (f32[32,128,128]{2,1,0:T(8,128)}, f32[32,128,128]{2,1,0:T(8,128)}) custom-call(s32[2,64]{1,0:T(2,128)} %pad_add_fusion.1.source, f32[128,64,128]{2,1,0:T(8,128)} %get-tuple-element.20.refs_0_, f32[128,64,128]{2,1,0:T(8,128)} %bitcast.51, f32[128,64,128]{2,1,0:T(8,128)} %bitcast.52, f32[128,64,128]{2,1,0:T(8,128)} %bitcast.53, ...), custom_call_target="tpu_custom_call" | custom-call | tf_op jit(solution)/shard_map/collect/pallas_call | solution.py:376
  182.2 1.0 collective-permute-start.7
  183.2 4.7 %collective-permute-start.8 = (f32[32,128,128]{2,1,0:T(8,128)}, f32[32,128,128]{2,1,0:T(8,128)}, u32[]{:S(2)}, u32[]{:S(2)}) collective-permute-start(f32[32,128,128]{2,1,0:T(8,128)} %get-tuple-element.34.refs_2_), channel_id=1, source_target_pairs={{0,112},{16,0},{32,16},{48,32},{64,48},{80,64},{96,80},{112,96},{1... | collective-permute-start | bytes 6291464 | tf_op jit(solution)/shard_map/ppermute | solution.py:20
  188.5 0.1 select_reduce_fusion.7
  188.8 0.1 select_reduce_fusion.8
  189.0 0.6 convert_reduce_fusion.1
  190.2 0.1 copy.25
  190.4 0.6 convert_reduce_fusion
  191.6 0.1 copy.29
  191.9 0.1 select_reduce_fusion.5
  192.1 0.6 broadcast_add_fusion.2
  193.4 0.1 copy.27
  193.5 0.1 reshape.660
  193.6 0.1 copy.26
  193.7 0.1 reshape.652
  193.9 0.3 reduce-window.25
  194.3 0.1 reshape.651
  194.6 0.1 copy.31
  194.7 0.1 reshape.662
  194.8 0.1 copy.30
  194.9 0.1 reshape.656
  195.0 0.3 reduce-window.29
  195.4 0.1 reshape.655
  195.6 0.1 copy.33
  195.7 0.1 sub.163
  195.8 0.1 add.742
  196.0 0.1 add.734
  196.2 0.1 add.736
  196.4 0.1 add.738
  196.5 0.1 copy.34
  196.6 0.1 reshape.658
  196.7 0.3 reduce-window.37
  197.1 0.1 slice_reduce_fusion.2
  197.2 0.1 slice_reduce_fusion.1
  197.4 46.3 %collective-permute-done.1.refs_1_ = f32[64,64,128]{2,1,0:T(8,128)} collective-permute-done((f32[64,64,128]{2,1,0:T(8,128)}, f32[64,64,128]{2,1,0:T(8,128)}, u32[]{:S(2)}, u32[]{:S(2)}) %collective-permute-start.1) | collective-permute-done | bytes 2097184 | tf_op jit(solution)/shard_map/ppermute | solution.py:20
  243.8 1.8 collective-permute-start.4
  245.6 0.1 slice_reduce_fusion
  245.7 1.0 collective-permute-start.5
  246.7 22.0 %collective-permute-done.7.refs_4_ = f32[32,128,128]{2,1,0:T(8,128)} collective-permute-done((f32[32,128,128]{2,1,0:T(8,128)}, f32[32,128,128]{2,1,0:T(8,128)}, u32[]{:S(2)}, u32[]{:S(2)}) %collective-permute-start.7) | collective-permute-done | bytes 2097184 | tf_op jit(solution)/shard_map/ppermute | solution.py:20
  268.7 0.1 select_reduce_fusion.4
  268.9 0.3 select_reduce_fusion.3
  269.3 0.3 select_reduce_fusion.2
  269.6 1.6 copy-done
  271.2 1.6 copy-done.1
  272.8 1.6 copy-done.2
  274.4 5.1 %products.3.refs_6_ = f32[96,128,128]{2,1,0:T(8,128)S(1)} custom-call(s32[1]{0:T(128)} %bitcast.25.counts, s32[256]{0:T(256)S(1)} %broadcast_add_fusion.6.items, s32[1]{0:T(128)S(1)} %bitcast.47, f32[64,64,128]{2,1,0:T(8,128)S(1)} %copy-done, f32[64,64,128]{2,1,0:T(8,128)} %collective-permute-done.1.refs_1_, f32[32,128,128]{2,1,0:T(8,128)S(1)} %copy-done.2, ...), custom_call_target="tpu_custom_call" | custom-call | flops 600000000 | bytes 8000000 | tf_op jit(solution)/shard_map/products/pallas_call | solution.py:477
  279.5 14.0 %collective-permute-done.4.refs_3_ = f32[64,64,128]{2,1,0:T(8,128)S(1)} collective-permute-done((f32[64,64,128]{2,1,0:T(8,128)}, f32[64,64,128]{2,1,0:T(8,128)S(1)}, u32[]{:S(2)}, u32[]{:S(2)}) %collective-permute-start.4) | collective-permute-done | bytes 2097184 | tf_op jit(solution)/shard_map/ppermute | solution.py:20
  293.5 7.0 %products.4.refs_6_ = f32[96,128,128]{2,1,0:T(8,128)S(1)} custom-call(s32[1]{0:T(128)} %bitcast.22.counts, s32[512]{0:T(512)S(1)} %broadcast_add_fusion.4.items, s32[2]{0:T(128)S(1)} %slice.59.order, f32[64,64,128]{2,1,0:T(8,128)S(1)} %collective-permute-done.refs_0_, f32[64,64,128]{2,1,0:T(8,128)S(1)} %collective-permute-done.2.refs_1_, ...), custom_call_target="tpu_custom_call" | custom-call | flops 1200000000 | bytes 16000000 | tf_op jit(solution)/shard_map/products/pallas_call | solution.py:477
  300.5 12.8 %collective-permute-done.5.refs_4_ = f32[32,128,128]{2,1,0:T(8,128)S(1)} collective-permute-done((f32[32,128,128]{2,1,0:T(8,128)}, f32[32,128,128]{2,1,0:T(8,128)S(1)}, u32[]{:S(2)}, u32[]{:S(2)}) %collective-permute-start.5) | collective-permute-done | bytes 2097184 | tf_op jit(solution)/shard_map/ppermute | solution.py:20
  313.3 2.9 collective-permute-done.6.refs_5_
  316.2 7.9 %products.5 = f32[96,128,128]{2,1,0:T(8,128)} custom-call(s32[1]{0:T(128)} %bitcast.7.counts, s32[512]{0:T(512)S(1)} %broadcast_add_fusion.5.items, s32[2]{0:T(128)S(1)} %slice.59.order, f32[64,64,128]{2,1,0:T(8,128)S(1)} %collective-permute-done.refs_0_, f32[64,64,128]{2,1,0:T(8,128)S(1)} %collective-permute-done.2.refs_1_, ...), custom_call_target="tpu_custom_call" | custom-call | flops 1200000000 | bytes 16000000 | tf_op jit(solution)/shard_map/products/pallas_call | solution.py:477
  (82 shorter events, 3.0 us)
Async XLA Ops:
  171.0 74.6 %collective-permute-start = (f32[64,64,128]{2,1,0:T(8,128)}, f32[64,64,128]{2,1,0:T(8,128)S(1)}, u32[]{:S(2)}, u32[]{:S(2)}) collective-permute-start(f32[64,64,128]{2,1,0:T(8,128)} %collect.2.refs_0_), channel_id=1, source_target_pairs={{0,1},{1,0},{2,3},{3,2},{4,5},{5,4},{6,7},{7,6},{8,9},{9,8},{10,11... | collective-permute-start | bytes 6291464 | tf_op jit(solution)/shard_map/ppermute | solution.py:25
  171.1 72.6 %collective-permute-start.1 = (f32[64,64,128]{2,1,0:T(8,128)}, f32[64,64,128]{2,1,0:T(8,128)}, u32[]{:S(2)}, u32[]{:S(2)}) collective-permute-start(f32[64,64,128]{2,1,0:T(8,128)} %collect.2.refs_0_), channel_id=1, source_target_pairs={{0,8},{1,9},{2,10},{3,11},{4,12},{5,13},{6,14},{7,15},{8,0},{9,1},... | collective-permute-start | bytes 6291464 | tf_op jit(solution)/shard_map/ppermute | solution.py:20
  173.3 70.5 %collective-permute-start.3 = (f32[64,64,128]{2,1,0:T(8,128)}, f32[64,64,128]{2,1,0:T(8,128)}, u32[]{:S(2)}, u32[]{:S(2)}) collective-permute-start(f32[64,64,128]{2,1,0:T(8,128)} %collect.2.refs_0_), channel_id=1, source_target_pairs={{0,15},{1,2},{2,1},{3,4},{4,3},{5,6},{6,5},{7,8},{8,7},{9,10},{10,... | collective-permute-start | bytes 6291464 | tf_op jit(solution)/shard_map/ppermute | solution.py:25
  176.3 12.4 %copy-start.3 = (s32[16,6]{0,1:T(8,128)S(1)}, s32[16,6]{0,1:T(8,128)}, u32[]{:S(2)}) copy-start(s32[16,6]{0,1:T(8,128)} %param.13) | copy-start | bytes 1156
  182.2 86.5 %collective-permute-start.7 = (f32[32,128,128]{2,1,0:T(8,128)}, f32[32,128,128]{2,1,0:T(8,128)}, u32[]{:S(2)}, u32[]{:S(2)}) collective-permute-start(f32[32,128,128]{2,1,0:T(8,128)} %get-tuple-element.34.refs_2_), channel_id=1, source_target_pairs={{0,16},{16,32},{32,48},{48,64},{64,80},{80,96},{96,112},{112,0},{1... | collective-permute-start | bytes 6291464 | tf_op jit(solution)/shard_map/ppermute | solution.py:20
  183.2 96.3 %collective-permute-start.8 = (f32[32,128,128]{2,1,0:T(8,128)}, f32[32,128,128]{2,1,0:T(8,128)}, u32[]{:S(2)}, u32[]{:S(2)}) collective-permute-start(f32[32,128,128]{2,1,0:T(8,128)} %get-tuple-element.34.refs_2_), channel_id=1, source_target_pairs={{0,112},{16,0},{32,16},{48,32},{64,48},{80,64},{96,80},{112,96},{1... | collective-permute-start | bytes 6291464 | tf_op jit(solution)/shard_map/ppermute | solution.py:20
  243.8 35.8 %collective-permute-start.2 = (f32[64,64,128]{2,1,0:T(8,128)}, f32[64,64,128]{2,1,0:T(8,128)S(1)}, u32[]{:S(2)}, u32[]{:S(2)}) collective-permute-start(f32[64,64,128]{2,1,0:T(8,128)} %collective-permute-done.1.refs_1_), channel_id=1, source_target_pairs={{0,1},{1,0},{2,3},{3,2},{4,5},{5,4},{6,7},{7,6},{8,9},{9,8},{10,11... | collective-permute-start | bytes 6291464 | tf_op jit(solution)/shard_map/ppermute | solution.py:25
  243.8 49.8 %collective-permute-start.4 = (f32[64,64,128]{2,1,0:T(8,128)}, f32[64,64,128]{2,1,0:T(8,128)S(1)}, u32[]{:S(2)}, u32[]{:S(2)}) collective-permute-start(f32[64,64,128]{2,1,0:T(8,128)} %collective-permute-done.3.refs_2_), channel_id=1, source_target_pairs={{0,8},{1,9},{2,10},{3,11},{4,12},{5,13},{6,14},{7,15},{8,0},{9,1},... | collective-permute-start | bytes 6291464 | tf_op jit(solution)/shard_map/ppermute | solution.py:20
  245.7 67.7 %collective-permute-start.5 = (f32[32,128,128]{2,1,0:T(8,128)}, f32[32,128,128]{2,1,0:T(8,128)S(1)}, u32[]{:S(2)}, u32[]{:S(2)}) collective-permute-start(f32[32,128,128]{2,1,0:T(8,128)} %get-tuple-element.33.refs_3_), channel_id=1, source_target_pairs={{0,16},{16,32},{32,48},{48,64},{64,80},{80,96},{96,112},{112,0},{1... | collective-permute-start | bytes 6291464 | tf_op jit(solution)/shard_map/ppermute | solution.py:20
  268.7 47.5 %collective-permute-start.6 = (f32[32,128,128]{2,1,0:T(8,128)}, f32[32,128,128]{2,1,0:T(8,128)S(1)}, u32[]{:S(2)}, u32[]{:S(2)}) collective-permute-start(f32[32,128,128]{2,1,0:T(8,128)} %get-tuple-element.33.refs_3_), channel_id=1, source_target_pairs={{0,112},{16,0},{32,16},{48,32},{64,48},{80,64},{96,80},{112,96},{1... | collective-permute-start | bytes 6291464 | tf_op jit(solution)/shard_map/ppermute | solution.py:20
  269.6 1.6 copy-start
  271.2 1.6 copy-start.1
  272.8 1.6 copy-start.2
